TPU v7x, 32 devices: a whole 2x2x4 slice. The times are simulated.
32 devices in a mesh: dp: 4 (over z), context: 4 (over y, core), tensor: 2 (over x).
Axes of the slice: x: 2, y: 2, z: 4, core: 2. Of those that a mesh axis runs over, the one named last changes fastest.
Arguments:
- inputs: bfloat16 [16, 1024, 1024], P('dp', 'context'), may hold values from -6 to 6
- lengths: int32 [16], P('dp'), may hold values from 256 to 1024
- query_weight: bfloat16 [1024, 1024], P('dp', 'tensor'), may hold values from -0.1875 to 0.1875
- key_weight: bfloat16 [1024, 512], P('dp', 'tensor'), may hold values from -0.1875 to 0.1875
- value_weight: bfloat16 [1024, 512], P('dp', 'tensor'), may hold values from -0.1875 to 0.1875
- out_weight: bfloat16 [1024, 1024], P('tensor', 'dp'), may hold values from -1 to 1
- gate_weight: bfloat16 [1024, 4608], P('dp', 'tensor'), may hold values from -0.1875 to 0.1875
- up_weight: bfloat16 [1024, 4608], P('dp', 'tensor'), may hold values from -0.1875 to 0.1875
- down_weight: bfloat16 [4608, 1024], P('tensor', 'dp'), may hold values from -0.09375 to 0.09375
- norm_gains: bfloat16 [2, 1024], P(None, 'dp'), may hold values from 0.25 to 1.75
- head_gains: bfloat16 [2, 64], P(None, 'dp'), may hold values from 0.25 to 1.75
- cotangent: bfloat16 [16, 1024, 1024], P('dp', 'context'), may hold values from -6 to 6
Outputs:
- outputs: bfloat16 [16, 1024, 1024], P('dp', 'context')
- input_grad: float32 [16, 1024, 1024], P('dp', 'context')
- query_weight_grad: float32 [1024, 1024], P('dp', 'tensor')
- key_weight_grad: float32 [1024, 512], P('dp', 'tensor')
- value_weight_grad: float32 [1024, 512], P('dp', 'tensor')
- out_weight_grad: float32 [1024, 1024], P('tensor', 'dp')
- gate_weight_grad: float32 [1024, 4608], P('dp', 'tensor')
- up_weight_grad: float32 [1024, 4608], P('dp', 'tensor')
- down_weight_grad: float32 [4608, 1024], P('tensor', 'dp')
- norm_gains_grad: float32 [2, 1024], P(None, 'dp')
- head_gains_grad: float32 [2, 64], P(None, 'dp')
All inputs are finite; a program needn't handle non-finite values.
Results may differ from a plain program's by a relative error of at most 0.013.
Values may be sent and summed in bfloat16 or wider, within the bound.
A program may use at most 192 MiB of HBM per device.

v0:
```python
import jax
import jax.numpy as jnp
from jax import lax
from jax.sharding import PartitionSpec as P

HD = 64


epsilon = 1e-05
rope_base = 1000000.0


def matmul(left_side, right_side):
    return jnp.dot(left_side, right_side, preferred_element_type=jnp.float32)


def left_transposed(left_side, right_side):
    return lax.dot_general(
        left_side, right_side, (((0,), (0,)), ((), ())), preferred_element_type=jnp.float32
    )


def right_transposed(left_side, right_side):
    return lax.dot_general(
        left_side, right_side, (((1,), (1,)), ((), ())), preferred_element_type=jnp.float32
    )


def rms_scale(values):
    return lax.rsqrt(jnp.mean(values * values, axis=-1, keepdims=True) + epsilon)


def norm_back(upstream, normal, scale):
    return scale * (upstream - normal * jnp.mean(upstream * normal, axis=-1, keepdims=True))


def rotate(values, cosine_table, sine_table):
    half_width = values.shape[-1] // 2
    front_half = values[..., :half_width]
    back_half = values[..., half_width:]
    return jnp.concatenate(
        [
            front_half * cosine_table - back_half * sine_table,
            back_half * cosine_table + front_half * sine_table,
        ],
        axis=-1,
    )


def unrotate(values, cosine_table, sine_table):
    half_width = values.shape[-1] // 2
    front_half = values[..., :half_width]
    back_half = values[..., half_width:]
    return jnp.concatenate(
        [
            front_half * cosine_table + back_half * sine_table,
            back_half * cosine_table - front_half * sine_table,
        ],
        axis=-1,
    )


def rope_tables(positions):
    half_width = HD // 2
    frequency = rope_base ** (-2.0 * jnp.arange(half_width, dtype=jnp.float32) / HD)
    angles = positions.astype(jnp.float32)[:, None] * frequency[None, :]
    return (jnp.cos(angles)[:, None, :], jnp.sin(angles)[:, None, :])


def score_block(query_rows, key_rows, length, offset):
    block_len = query_rows.shape[0]
    full_len = key_rows.shape[0]
    kv_heads = key_rows.shape[1] // HD
    group_size = query_rows.shape[1] // HD // kv_heads
    grouped = query_rows.reshape(block_len, kv_heads, group_size, HD)
    keyed = key_rows.reshape(full_len, kv_heads, HD)
    scores = jnp.einsum(
        "qkgd,skd->kgqs", grouped, keyed, preferred_element_type=jnp.float32
    ) * HD ** (-0.5)
    query_pos = offset + jnp.arange(block_len, dtype=jnp.int32)
    key_pos = jnp.arange(full_len, dtype=jnp.int32)
    allowed = (key_pos[None, :] <= query_pos[:, None]) & (key_pos[None, :] < length)
    return (jnp.where(allowed, scores, -1e30), grouped, keyed)


def on_device(
    inputs,
    lengths,
    query_weight,
    key_weight,
    value_weight,
    out_weight,
    gate_weight,
    up_weight,
    down_weight,
    norm_gains,
    head_gains,
    cotangent,
):
    seq_here, block_len, width = inputs.shape
    tokens = seq_here * block_len
    offset = lax.axis_index("context") * block_len
    (
        query_full,
        key_full,
        value_full,
        out_full,
        gate_full,
        up_full,
        down_full,
        gains_full,
        head_full,
    ) = (
        lax.all_gather(query_weight, "dp", axis=0, tiled=True),
        lax.all_gather(key_weight, "dp", axis=0, tiled=True),
        lax.all_gather(value_weight, "dp", axis=0, tiled=True),
        lax.all_gather(out_weight, "dp", axis=1, tiled=True),
        lax.all_gather(gate_weight, "dp", axis=0, tiled=True),
        lax.all_gather(up_weight, "dp", axis=0, tiled=True),
        lax.all_gather(down_weight, "dp", axis=1, tiled=True),
        lax.all_gather(norm_gains, "dp", axis=1, tiled=True),
        lax.all_gather(head_gains, "dp", axis=1, tiled=True),
    )
    q_heads = query_full.shape[1] // HD
    kv_heads = key_full.shape[1] // HD
    gain_attn = gains_full[0].astype(jnp.float32)
    gain_ffn = gains_full[1].astype(jnp.float32)
    gain_query = head_full[0].astype(jnp.float32)
    gain_key = head_full[1].astype(jnp.float32)
    cosine_table, sine_table = rope_tables(offset + jnp.arange(block_len, dtype=jnp.int32))
    flat_in = inputs.reshape(tokens, width).astype(jnp.float32)
    scale_one = rms_scale(flat_in)
    normal_one = flat_in * scale_one
    normed_one = (normal_one * gain_attn).astype(jnp.bfloat16)
    query_lin = matmul(normed_one, query_full).reshape(seq_here, block_len, q_heads, HD)
    key_lin = matmul(normed_one, key_full).reshape(seq_here, block_len, kv_heads, HD)
    value_low = (
        matmul(normed_one, value_full)
        .astype(jnp.bfloat16)
        .reshape(seq_here, block_len, kv_heads * HD)
    )
    query_scale = rms_scale(query_lin)
    query_normal = query_lin * query_scale
    query_rot = (
        rotate(query_normal * gain_query, cosine_table, sine_table)
        .astype(jnp.bfloat16)
        .reshape(seq_here, block_len, q_heads * HD)
    )
    key_scale = rms_scale(key_lin)
    key_normal = key_lin * key_scale
    key_rot = (
        rotate(key_normal * gain_key, cosine_table, sine_table)
        .astype(jnp.bfloat16)
        .reshape(seq_here, block_len, kv_heads * HD)
    )
    key_all, value_all = (
        lax.all_gather(key_rot, "context", axis=1, tiled=True),
        lax.all_gather(value_low, "context", axis=1, tiled=True),
    )
    full_len = key_all.shape[1]

    def attend_forward(operands):
        query_rows, key_rows, value_rows, length = operands
        scores, grouped, keyed = score_block(query_rows, key_rows, length, offset)
        row_max = jnp.max(scores, axis=-1, keepdims=True)
        exponent = jnp.exp(scores - row_max)
        row_sum = jnp.sum(exponent, axis=-1, keepdims=True)
        probability = (exponent / row_sum).astype(jnp.bfloat16)
        mixed_heads = jnp.einsum(
            "kgqs,skd->qkgd",
            probability,
            value_rows.reshape(full_len, kv_heads, HD),
            preferred_element_type=jnp.float32,
        )
        return (
            mixed_heads.reshape(block_len, q_heads * HD).astype(jnp.bfloat16),
            row_max + jnp.log(row_sum),
        )

    mixed_low, log_total = lax.map(attend_forward, (query_rot, key_all, value_all, lengths))
    mixed_flat = mixed_low.reshape(tokens, q_heads * HD)
    attention = lax.psum(matmul(mixed_flat, out_full), "tensor")
    middle = flat_in + attention
    scale_two = rms_scale(middle)
    normal_two = middle * scale_two
    normed_two = (normal_two * gain_ffn).astype(jnp.bfloat16)
    gate_proj = matmul(normed_two, gate_full)
    up_proj = matmul(normed_two, up_full)
    sigmoid_gate = jax.nn.sigmoid(gate_proj)
    silu_gate = gate_proj * sigmoid_gate
    hidden = (silu_gate * up_proj).astype(jnp.bfloat16)
    feed = lax.psum(matmul(hidden, down_full).astype(jnp.bfloat16), "tensor").astype(jnp.float32)
    outputs = (middle + feed).astype(jnp.bfloat16).reshape(seq_here, block_len, width)
    live_mask = (
        (offset + jnp.arange(block_len, dtype=jnp.int32))[None, :] < lengths[:, None]
    ).astype(jnp.float32)
    upstream = (cotangent.astype(jnp.float32) * live_mask[:, :, None]).reshape(tokens, width)
    feed_low = upstream.astype(jnp.bfloat16)
    down_grad = left_transposed(hidden, feed_low)
    hidden_grad = right_transposed(feed_low, down_full)
    gate_grad = (
        hidden_grad * up_proj * sigmoid_gate * (1.0 + gate_proj * (1.0 - sigmoid_gate))
    ).astype(jnp.bfloat16)
    up_grad = (hidden_grad * silu_gate).astype(jnp.bfloat16)
    gate_weight_grad = left_transposed(normed_two, gate_grad)
    up_weight_grad = left_transposed(normed_two, up_grad)
    normed_two_grad = lax.psum(
        right_transposed(gate_grad, gate_full) + right_transposed(up_grad, up_full), "tensor"
    )
    gain_ffn_grad = jnp.sum(normed_two_grad * normal_two, axis=0)
    middle_grad = upstream + norm_back(normed_two_grad * gain_ffn, normal_two, scale_two)
    attn_low = middle_grad.astype(jnp.bfloat16)
    out_weight_grad = left_transposed(mixed_flat, attn_low)
    mixed_grad = (
        right_transposed(attn_low, out_full)
        .astype(jnp.bfloat16)
        .reshape(seq_here, block_len, q_heads * HD)
    )

    def attend_backward(operands):
        query_rows, key_rows, value_rows, length, log_row, grad_rows = operands
        scores, grouped, keyed = score_block(query_rows, key_rows, length, offset)
        probability = jnp.exp(scores - log_row)
        weights_low = probability.astype(jnp.bfloat16)
        value_heads = value_rows.reshape(full_len, kv_heads, HD)
        grad_heads = grad_rows.reshape(block_len, kv_heads, q_heads // kv_heads, HD)
        prob_grad = jnp.einsum(
            "qkgd,skd->kgqs", grad_heads, value_heads, preferred_element_type=jnp.float32
        )
        delta = jnp.sum(probability * prob_grad, axis=-1, keepdims=True)
        score_grad = (probability * (prob_grad - delta)).astype(jnp.bfloat16)
        value_part = jnp.einsum(
            "kgqs,qkgd->skd", weights_low, grad_heads, preferred_element_type=jnp.float32
        )
        query_part = jnp.einsum(
            "kgqs,skd->qkgd", score_grad, keyed, preferred_element_type=jnp.float32
        ) * HD ** (-0.5)
        key_part = jnp.einsum(
            "kgqs,qkgd->skd", score_grad, grouped, preferred_element_type=jnp.float32
        ) * HD ** (-0.5)
        return (
            query_part.reshape(block_len, q_heads * HD),
            key_part.reshape(full_len, kv_heads * HD),
            value_part.reshape(full_len, kv_heads * HD),
        )

    query_grad, key_part, value_part = lax.map(
        attend_backward, (query_rot, key_all, value_all, lengths, log_total, mixed_grad)
    )
    key_grad, value_grad = (
        lax.psum_scatter(key_part, "context", scatter_dimension=1, tiled=True),
        lax.psum_scatter(value_part, "context", scatter_dimension=1, tiled=True),
    )
    query_unrot = unrotate(
        query_grad.reshape(seq_here, block_len, q_heads, HD), cosine_table, sine_table
    )
    key_unrot = unrotate(
        key_grad.reshape(seq_here, block_len, kv_heads, HD), cosine_table, sine_table
    )
    gain_query_grad = jnp.sum(query_unrot * query_normal, axis=(0, 1, 2))
    gain_key_grad = jnp.sum(key_unrot * key_normal, axis=(0, 1, 2))
    query_lin_grad = (
        norm_back(query_unrot * gain_query, query_normal, query_scale)
        .astype(jnp.bfloat16)
        .reshape(tokens, q_heads * HD)
    )
    key_lin_grad = (
        norm_back(key_unrot * gain_key, key_normal, key_scale)
        .astype(jnp.bfloat16)
        .reshape(tokens, kv_heads * HD)
    )
    value_lin_grad = value_grad.astype(jnp.bfloat16).reshape(tokens, kv_heads * HD)
    query_weight_grad = left_transposed(normed_one, query_lin_grad)
    key_weight_grad = left_transposed(normed_one, key_lin_grad)
    value_weight_grad = left_transposed(normed_one, value_lin_grad)
    normed_one_part = (
        right_transposed(query_lin_grad, query_full)
        + right_transposed(key_lin_grad, key_full)
        + right_transposed(value_lin_grad, value_full)
    )
    normed_one_grad, head_grad = lax.psum(
        (normed_one_part, jnp.stack([gain_query_grad, gain_key_grad])), "tensor"
    )
    gain_attn_grad = jnp.sum(normed_one_grad * normal_one, axis=0)
    input_grad = (
        middle_grad + norm_back(normed_one_grad * gain_attn, normal_one, scale_one)
    ).reshape(seq_here, block_len, width)
    gain_stack = jnp.stack([gain_attn_grad, gain_ffn_grad])
    (
        query_shard,
        key_shard,
        value_shard,
        out_shard,
        gate_shard,
        up_shard,
        down_shard,
        gain_shard,
        head_shard,
    ) = (
        lax.psum_scatter(query_weight_grad, "dp", scatter_dimension=0, tiled=True),
        lax.psum_scatter(key_weight_grad, "dp", scatter_dimension=0, tiled=True),
        lax.psum_scatter(value_weight_grad, "dp", scatter_dimension=0, tiled=True),
        lax.psum_scatter(out_weight_grad, "dp", scatter_dimension=1, tiled=True),
        lax.psum_scatter(gate_weight_grad, "dp", scatter_dimension=0, tiled=True),
        lax.psum_scatter(up_weight_grad, "dp", scatter_dimension=0, tiled=True),
        lax.psum_scatter(down_grad, "dp", scatter_dimension=1, tiled=True),
        lax.psum_scatter(gain_stack, "dp", scatter_dimension=1, tiled=True),
        lax.psum_scatter(head_grad, "dp", scatter_dimension=1, tiled=True),
    )
    (
        query_shard,
        key_shard,
        value_shard,
        out_shard,
        gate_shard,
        up_shard,
        down_shard,
        gain_shard,
        head_shard,
    ) = lax.psum(
        (
            query_shard,
            key_shard,
            value_shard,
            out_shard,
            gate_shard,
            up_shard,
            down_shard,
            gain_shard,
            head_shard,
        ),
        "context",
    )
    return (
        outputs,
        input_grad,
        query_shard,
        key_shard,
        value_shard,
        out_shard,
        gate_shard,
        up_shard,
        down_shard,
        gain_shard,
        head_shard,
    )


def solution(mesh):
    in_specs = (
        P("dp", "context", None),
        P("dp"),
        P("dp", "tensor"),
        P("dp", "tensor"),
        P("dp", "tensor"),
        P("tensor", "dp"),
        P("dp", "tensor"),
        P("dp", "tensor"),
        P("tensor", "dp"),
        P(None, "dp"),
        P(None, "dp"),
        P("dp", "context", None),
    )
    out_specs = (
        P("dp", "context", None),
        P("dp", "context", None),
        P("dp", "tensor"),
        P("dp", "tensor"),
        P("dp", "tensor"),
        P("tensor", "dp"),
        P("dp", "tensor"),
        P("dp", "tensor"),
        P("tensor", "dp"),
        P(None, "dp"),
        P(None, "dp"),
    )
    return jax.shard_map(
        on_device, mesh=mesh, in_specs=in_specs, out_specs=out_specs, check_vma=False
    )
```

profile of v0, /device:TPU:0, one launch (start us, length us, event | category | flops | bytes accessed | tf_op | source)
XLA Modules:
  0.0 1917.1 jit_solution(4093974741665338262)
XLA Ops:
  8.0 12.9 all_gather.33
  31.1 19.5 %all_gather.36 = bf16[1024,256]{1,0:T(8,128)(2,1)S(1)} all-gather(bf16[256,256]{1,0:T(8,128)(2,1)} %param.19), channel_id=1, replica_groups=mesh['dp'=4,'context'=4,'tensor'=2] {'dp'}, dimensions={0}, use_global_device_ids=true | all-gather | bytes 655360 | tf_op jit(solution)/shard_map/all_gather | solution.py:115
  57.5 14.8 all_gather.34
  83.2 22.7 %all-gather.9.cloned.1.call-done = bf16[4,1024,256]{1,2,0:T(8,128)(2,1)} async-done(((bf16[4,256,256]{1,2,0:T(8,128)(2,1)}), bf16[4,1024,256]{1,2,0:T(8,128)(2,1)}) %all-gather.9.cloned.1.call-update) | async-done | bytes 2097168 | tf_op jit(solution)/shard_map/all_gather | solution.py:158
  105.8 40.4 %while.26 = (s32[]{:T(128)}, bf16[4,256,512]{2,1,0:T(8,128)(2,1)}, f32[4,4,2,256,1]{3,2,1,4,0:T(2,128)S(1)}, bf16[4,1024,256]{1,2,0:T(8,128)(2,1)}, s32[]{:T(128...) while((s32[]{:T(128)}, bf16[4,256,512]{2,1,0:T(8,128)(2,1)}, ...), condition=%wide.region_6.7_spmd, body=%wide.region_3.6_spmd.sunk | while | flops 562691328 | bytes 31527548 | solution.py:180
  159.4 99.8 %all-reduce.8.cloned.1.call-done = f32[1024,1024]{1,0:T(8,128)} async-done(((f32[1024,1024]{1,0:T(8,128)}), f32[1024,1024]{1,0:T(8,128)}) %all-reduce.8.cloned.1.call-update) | async-done | bytes 4194320 | tf_op jit(solution)/shard_map/psum | solution.py:182
  264.3 85.7 %all-gather.17.cloned.1.call-done = bf16[1024,2304]{1,0:T(8,128)(2,1)} async-done(((bf16[256,2304]{1,0:T(8,128)(2,1)}), bf16[1024,2304]{1,0:T(8,128)(2,1)}) %all-gather.17.cloned.1.call-update) | async-done | bytes 4718608 | tf_op jit(solution)/shard_map/all_gather | solution.py:118
  350.0 9.7 fusion.45
  359.8 79.7 %all-gather.19.cloned.1.call-done = bf16[1024,2304]{1,0:T(8,128)(2,1)} async-done(((bf16[256,2304]{1,0:T(8,128)(2,1)}), bf16[1024,2304]{1,0:T(8,128)(2,1)}) %all-gather.19.cloned.1.call-update) | async-done | bytes 4718608 | tf_op jit(solution)/shard_map/all_gather | solution.py:119
  439.4 10.0 fusion.46
  449.4 79.1 %all-gather.21.cloned.1.call-done = bf16[2304,1024]{1,0:T(8,128)(2,1)} async-done(((bf16[2304,256]{1,0:T(8,128)(2,1)}), bf16[2304,1024]{1,0:T(8,128)(2,1)}) %all-gather.21.cloned.1.call-update) | async-done | bytes 4718608 | tf_op jit(solution)/shard_map/all_gather | solution.py:120
  528.5 18.2 multiply_convert_fusion
  562.3 9.2 convolution_convert_fusion
  571.6 96.7 %all-reduce.12.cloned.1.call-done = f32[1024,1024]{1,0:T(8,128)} async-done(((f32[1024,1024]{1,0:T(8,128)}), f32[1024,1024]{1,0:T(8,128)}) %all-reduce.12.cloned.1.call-update) | async-done | bytes 4194320 | tf_op jit(solution)/shard_map/psum | solution.py:207
  673.4 60.6 %all-reduce.10.cloned.1.call-done = bf16[1024,1024]{1,0:T(8,128)(2,1)} async-done(((bf16[1024,1024]{1,0:T(8,128)(2,1)}), bf16[1024,1024]{1,0:T(8,128)(2,1)}) %all-reduce.10.cloned.1.call-update) | async-done | bytes 2097168 | tf_op jit(solution)/shard_map/psum | solution.py:192
  745.5 102.2 %while.27 = (s32[]{:T(128)}, f32[4,256,512]{1,2,0:T(8,128)}, f32[4,1024,256]{1,2,0:T(8,128)}, f32[4,1024,256]{2,1,0:T(8,128)}, bf16[4,1024,256]{1,2,0:T(8,128)(2...) while((s32[]{:T(128)}, f32[4,256,512]{1,2,0:T(8,128)}, ...), condition=%wide.region_14.15_spmd, body=%wide.region_12.14_spmd.sunk | while | flops 1374551296 | bytes 105445064 | solution.py:247
  854.0 38.2 %reduce-scatter.16.cloned.1.call-done = f32[4,256,256]{1,2,0:T(8,128)} async-done(((f32[4,1024,256]{1,2,0:T(8,128)}), f32[4,256,256]{1,2,0:T(8,128)}) %reduce-scatter.16.cloned.1.call-update) | async-done | bytes 1048592 | tf_op jit(solution)/shard_map/reduce_scatter | solution.py:251
  897.8 41.3 %reduce-scatter.18.cloned.1.call-done = f32[4,256,256]{2,1,0:T(8,128)} async-done(((f32[4,1024,256]{2,1,0:T(8,128)}), f32[4,256,256]{2,1,0:T(8,128)}) %reduce-scatter.18.cloned.1.call-update) | async-done | bytes 1048592 | tf_op jit(solution)/shard_map/reduce_scatter | solution.py:252
  960.0 10.2 fusion.52
  971.9 9.8 fusion.53
  983.4 9.8 fusion.54
  994.1 59.0 %all-reduce.14.cloned.1.call-done = f32[1024,1024]{1,0:T(8,128)} async-done(((f32[1024,1024]{1,0:T(8,128)}), f32[1024,1024]{1,0:T(8,128)}) %all-reduce.14.cloned.1.call-update) | async-done | bytes 4194320 | tf_op jit(solution)/shard_map/psum | solution.py:281
  1057.6 41.9 %reduce-scatter.20.cloned.1.call-done = f32[256,512]{1,0:T(8,128)} async-done(((f32[1024,512]{1,0:T(8,128)}), f32[256,512]{1,0:T(8,128)}) %reduce-scatter.20.cloned.1.call-update) | async-done | bytes 524304 | tf_op jit(solution)/shard_map/reduce_scatter | solution.py:300
  1099.6 45.0 %reduce-scatter.26.cloned.1.call-done = f32[512,256]{1,0:T(8,128)} async-done(((f32[512,1024]{1,0:T(8,128)}), f32[512,256]{1,0:T(8,128)}) %reduce-scatter.26.cloned.1.call-update) | async-done | bytes 524304 | tf_op jit(solution)/shard_map/reduce_scatter | solution.py:303
  1144.6 28.7 %reduce-scatter.22.cloned.1.call-done = f32[256,256]{1,0:T(8,128)} async-done(((f32[1024,256]{1,0:T(8,128)}), f32[256,256]{1,0:T(8,128)}) %reduce-scatter.22.cloned.1.call-update) | async-done | bytes 262160 | tf_op jit(solution)/shard_map/reduce_scatter | solution.py:301
  1173.2 27.9 %reduce-scatter.24.cloned.1.call-done = f32[256,256]{1,0:T(8,128)} async-done(((f32[1024,256]{1,0:T(8,128)}), f32[256,256]{1,0:T(8,128)}) %reduce-scatter.24.cloned.1.call-update) | async-done | bytes 262160 | tf_op jit(solution)/shard_map/reduce_scatter | solution.py:302
  1201.2 161.9 %reduce-scatter.28.cloned.1.call-done = f32[256,2304]{1,0:T(8,128)} async-done(((f32[1024,2304]{1,0:T(8,128)}), f32[256,2304]{1,0:T(8,128)}) %reduce-scatter.28.cloned.1.call-update) | async-done | bytes 2359312 | tf_op jit(solution)/shard_map/reduce_scatter | solution.py:304
  1363.1 164.5 %reduce-scatter.30.cloned.1.call-done = f32[256,2304]{1,0:T(8,128)} async-done(((f32[1024,2304]{1,0:T(8,128)}), f32[256,2304]{1,0:T(8,128)}) %reduce-scatter.30.cloned.1.call-update) | async-done | bytes 2359312 | tf_op jit(solution)/shard_map/reduce_scatter | solution.py:305
  1527.7 164.4 %reduce-scatter.32.cloned.1.call-done = f32[2304,256]{1,0:T(8,128)} async-done(((f32[2304,1024]{1,0:T(8,128)}), f32[2304,256]{1,0:T(8,128)}) %reduce-scatter.32.cloned.1.call-update) | async-done | bytes 2359312 | tf_op jit(solution)/shard_map/reduce_scatter | solution.py:306
  1692.1 23.0 %reduce-scatter.36.cloned.1.call-done = f32[16,2]{1,0:T(8,128)} async-done(((f32[64,2]{1,0:T(8,128)}), f32[16,2]{1,0:T(8,128)}) %reduce-scatter.36.cloned.1.call-update) | async-done | bytes 144
  1726.3 11.6 reduce-scatter.34.cloned.1.call-done
  1745.1 151.6 %all-reduce.16.cloned.1.call-done = (f32[256,512]{1,0:T(8,128)}, f32[256,256]{1,0:T(8,128)}, f32[256,256]{1,0:T(8,128)}, f32[512,256]{1,0:T(8,128)}, f32[256,230...) async-done(((f32[256,512]{1,0:T(8,128)}, f32[256,256]{1,0:T(8,128)}, f32[256,256]{1,0:T(8,128)}, f32[512,256]{1,0:T(8,128)}, f32[256,2304]{1,0:T(8,128)}, ...) | async-done | bytes 8650768 | tf_op jit(solution)/shard_map/psum | solution.py:320
  (370 shorter events, 293.7 us)
Async XLA Ops:
  7.2 68.4 %all-gather.13.cloned.1.call-start = ((), (), s32[]{:S(2)}) async-start(), calls=%async_computation.13 | async-start | bytes 1310720 | tf_op jit(solution)/shard_map/all_gather | solution.py:114
  7.9 75.2 %all-gather.11.cloned.1.call-start = ((), (), s32[]{:S(2)}) async-start(), calls=%async_computation.12 | async-start | bytes 2621440 | tf_op jit(solution)/shard_map/all_gather | solution.py:157
  20.9 51.4 %copy-start.34 = (f32[1,1024]{1,0:T(1,128)}, f32[1,1024]{1,0:T(1,128)S(1)}, u32[]{:S(2)}) copy-start(f32[1,1024]{1,0:T(1,128)S(1)} %get-tuple-element.230) | copy-start | bytes 12292
  31.1 48.9 %copy-start.39 = (f32[64]{0:T(128)}, f32[64]{0:T(128)S(1)}, u32[]{:S(2)}) copy-start(f32[64]{0:T(128)S(1)} %get-tuple-element.235) | copy-start | bytes 772
  57.4 48.5 %all-gather.9.cloned.1.call-start = ((), (), s32[]{:S(2)}) async-start(), calls=%async_computation.11 | async-start | bytes 2621440 | tf_op jit(solution)/shard_map/all_gather | solution.py:158
  74.6 71.7 %all-gather.15.cloned.1.call-start = ((), (), s32[]{:S(2)}) async-start(), calls=%async_computation.14 | async-start | bytes 1310720 | tf_op jit(solution)/shard_map/all_gather | solution.py:117
  75.2 184.0 %all-reduce.8.cloned.1.call-start = ((), (), s32[]{:S(2)}) async-start(), calls=%async_computation.15 | async-start | bytes 8388608 | tf_op jit(solution)/shard_map/psum | solution.py:182
  151.1 198.9 %all-gather.17.cloned.1.call-start = ((), (), s32[]{:S(2)}) async-start(), calls=%async_computation.16 | async-start | bytes 5898240 | tf_op jit(solution)/shard_map/all_gather | solution.py:118
  151.7 287.7 %all-gather.19.cloned.1.call-start = ((), (), s32[]{:S(2)}) async-start(), calls=%async_computation.17 | async-start | bytes 5898240 | tf_op jit(solution)/shard_map/all_gather | solution.py:119
  152.4 376.1 %all-gather.21.cloned.1.call-start = ((), (), s32[]{:S(2)}) async-start(), calls=%async_computation.18 | async-start | bytes 5898240 | tf_op jit(solution)/shard_map/all_gather | solution.py:120
  153.2 515.1 %all-reduce.12.cloned.1.call-start = ((), (), s32[]{:S(2)}) async-start(), calls=%async_computation.20 | async-start | bytes 8388608 | tf_op jit(solution)/shard_map/psum | solution.py:207
  264.3 85.7 %copy-start.23 = (bf16[1024,1024]{1,0:T(8,128)(2,1)}, bf16[1024,1024]{1,0:T(8,128)(2,1)S(1)}, u32[]{:S(2)}) copy-start(bf16[1024,1024]{1,0:T(8,128)(2,1)S(1)} %multiply_convert_fusion.3) | copy-start | bytes 6291460
  359.8 168.8 %copy-start.17 = (bf16[1024,1024]{1,0:T(8,128)(2,1)S(1)}, bf16[1024,1024]{1,0:T(8,128)(2,1)}, u32[]{:S(2)}) copy-start(bf16[1024,1024]{1,0:T(8,128)(2,1)} %bitcast_convert_fusion) | copy-start | bytes 6291460
  562.0 172.0 %all-reduce.10.cloned.1.call-start = ((), (), s32[]{:S(2)}) async-start(), calls=%async_computation.19 | async-start | bytes 4194304 | tf_op jit(solution)/shard_map/psum | solution.py:192
  571.5 320.7 %reduce-scatter.16.cloned.1.call-start = ((), (), s32[]{:S(2)}) async-start(), calls=%async_computation.21 | async-start | bytes 5242880 | tf_op jit(solution)/shard_map/reduce_scatter | solution.py:251
  673.4 69.8 %copy-start.45 = (bf16[512,1024]{1,0:T(8,128)(2,1)S(1)}, bf16[512,1024]{1,0:T(8,128)(2,1)}, u32[]{:S(2)}) copy-start(bf16[512,1024]{1,0:T(8,128)(2,1)} %all-gather.15.cloned.1.call-done) | copy-start | bytes 3145732
  847.7 91.4 %reduce-scatter.18.cloned.1.call-start = ((), (), s32[]{:S(2)}) async-start(), calls=%async_computation.22 | async-start | bytes 5242880 | tf_op jit(solution)/shard_map/reduce_scatter | solution.py:252
  848.3 204.9 %all-reduce.14.cloned.1.call-start = ((), (), s32[]{:S(2)}) async-start(), calls=%async_computation.23 | async-start | bytes 8388608 | tf_op jit(solution)/shard_map/psum | solution.py:281
  945.1 154.4 %reduce-scatter.20.cloned.1.call-start = ((), (), s32[]{:S(2)}) async-start(), calls=%async_computation.24 | async-start | bytes 2621440 | tf_op jit(solution)/shard_map/reduce_scatter | solution.py:300
  950.6 194.0 %reduce-scatter.26.cloned.1.call-start = ((), (), s32[]{:S(2)}) async-start(), calls=%async_computation.27 | async-start | bytes 2621440 | tf_op jit(solution)/shard_map/reduce_scatter | solution.py:303
  956.0 217.2 %reduce-scatter.22.cloned.1.call-start = ((), (), s32[]{:S(2)}) async-start(), calls=%async_computation.25 | async-start | bytes 1310720 | tf_op jit(solution)/shard_map/reduce_scatter | solution.py:301
  957.9 243.3 %reduce-scatter.24.cloned.1.call-start = ((), (), s32[]{:S(2)}) async-start(), calls=%async_computation.26 | async-start | bytes 1310720 | tf_op jit(solution)/shard_map/reduce_scatter | solution.py:302
  959.7 403.4 %reduce-scatter.28.cloned.1.call-start = ((), (), s32[]{:S(2)}) async-start(), calls=%async_computation.28 | async-start | bytes 11796480 | tf_op jit(solution)/shard_map/reduce_scatter | solution.py:304
  970.2 557.5 %reduce-scatter.30.cloned.1.call-start = ((), (), s32[]{:S(2)}) async-start(), calls=%async_computation.29 | async-start | bytes 11796480 | tf_op jit(solution)/shard_map/reduce_scatter | solution.py:305
  981.8 710.3 %reduce-scatter.32.cloned.1.call-start = ((), (), s32[]{:S(2)}) async-start(), calls=%async_computation.30 | async-start | bytes 11796480 | tf_op jit(solution)/shard_map/reduce_scatter | solution.py:306
  993.2 59.9 %copy-start.1 = (bf16[4,256,1024]{2,1,0:T(8,128)(2,1)S(1)}, bf16[4,256,1024]{2,1,0:T(8,128)(2,1)}, u32[]{:S(2)}) copy-start(bf16[4,256,1024]{2,1,0:T(8,128)(2,1)} %param.16) | copy-start | bytes 6291460
  993.2 59.9 %copy-start.35 = (f32[1,1024]{1,0:T(1,128)S(1)}, f32[1,1024]{1,0:T(1,128)}, u32[]{:S(2)}) copy-start(f32[1,1024]{1,0:T(1,128)} %copy-done.34) | copy-start | bytes 12292
  993.2 59.9 %copy-start.37 = (f32[1,2,4,128]{3,1,2,0:T(2,128)S(1)}, f32[1,2,4,128]{3,1,2,0:T(2,128)}, u32[]{:S(2)}) copy-start(f32[1,2,4,128]{3,1,2,0:T(2,128)} %copy-done.36) | copy-start | bytes 12292
  993.3 63.2 %copy-start.38 = (f32[1024]{0:T(1024)S(1)}, f32[1024]{0:T(1024)}, u32[]{:S(2)}) copy-start(f32[1024]{0:T(1024)} %get-tuple-element.151) | copy-start | bytes 12292
  993.3 721.8 %reduce-scatter.36.cloned.1.call-start = ((), (), s32[]{:S(2)}) async-start(), calls=%async_computation.32 | async-start | bytes 40960
  994.1 743.8 %reduce-scatter.34.cloned.1.call-start = ((), (), s32[]{:S(2)}) async-start(), calls=%async_computation.31 | async-start | bytes 655360
  1057.6 839.1 %all-reduce.16.cloned.1.call-start = ((), (), s32[]{:S(2)}) async-start(), calls=%async_computation.33 | async-start | bytes 17301504 | tf_op jit(solution)/shard_map/psum | solution.py:320
  (46 other events, 556.7 us)
Sparse Core Ops, SparseCore 0:
  9.6 37.6 all-gather.12
  57.5 23.3 all-gather.10
  83.0 22.8 all-gather.8
  107.2 29.8 all-gather.14
  151.2 107.9 all-reduce.7
  260.6 89.3 all-gather.16
  351.6 87.7 all-gather.18
  441.0 87.5 all-gather.20
  562.1 106.0 all-reduce.11
  671.0 62.9 all-reduce.9
  847.8 44.3 reduce-scatter.15
  894.6 44.4 reduce-scatter.17
  945.2 107.8 all-reduce.13
  1055.9 43.6 reduce-scatter.19
  1101.7 42.8 reduce-scatter.25
  1146.7 26.4 reduce-scatter.21
  1175.4 25.7 reduce-scatter.23
  1203.4 159.6 reduce-scatter.27
  1365.5 162.1 reduce-scatter.29
  1529.9 162.1 reduce-scatter.31
  1694.9 20.1 reduce-scatter.35
  1717.9 19.9 reduce-scatter.33
  1741.2 155.4 all-reduce.15
where the time goes:
time: 1920 us
  waiting for transfers between devices  1490 us (78%)
  matrix products  197 us (10%)
  local copies, waits for them, and re-layouts  82.1 us (4%)
  blocking collectives  66.4 us (3%)
  other arithmetic  66.3 us (3%)
    reduce_scatter x1, waiting for transfers between devices, on_device(): lax.psum_scatter(up_weight_grad, 'dp', scatter_dimension=0, tiled=True)  165 us
    reduce_scatter x1, waiting for transfers between devices, on_device(): lax.psum_scatter(down_grad, 'dp', scatter_dimension=1, tiled=True)  164 us
    reduce_scatter x1, waiting for transfers between devices, on_device(): lax.psum_scatter(gate_weight_grad, 'dp', scatter_dimension=0, tiled=True)  162 us
    psum x1, waiting for transfers between devices, on_device(): lax.psum((query_shard, key_shard, value_shard, out_shard, gate_shard, up_...  152 us
    psum x1, waiting for transfers between devices, on_device(): attention = lax.psum(matmul(mixed_flat, out_full), 'tensor')  99.8 us
    psum x1, waiting for transfers between devices, on_device(): lax.psum(right_transposed(gate_grad, gate_full) + right_transposed(up_gra...  96.7 us
    all_gather x1, waiting for transfers between devices, on_device(): lax.all_gather(gate_weight, 'dp', axis=0, tiled=True)  85.7 us
    all_gather x1, waiting for transfers between devices, on_device(): lax.all_gather(up_weight, 'dp', axis=0, tiled=True)  79.7 us
  transfers between devices with their start and end apart: 23, of which 20 were waited for; matrix products, arithmetic and copies ran while one was open for 9% of the time, Pallas kernels for 0%

commit v1 on v0

v1 whole, which is shorter than its diff:
```python
import functools

import jax
import jax.numpy as jnp
from jax import lax
from jax.experimental import pallas as pl
from jax.experimental.pallas import tpu as pltpu
from jax.sharding import PartitionSpec as P

HD = 64
ROWS = 256

epsilon = 1e-05
rope_base = 1000000.0

f32 = jnp.float32
bf16 = jnp.bfloat16

LANE_SWAP = [(0, 1), (1, 0), (2, 3), (3, 2)]
PAIR_SWAP = [(0, 2), (2, 0), (1, 3), (3, 1)]
SIDE_SWAP = [(0, 1), (1, 0)]
TURN = [(0, 0), (1, 2), (2, 1), (3, 3)]
TWIST_IN = [(0, 2), (1, 0), (2, 3), (3, 1)]
TWIST_OUT = [(b, a) for a, b in TWIST_IN]
CROSS = [(0, 0), (1, 2), (2, 1), (3, 3), (4, 4), (5, 6), (6, 5), (7, 7)]


def lane_swap(value):
    return lax.ppermute(value, "context", LANE_SWAP)


def pair_swap(value):
    return lax.ppermute(value, "context", PAIR_SWAP)


def side_swap(value):
    return lax.ppermute(value, "tensor", SIDE_SWAP)


def cross_swap(value):
    return lax.ppermute(value, ("context", "tensor"), CROSS)


def nn(left, right):
    return jnp.dot(left, right, preferred_element_type=f32)


def nt(left, right):
    return lax.dot_general(left, right, (((1,), (1,)), ((), ())), preferred_element_type=f32)


def tn(left, right):
    return lax.dot_general(left, right, (((0,), (0,)), ((), ())), preferred_element_type=f32)


def rms_scale(values):
    return lax.rsqrt(jnp.mean(values * values, axis=-1, keepdims=True) + epsilon)


def norm_back(upstream, normal, scale):
    return scale * (upstream - normal * jnp.mean(upstream * normal, axis=-1, keepdims=True))


def rope_tables(full_len):
    half_width = HD // 2
    frequency = rope_base ** (-2.0 * jnp.arange(half_width, dtype=f32) / HD)
    angles = jnp.arange(full_len, dtype=jnp.int32).astype(f32)[:, None] * frequency[None, :]
    cosine, sine = jnp.cos(angles), jnp.sin(angles)
    return (
        jnp.concatenate([cosine, cosine, cosine, cosine], axis=1),
        jnp.concatenate([-sine, sine, -sine, sine], axis=1),
    )


def head_ones():
    row = lax.broadcasted_iota(jnp.int32, (128, 128), 0) // HD
    column = lax.broadcasted_iota(jnp.int32, (128, 128), 1) // HD
    return (row == column).astype(bf16)


def head_sum(values, ones):
    high = values.astype(bf16)
    low = (values - high.astype(f32)).astype(bf16)
    return nn(high, ones) + nn(low, ones)


def half_turn(values):
    lane = lax.broadcasted_iota(jnp.int32, values.shape, 1)
    return jnp.where(lane % HD < HD // 2, pltpu.roll(values, 128 - HD // 2, 1), pltpu.roll(values, HD // 2, 1))


def attend_forward_kernel(
    table, qkv_ref, cos_ref, sin_ref, gain_ref, out_ref, inv_ref, qr_ref, kr_ref, vx_ref
):
    full_len = qkv_ref.shape[0]
    blocks = full_len // ROWS
    length = table[blocks]
    ones = head_ones()
    lane = lax.broadcasted_iota(jnp.int32, (ROWS, 128), 1)
    for block in range(blocks):
        local = pl.ds(pl.multiple_of(table[block] * ROWS, ROWS), ROWS)
        rows = slice(block * ROWS, (block + 1) * ROWS)
        cosine, sine = cos_ref[rows, :], sin_ref[rows, :]
        for part in range(3):
            value = qkv_ref[local, part * 128 : (part + 1) * 128]
            scale = lax.rsqrt(head_sum(value * value, ones) * (1.0 / HD) + epsilon)
            scaled = value * scale * gain_ref[min(part, 2) // 2 : min(part, 2) // 2 + 1, :]
            turned = (scaled * cosine + half_turn(scaled) * sine).astype(bf16)
            if part < 2:
                qr_ref[rows, part * 128 : (part + 1) * 128] = turned * HD ** (-0.5)
            else:
                kr_ref[rows, :] = turned
        value = qkv_ref[local, 384:512]
        position = block * ROWS + lax.broadcasted_iota(jnp.int32, (ROWS, 128), 0)
        valid = (position < length).astype(f32)
        value = value * valid
        vx_ref[0, rows, :] = jnp.where(lane < HD, value, valid).astype(bf16)
        vx_ref[1, rows, :] = jnp.where(lane < HD, pltpu.roll(value, HD, 1), valid).astype(bf16)
    for block in range(blocks):
        local = pl.ds(pl.multiple_of(table[block] * ROWS, ROWS), ROWS)
        rows = slice(block * ROWS, (block + 1) * ROWS)
        extent = (block + 1) * ROWS
        for head in range(2):
            query = jnp.concatenate(
                [
                    qr_ref[rows, head * 128 : head * 128 + HD],
                    qr_ref[rows, head * 128 + HD : head * 128 + 128],
                ],
                axis=0,
            )
            key = kr_ref[:extent, head * HD : (head + 1) * HD]
            scores = nt(query, key)
            total = None
            for piece in range(block + 1):
                weight = jnp.exp(scores[:, piece * ROWS : (piece + 1) * ROWS])
                if piece == block:
                    row = lax.broadcasted_iota(jnp.int32, weight.shape, 0) % ROWS
                    column = lax.broadcasted_iota(jnp.int32, weight.shape, 1)
                    weight = jnp.where(column <= row, weight, 0.0)
                term = nn(weight.astype(bf16), vx_ref[head, piece * ROWS : (piece + 1) * ROWS, :])
                total = term if total is None else total + term
            inverse = 1.0 / total
            mixed = total * pltpu.roll(inverse, HD, 1)
            first, second = mixed[:ROWS], mixed[ROWS:]
            inv_first, inv_second = inverse[:ROWS], inverse[ROWS:]
            columns = slice(head * 128, (head + 1) * 128)
            out_ref[local, columns] = jnp.where(lane < HD, first, pltpu.roll(second, HD, 1)).astype(bf16)
            inv_ref[local, columns] = jnp.where(lane < HD, pltpu.roll(inv_first, HD, 1), inv_second)


def attend_backward_kernel(
    table,
    qkv_ref,
    cos_ref,
    sin_ref,
    gain_ref,
    qr_ref,
    kr_ref,
    out_ref,
    inv_ref,
    grad_ref,
    dqkv_ref,
    dgain_ref,
    do_ref,
    vz_ref,
    kz_ref,
    dq_ref,
    dk_ref,
    dv_ref,
):
    full_len = qkv_ref.shape[0]
    blocks = full_len // ROWS
    length = table[blocks]
    ones = head_ones()
    dk_ref[...] = jnp.zeros_like(dk_ref)
    dv_ref[...] = jnp.zeros_like(dv_ref)
    for block in range(blocks):
        local = pl.ds(pl.multiple_of(table[block] * ROWS, ROWS), ROWS)
        rows = slice(block * ROWS, (block + 1) * ROWS)
        position = block * ROWS + lax.broadcasted_iota(jnp.int32, (ROWS, 128), 0)
        valid = (position < length).astype(f32)
        vz_ref[rows, :] = (qkv_ref[local, 384:512] * valid).astype(bf16)
        kz_ref[rows, :] = (kr_ref[rows, :].astype(f32) * valid).astype(bf16)
        do_ref[rows, :] = (grad_ref[local, :].astype(f32) * inv_ref[local, :]).astype(bf16)
    eight = jnp.ones((8, HD), bf16)
    for block in range(blocks):
        local = pl.ds(pl.multiple_of(table[block] * ROWS, ROWS), ROWS)
        rows = slice(block * ROWS, (block + 1) * ROWS)
        for head in range(2):
            low, mid, high = head * 128, head * 128 + HD, head * 128 + 128
            query = jnp.concatenate([qr_ref[rows, low:mid], qr_ref[rows, mid:high]], axis=0)
            upstream = jnp.concatenate([do_ref[rows, low:mid], do_ref[rows, mid:high]], axis=0)
            mixed = jnp.concatenate([out_ref[local, low:mid], out_ref[local, mid:high]], axis=0)
            product = upstream.astype(f32) * mixed.astype(f32)
            product_high = product.astype(bf16)
            product_low = (product - product_high.astype(f32)).astype(bf16)
            delta = (nt(eight, product_high) + nt(eight, product_low))[:1, :]
            dq_total = None
            for piece in range(block + 1):
                keys = slice(piece * ROWS, (piece + 1) * ROWS)
                half = slice(head * HD, (head + 1) * HD)
                weight = jnp.exp(nt(kr_ref[keys, half], query))
                if piece == block:
                    row = lax.broadcasted_iota(jnp.int32, weight.shape, 0)
                    column = lax.broadcasted_iota(jnp.int32, weight.shape, 1) % ROWS
                    weight = jnp.where(row <= column, weight, 0.0)
                score_grad = (weight * (nt(vz_ref[keys, half], upstream) - delta)).astype(bf16)
                dv_ref[head, keys, :] += nn(weight.astype(bf16), upstream)
                dk_ref[head, keys, :] += nn(score_grad, query)
                term = tn(score_grad, kz_ref[keys, half])
                dq_total = term if dq_total is None else dq_total + term
            dq_total = dq_total * HD ** (-0.5)
            dq_ref[rows, low:mid] = dq_total[:ROWS]
            dq_ref[rows, mid:high] = dq_total[ROWS:]
    gain_sums = [jnp.zeros((1, 128), f32) for _ in range(2)]
    for block in range(blocks):
        local = pl.ds(pl.multiple_of(table[block] * ROWS, ROWS), ROWS)
        rows = slice(block * ROWS, (block + 1) * ROWS)
        cosine, sine = cos_ref[rows, :], sin_ref[rows, :]
        position = block * ROWS + lax.broadcasted_iota(jnp.int32, (ROWS, 128), 0)
        valid = position < length
        for part in range(3):
            which = part // 2
            value = qkv_ref[local, part * 128 : (part + 1) * 128]
            scale = lax.rsqrt(head_sum(value * value, ones) * (1.0 / HD) + epsilon)
            normal = value * scale
            if part < 2:
                grad = dq_ref[rows, part * 128 : (part + 1) * 128]
            else:
                grad = jnp.concatenate([dk_ref[0, rows, :], dk_ref[1, rows, :]], axis=1)
                grad = jnp.where(valid, grad, 0.0)
            back = grad * cosine - half_turn(grad) * sine
            gain_sums[which] += jnp.sum(back * normal, axis=0, keepdims=True)
            scaled = back * gain_ref[which : which + 1, :]
            mean = head_sum(scaled * normal, ones) * (1.0 / HD)
            dqkv_ref[local, part * 128 : (part + 1) * 128] = (scale * (scaled - normal * mean)).astype(bf16)
        grad = jnp.concatenate([dv_ref[0, rows, :], dv_ref[1, rows, :]], axis=1)
        dqkv_ref[local, 384:512] = jnp.where(valid, grad, 0.0).astype(bf16)
    dgain_ref[0:1, :] = gain_sums[0]
    dgain_ref[1:2, :] = gain_sums[1]
    dgain_ref[2:8, :] = jnp.zeros((6, 128), f32)


def whole_spec():
    return pl.BlockSpec(memory_space=pltpu.VMEM)


def attend_forward(table, qkv, cosine, sine, gains):
    full_len = qkv.shape[0]
    return pl.pallas_call(
        attend_forward_kernel,
        out_shape=(
            jax.ShapeDtypeStruct((full_len, 256), bf16),
            jax.ShapeDtypeStruct((full_len, 256), f32),
            jax.ShapeDtypeStruct((full_len, 256), bf16),
            jax.ShapeDtypeStruct((full_len, 128), bf16),
        ),
        in_specs=[pl.BlockSpec(memory_space=pltpu.SMEM)] + [whole_spec()] * 4,
        out_specs=(whole_spec(),) * 4,
        scratch_shapes=[pltpu.VMEM((2, full_len, 128), bf16)],
        cost_estimate=pl.CostEstimate(flops=6 * 10**9, bytes_accessed=5 * 10**6, transcendentals=3 * 10**6),
    )(table, qkv, cosine, sine, gains)


def attend_backward(table, qkv, cosine, sine, gains, qr, kr, out, inverse, grad):
    full_len = qkv.shape[0]
    return pl.pallas_call(
        attend_backward_kernel,
        out_shape=(
            jax.ShapeDtypeStruct((full_len, 512), bf16),
            jax.ShapeDtypeStruct((8, 128), f32),
        ),
        in_specs=[pl.BlockSpec(memory_space=pltpu.SMEM)] + [whole_spec()] * 9,
        out_specs=(whole_spec(),) * 2,
        scratch_shapes=[
            pltpu.VMEM((full_len, 256), bf16),
            pltpu.VMEM((full_len, 128), bf16),
            pltpu.VMEM((full_len, 128), bf16),
            pltpu.VMEM((full_len, 256), f32),
            pltpu.VMEM((2, full_len, HD), f32),
            pltpu.VMEM((2, full_len, HD), f32),
        ],
        cost_estimate=pl.CostEstimate(flops=15 * 10**9, bytes_accessed=6 * 10**6, transcendentals=3 * 10**6),
    )(table, qkv, cosine, sine, gains, qr, kr, out, inverse, grad)


def cut(value, index, size, axis):
    return lax.dynamic_slice_in_dim(value, index * size, size, axis)


def pick(flag, first, second):
    return jnp.where(flag, first, second)


def spread(half, lane, side, out_dtype):
    block = half.shape[0] // 2
    first = lax.ppermute(half[:block], "context", TURN)
    second = lax.ppermute(half[block:], "context", TWIST_OUT)
    near = jnp.stack([first, second])
    far = side_swap(near)
    result = jnp.zeros((4,) + first.shape, out_dtype)
    for value, pair, other in ((near[0], 0, 0), (near[1], 1, 0), (far[0], 0, 1), (far[1], 1, 1)):
        place = 2 * lax.rem(lane + pair, 2) + lax.rem(side + other, 2)
        result = lax.dynamic_update_slice(result, value.astype(out_dtype)[None], (place, 0, 0))
    return result


def on_device(
    inputs,
    lengths,
    query_weight,
    key_weight,
    value_weight,
    out_weight,
    gate_weight,
    up_weight,
    down_weight,
    norm_gains,
    head_gains,
    cotangent,
):
    block_len, width = inputs.shape[1:]
    full_len = 4 * block_len
    context = lax.axis_index("context")
    pair, lane, side = context // 2, context % 2, lax.axis_index("tensor")
    owner = lax.axis_index("dp")
    shards = lax.axis_size("dp")
    shard = width // shards
    mine = 2 * pair + side

    q_cols, kv_cols, o_rows = query_weight.shape[1] // 2, key_weight.shape[1] // 2, out_weight.shape[0] // 2
    attn_shard = jnp.concatenate(
        [
            cut(query_weight, lane, q_cols, 1),
            cut(key_weight, lane, kv_cols, 1),
            cut(value_weight, lane, kv_cols, 1),
            cut(out_weight, lane, o_rows, 0).T,
        ],
        axis=1,
    )
    qkv_cols = q_cols + 2 * kv_cols
    attn_own = lax.all_gather(cross_swap(attn_shard), "dp", axis=0, tiled=True)
    qkv_own, out_own = attn_own[:, :qkv_cols], attn_own[:, qkv_cols:]
    qkv_far, out_far = side_swap(qkv_own), side_swap(out_own)

    gains_all = lax.all_gather(jnp.concatenate([norm_gains, head_gains], axis=1), "dp", axis=0)
    gains_full = gains_all[:, :, :shard].transpose(1, 0, 2).reshape(2, width).astype(f32)
    head_full = gains_all[:, :, shard:].transpose(1, 0, 2).reshape(2, HD).astype(f32)
    head_pair = jnp.concatenate([head_full, head_full], axis=1)
    gain_attn, gain_ffn = gains_full[0], gains_full[1]

    hidden = gate_weight.shape[1] // 2
    half_shard = shard // 2
    ffn_shard = jnp.concatenate(
        [
            cut(cut(gate_weight, lane, half_shard, 0), pair, hidden, 1),
            cut(cut(up_weight, lane, half_shard, 0), pair, hidden, 1),
            cut(cut(down_weight, lane, half_shard, 1), pair, hidden, 0).T,
        ],
        axis=1,
    )
    ffn_own = lax.all_gather(ffn_shard, "dp", axis=0, tiled=True).reshape(shards, half_shard, 3 * hidden)
    ffn_far = lane_swap(ffn_own)
    ffn_full = jnp.concatenate(
        [pick(lane == 0, ffn_own, ffn_far), pick(lane == 0, ffn_far, ffn_own)], axis=1
    ).reshape(width, 3 * hidden)
    gate_full, up_full, down_full = (
        ffn_full[:, :hidden],
        ffn_full[:, hidden : 2 * hidden],
        ffn_full[:, 2 * hidden :],
    )

    first_in = lax.ppermute(
        lax.dynamic_index_in_dim(inputs, 2 * lane + side, 0, False), "context", TURN
    )
    second_in = lax.ppermute(
        lax.dynamic_index_in_dim(inputs, 2 * (1 - lane) + side, 0, False), "context", TWIST_IN
    )
    x_half = jnp.concatenate([first_in, second_in], axis=0).astype(f32)
    half_len = x_half.shape[0]

    position = context * block_len + jnp.arange(block_len, dtype=jnp.int32)
    live = position[None, :] < lengths[:, None]
    upstream_low = jnp.where(live[:, :, None], cotangent, jnp.zeros((), bf16))
    up_first = lax.ppermute(upstream_low, "context", TURN)
    up_second = lax.ppermute(upstream_low, "context", TWIST_IN)

    def upstream_rows(sequence, turned):
        one = lax.dynamic_index_in_dim(up_first, sequence, 0, False)
        two = lax.dynamic_index_in_dim(up_second, sequence, 0, False)
        return jnp.concatenate([two, one] if turned else [one, two], axis=0)

    scale_one = rms_scale(x_half)
    normal_one = x_half * scale_one
    normed_half = (normal_one * gain_attn).astype(bf16)
    normed_one = jnp.concatenate([normed_half, lane_swap(normed_half)], axis=0)
    true_block = jnp.arange(4, dtype=jnp.int32)
    local_block = jnp.where(true_block // 2 == lane, 0, 2) + jnp.where(true_block % 2 == pair, 0, 1)
    table = jnp.concatenate([local_block, lax.dynamic_slice_in_dim(lengths, mine, 1)]).astype(jnp.int32)
    cosine, sine = rope_tables(full_len)
    qkv = [nn(normed_one, qkv_own), nn(normed_one, qkv_far)]
    mixed, inverse, q_rot, k_rot = zip(
        *[attend_forward(table, value, cosine, sine, head_pair) for value in qkv]
    )
    attn_part = nt(mixed[0], out_own) + nt(mixed[1], out_far)
    attn_recv = lane_swap(attn_part[half_len:].astype(bf16))
    middle = x_half + attn_part[:half_len] + attn_recv.astype(f32)
    scale_two = rms_scale(middle)
    normal_two = middle * scale_two
    normed_a = (normal_two * gain_ffn).astype(bf16)
    normed_b = side_swap(normed_a)
    normed_c = pair_swap(normed_a)
    normed_d = jnp.concatenate(
        [side_swap(normed_c[:block_len]), pair_swap(normed_b[block_len:])], axis=0
    )

    def feed_forward(normed, grad):
        gate_proj = nn(normed, gate_full)
        up_proj = nn(normed, up_full)
        hidden_grad = nn(grad, down_full)
        sigmoid_gate = jax.nn.sigmoid(gate_proj)
        silu_gate = gate_proj * sigmoid_gate
        hidden_low = (silu_gate * up_proj).astype(bf16)
        gate_grad = (
            hidden_grad * up_proj * sigmoid_gate * (1.0 + gate_proj * (1.0 - sigmoid_gate))
        ).astype(bf16)
        up_grad = (hidden_grad * silu_gate).astype(bf16)
        feed = nt(hidden_low, down_full)
        back = nt(gate_grad, gate_full) + nt(up_grad, up_full)
        return feed, back, hidden_low, gate_grad, up_grad

    far_pair = 2 * (1 - pair)
    grads = {
        "a": upstream_rows(mine, False),
        "b": upstream_rows(2 * pair + 1 - side, False),
        "c": upstream_rows(far_pair + side, True),
        "d": upstream_rows(far_pair + 1 - side, True),
    }
    normed = {"a": normed_a, "b": normed_b, "c": normed_c, "d": normed_d}
    done = {key: feed_forward(normed[key], grads[key]) for key in "abdc"}

    def gather_sum(which):
        part = {key: done[key][which] for key in "abcd"}
        low_d = part["d"].astype(bf16)
        from_side = side_swap(low_d[block_len:])
        from_pair = pair_swap(low_d[:block_len])
        send_b = jnp.concatenate(
            [part["b"][:block_len] + from_pair.astype(f32), part["b"][block_len:]], axis=0
        ).astype(bf16)
        send_c = jnp.concatenate(
            [part["c"][:block_len], part["c"][block_len:] + from_side.astype(f32)], axis=0
        ).astype(bf16)
        return part["a"] + side_swap(send_b).astype(f32) + pair_swap(send_c).astype(f32)

    back_two = gather_sum(1)
    normed_rows = jnp.concatenate([normed[key] for key in "abcd"], axis=0)
    grad_rows = jnp.concatenate([grads[key] for key in "abcd"], axis=0)
    hidden_rows = jnp.concatenate([done[key][2] for key in "abcd"], axis=0)
    gate_rows = jnp.concatenate([done[key][3] for key in "abcd"], axis=0)
    up_rows = jnp.concatenate([done[key][4] for key in "abcd"], axis=0)
    ffn_grad = jnp.concatenate(
        [tn(normed_rows, gate_rows), tn(normed_rows, up_rows), tn(grad_rows, hidden_rows)], axis=1
    ).reshape(shards, 2, half_shard, 3 * hidden)
    ffn_send = lax.dynamic_index_in_dim(ffn_grad, 1 - lane, 1, False).astype(bf16)
    ffn_keep = lax.dynamic_index_in_dim(ffn_grad, lane, 1, False)
    ffn_sum = (ffn_keep + lane_swap(ffn_send).astype(f32)).astype(bf16).reshape(shards * half_shard, 3 * hidden)
    ffn_piece = lax.psum_scatter(ffn_sum, "dp", scatter_dimension=0, tiled=True)
    ffn_pair = pair_swap(ffn_piece)
    both = jnp.concatenate([ffn_piece, ffn_pair], axis=1)
    both_far = lane_swap(both)
    low_rows, high_rows = pick(lane == 0, both, both_far), pick(lane == 0, both_far, both)
    rows_all = jnp.concatenate([low_rows, high_rows], axis=0).astype(f32)
    near_cols, far_cols = rows_all[:, : 3 * hidden], rows_all[:, 3 * hidden :]
    left, right = pick(pair == 0, near_cols, far_cols), pick(pair == 0, far_cols, near_cols)
    gate_shard, up_shard, down_turned = [
        jnp.concatenate(
            [left[:, i * hidden : (i + 1) * hidden], right[:, i * hidden : (i + 1) * hidden]], axis=1
        )
        for i in range(3)
    ]
    down_shard = down_turned.T

    feed_sum = gather_sum(0)
    out_half = (middle + feed_sum).astype(bf16)
    outputs = spread(out_half, lane, side, bf16)

    gain_ffn_grad = jnp.sum(back_two * normal_two, axis=0)
    middle_grad = grads["a"].astype(f32) + norm_back(back_two * gain_ffn, normal_two, scale_two)
    attn_low = middle_grad.astype(bf16)
    attn_grad = jnp.concatenate([attn_low, lane_swap(attn_low)], axis=0)
    weights = [(qkv_own, out_own), (qkv_far, out_far)]
    parts, back_one, gain_parts = [], None, 0.0
    for which in (1, 0):
        mixed_grad = nn(attn_grad, weights[which][1]).astype(bf16)
        qkv_grad, gain_part = attend_backward(
            table,
            qkv[which],
            cosine,
            sine,
            head_pair,
            q_rot[which],
            k_rot[which],
            mixed[which],
            inverse[which],
            mixed_grad,
        )
        parts.append(
            jnp.concatenate([tn(normed_one, qkv_grad), tn(attn_grad, mixed[which])], axis=1)
        )
        term = nt(qkv_grad, weights[which][0])
        back_one = term if back_one is None else back_one + term
        gain_parts = gain_parts + gain_part
    back_recv = lane_swap(back_one[half_len:].astype(bf16))
    back_half = back_one[:half_len] + back_recv.astype(f32)
    gain_attn_grad = jnp.sum(back_half * normal_one, axis=0)
    input_half = middle_grad + norm_back(back_half * gain_attn, normal_one, scale_one)
    input_grad = spread(input_half.astype(bf16), lane, side, f32)

    attn_sum = (parts[1] + side_swap(parts[0].astype(bf16)).astype(f32)).reshape(
        shards, 2, half_shard, qkv_cols + o_rows
    )
    attn_send = lax.dynamic_index_in_dim(attn_sum, 1 - pair, 1, False).astype(bf16)
    attn_keep = lax.dynamic_index_in_dim(attn_sum, pair, 1, False)
    attn_sum = (attn_keep + pair_swap(attn_send).astype(f32)).astype(bf16)
    attn_piece = lax.psum_scatter(
        attn_sum.reshape(shards * half_shard, qkv_cols + o_rows), "dp", scatter_dimension=0, tiled=True
    )
    attn_piece = cross_swap(attn_piece)
    piece_pair = pair_swap(attn_piece)
    columns = jnp.concatenate(
        [pick(pair == 0, attn_piece, piece_pair), pick(pair == 0, piece_pair, attn_piece)], axis=0
    )
    columns_far = lane_swap(columns)
    left = pick(lane == 0, columns, columns_far).astype(f32)
    right = pick(lane == 0, columns_far, columns).astype(f32)
    query_shard = jnp.concatenate([left[:, :q_cols], right[:, :q_cols]], axis=1)
    key_shard = jnp.concatenate(
        [left[:, q_cols : q_cols + kv_cols], right[:, q_cols : q_cols + kv_cols]], axis=1
    )
    value_shard = jnp.concatenate(
        [left[:, q_cols + kv_cols : qkv_cols], right[:, q_cols + kv_cols : qkv_cols]], axis=1
    )
    out_shard = jnp.concatenate([left[:, qkv_cols:].T, right[:, qkv_cols:].T], axis=0)

    head_grad = gain_parts[:2, :HD] + gain_parts[:2, HD:]
    gain_total = lax.psum(
        jnp.concatenate([jnp.stack([gain_attn_grad, gain_ffn_grad]), head_grad], axis=1),
        ("dp", "context", "tensor"),
    )
    gain_shard = cut(gain_total[:, :width], owner, shard, 1)
    head_shard = cut(gain_total[:, width:], owner, HD // shards, 1)
    return (
        outputs,
        input_grad,
        query_shard,
        key_shard,
        value_shard,
        out_shard,
        gate_shard,
        up_shard,
        down_shard,
        gain_shard,
        head_shard,
    )


def solution(mesh):
    in_specs = (
        P("dp", "context", None),
        P("dp"),
        P("dp", "tensor"),
        P("dp", "tensor"),
        P("dp", "tensor"),
        P("tensor", "dp"),
        P("dp", "tensor"),
        P("dp", "tensor"),
        P("tensor", "dp"),
        P(None, "dp"),
        P(None, "dp"),
        P("dp", "context", None),
    )
    out_specs = (
        P("dp", "context", None),
        P("dp", "context", None),
        P("dp", "tensor"),
        P("dp", "tensor"),
        P("dp", "tensor"),
        P("tensor", "dp"),
        P("dp", "tensor"),
        P("dp", "tensor"),
        P("tensor", "dp"),
        P(None, "dp"),
        P(None, "dp"),
    )
    return jax.shard_map(
        on_device, mesh=mesh, in_specs=in_specs, out_specs=out_specs, check_vma=False
    )
```

time: 1920 us -> 670 us (0.35)
  waiting for transfers between devices: 1490 us -> 175 us
  matrix products: 197 us -> 120 us
  starting transfers between devices: 2.39 us -> 64.7 us
  Pallas kernels: 0 us -> 43 us
  local copies, waits for them, and re-layouts: 82.1 us -> 107 us
    reduce_scatter x9 -> x0, waiting for transfers between devices: 714 us -> none  [the longest x1 165 us: on_device(): lax.psum_scatter(up_weight_grad, 'dp', scatter_dimension=0, tiled=True)]
    psum x5 -> x0, waiting for transfers between devices: 468 us -> none  [the longest x1 152 us: on_device(): lax.psum((query_shard, key_shard, value_shard, out_shard, gate_shard, up_...]
    all_gather x7 -> x2, waiting for transfers between devices: 267 us -> 15 us  [the longest x1 10.6 us: on_device(): attn_own = lax.all_gather(cross_swap(attn_shard), 'dp', axis=0, tiled=True)]
    ppermute x0 -> x38, waiting for transfers between devices: none -> 160 us  [the longest x9 76.2 us: pair_swap(): return lax.ppermute(value, 'context', PAIR_SWAP)]
    dot_general x49 -> x39, matrix products: 197 us -> 120 us  [the longest x16 48.8 us: nn(): return jnp.dot(left, right, preferred_element_type=f32)]
    ppermute x0 -> x38, starting transfers between devices: none -> 64.5 us  [the longest x1 17.3 us: on_device(): up_first = lax.ppermute(upstream_low, 'context', TURN)]
    psum x2 -> x1, blocking collectives: 11.1 us -> 55.9 us  [on_device(): lax.psum(jnp.concatenate([jnp.stack([gain_attn_grad, gain_ffn_grad]), hea...]
    all_gather x4 -> x1, blocking collectives: 55.2 us -> 12.2 us  [on_device(): lax.all_gather(jnp.concatenate([norm_gains, head_gains], axis=1), 'dp', a...]
  transfers between devices with their start and end apart: 23 -> 42, of which waited for: 20 -> 18; matrix products, arithmetic and copies ran while one was open for 9% -> 33% of each run, Pallas kernels for 0% -> 7%
where the time goes in v1:
time: 670 us; the launch traced here: 657 us
  waiting for transfers between devices  175 us (26%)
  matrix products  120 us (18%)
  local copies, waits for them, and re-layouts  107 us (16%)
  blocking collectives  68.1 us (10%)
  starting transfers between devices  64.7 us (10%)
  other arithmetic  64.1 us (10%)
  Pallas kernels  43 us (6%)
  between operations  15.5 us (2%)
    ppermute x9, waiting for transfers between devices, pair_swap(): return lax.ppermute(value, 'context', PAIR_SWAP)  76.2 us
    psum x1, blocking collectives, on_device(): lax.psum(jnp.concatenate([jnp.stack([gain_attn_grad, gain_ffn_grad]), hea...  55.9 us
    dot_general x16, matrix products, nn(): return jnp.dot(left, right, preferred_element_type=f32)  48.8 us
    unnamed x150, local copies, waits for them, and re-layouts  47.4 us
    ppermute x11, waiting for transfers between devices, side_swap(): return lax.ppermute(value, 'tensor', SIDE_SWAP)  45.1 us
    dot_general x7, matrix products, tn(): lax.dot_general(left, right, (((0,), (0,)), ((), ())), preferred_element_...  40.1 us
    dot_general x16, matrix products, nt(): lax.dot_general(left, right, (((1,), (1,)), ((), ())), preferred_element_...  31 us
    pallas_call x2, Pallas kernels, attend_backward(): pl.pallas_call(attend_backward_kernel, out_shape=(jax.ShapeDtypeStruct((f...  27.6 us
  transfers between devices with their start and end apart: 42, of which 18 were waited for; matrix products, arithmetic and copies ran while one was open for 33% of the time, Pallas kernels for 7%

profile of v1, /device:TPU:0, one launch (start us, length us, event | category | flops | bytes accessed | tf_op | source)
XLA Modules:
  0.0 656.6 jit_solution(9835354671492829262)
XLA Ops:
  23.9 12.2 %all-gather.1 = bf16[4,2,272]{2,1,0:T(2,128)(2,1)S(1)} all-gather(bf16[1,2,272]{2,1,0:T(2,128)(2,1)S(1)} %maximum_bitcast_fusion.1), channel_id=2, replica_groups=mesh['dp'=4,'context'=4,'tensor'=2] {'dp'}, dimensions={0}, use_global_device_ids=true | all-gather | bytes 5440 | tf_op jit(solution)/shard_map/all_gather | solution.py:346
  39.2 10.6 %collective-permute-start.2 = (bf16[512,1024]{1,0:T(8,128)(2,1)}, bf16[512,1024]{1,0:T(8,128)(2,1)}, u32[]{:S(2)}, u32[]{:S(2)}) collective-permute-start(bf16[512,1024]{1,0:T(8,128)(2,1)} %fusion.34), channel_id=1, source_target_pairs={{0,2},{2,0},{4,6},{6,4},{1,3},{3,1},{5,7},{7,5},{8,10},{10,8},{12,... | collective-permute-start | bytes 3145736 | tf_op jit(solution)/shard_map/ppermute | solution.py:29
  51.8 10.6 %all-gather.5.cloned.1.call-done = bf16[1024,768]{0,1:T(8,128)(2,1)} async-done(((bf16[256,768]{0,1:T(8,128)(2,1)}), bf16[1024,768]{0,1:T(8,128)(2,1)}) %all-gather.5.cloned.1.call-update) | async-done | bytes 1572880 | tf_op jit(solution)/shard_map/all_gather | solution.py:342
  74.4 7.5 %shard_map.203 = (bf16[1024,256]{1,0:T(8,128)(2,1)}, f32[1024,256]{1,0:T(8,128)}, bf16[1024,256]{1,0:T(8,128)(2,1)}, bf16[1024,128]{1,0:T(8,128)(2,1)}) custom-call(s32[5]{0:T(128)} %pad_add_fusion.table, f32[1024,512]{1,0:T(8,128)} %fusion.114.qkv_ref, f32[1024,128]{1,0:T(8,128)} %get-tuple-element.166.cos_ref, f32[1024,128]{1,0:T(8,128)} %get-tuple-element.167.sin_ref, ...), custom_call_target="tpu_custom_call" | custom-call | flops 6000000000 | bytes 5000000 | tf_op jit(solution)/shard_map/pallas_call | solution.py:250
  81.9 9.3 %collective-permute-done.4 = bf16[1024,512]{0,1:T(8,128)(2,1)} collective-permute-done((bf16[1024,512]{0,1:T(8,128)(2,1)}, bf16[1024,512]{0,1:T(8,128)(2,1)}, u32[]{:S(2)}, u32[]{:S(2)}) %collective-permute-start.4) | collective-permute-done | bytes 1048608 | tf_op jit(solution)/shard_map/ppermute | solution.py:37
  91.1 4.5 fusion.113.qkv_ref
  95.6 7.9 %shard_map.204 = (bf16[1024,256]{1,0:T(8,128)(2,1)}, f32[1024,256]{1,0:T(8,128)}, bf16[1024,256]{1,0:T(8,128)(2,1)}, bf16[1024,128]{1,0:T(8,128)(2,1)}) custom-call(s32[5]{0:T(128)} %pad_add_fusion.table, f32[1024,512]{1,0:T(8,128)} %fusion.113.qkv_ref, f32[1024,128]{1,0:T(8,128)} %get-tuple-element.166.cos_ref, f32[1024,128]{1,0:T(8,128)} %get-tuple-element.167.sin_ref, ...), custom_call_target="tpu_custom_call" | custom-call | flops 6000000000 | bytes 5000000 | tf_op jit(solution)/shard_map/pallas_call | solution.py:250
  110.9 17.3 %collective-permute-start.19 = (bf16[4,256,1024]{2,1,0:T(8,128)(2,1)}, bf16[4,256,1024]{2,1,0:T(8,128)(2,1)}, u32[]{:S(2)}, u32[]{:S(2)}) collective-permute-start(bf16[4,256,1024]{2,1,0:T(8,128)(2,1)} %broadcast_select_fusion.2), channel_id=1, source_target_pairs={{0,0},{2,4},{4,2},{6,6},{1,1},{3,5},{5,3},{7,7},{8,8},{10,12},{12,... | collective-permute-start | bytes 6291464 | tf_op jit(solution)/shard_map/ppermute | solution.py:385
  128.2 4.4 all-gather.7.cloned.1.call-done
  132.6 7.2 %reshape.116 = bf16[4,128,3456]{1,0,2:T(4,128)(2,1)} reshape(bf16[512,3456]{0,1:T(8,128)(2,1)} %all-gather.7.cloned.1.call-done) | data formatting | bytes 7077888 | tf_op jit(solution)/shard_map/reshape | solution.py:362
  147.9 23.5 %collective-permute-done.20 = bf16[4,256,1024]{2,1,0:T(8,128)(2,1)} collective-permute-done((bf16[4,256,1024]{2,1,0:T(8,128)(2,1)}, bf16[4,256,1024]{2,1,0:T(8,128)(2,1)}, u32[]{:S(2)}, u32[]{:S(2)}) %collective-permute-start.20) | collective-permute-done | bytes 2097184 | tf_op jit(solution)/shard_map/ppermute | solution.py:386
  177.3 5.4 collective-permute-done.9
  210.0 5.2 copy.92
  248.2 4.3 multiply_convert_fusion.4
  263.4 8.2 %fusion.1 = f32[1024,1152]{1,0:T(8,128)S(1)} fusion(bf16[2048,1024]{1,0:T(8,128)(2,1)S(1)} %copy-done.34, bf16[512,1152]{1,0:T(8,128)(2,1)} %copy-done.57, bf16[512,1152]{1,0:T(8,128)(2,1)} %copy-done.55, bf16[512,1152]{1,0:T(8,128)(2,1)} %copy-done.58, bf16[512,1152]{1,0:T(8,128)(2,1)} %copy-done.59), kind=kOutput, calls=%fused_computation.5 | convolution fusion | flops 4850712576 | bytes 13631488 | tf_op jit(solution)/shard_map/dot_general | solution.py:53
  277.6 9.2 %fusion.9 = f32[1024,1152]{1,0:T(8,128)S(1)} fusion(bf16[2048,1024]{1,0:T(8,128)(2,1)} %get-tuple-element.150, bf16[512,1152]{1,0:T(8,128)(2,1)} %copy-done.62, bf16[512,1152]{1,0:T(8,128)(2,1)} %get-tuple-element.118, bf16[512,1152]{1,0:T(8,128)(2,1)} %get-tuple-element.112, bf16[512,1152]{1,0:T(8,128)(2,1)S(1)} %get-tuple-element.109), kind=kOutput, calls=%fused_computation.13 | convolution fusion | flops 4850712576 | bytes 13631488 | tf_op jit(solution)/shard_map/dot_general | solution.py:53
  286.9 11.4 %fusion.17 = f32[1024,1152]{1,0:T(8,128)} fusion(bf16[2048,1024]{1,0:T(8,128)(2,1)} %copy-done.39, bf16[512,1152]{1,0:T(8,128)(2,1)} %copy-done.61, bf16[512,1152]{1,0:T(8,128)(2,1)} %get-tuple-element.120, bf16[512,1152]{1,0:T(8,128)(2,1)} %get-tuple-element.114, bf16[512,1152]{1,0:T(8,128)(2,1)S(1)} %copy-done.52), kind=kOutput, calls=%fused_computation.21 | convolution fusion | flops 4850712576 | bytes 13631488 | tf_op jit(solution)/shard_map/dot_general | solution.py:53
  305.6 9.3 %collective-permute-done.21 = bf16[256,1024]{1,0:T(8,128)(2,1)S(1)} collective-permute-done((bf16[256,1024]{1,0:T(8,128)(2,1)}, bf16[256,1024]{1,0:T(8,128)(2,1)S(1)}, u32[]{:S(2)}, u32[]{:S(2)}) %collective-permute-start.21) | collective-permute-done | bytes 524320 | tf_op jit(solution)/shard_map/ppermute | solution.py:33
  323.1 14.2 %collective-permute-done.24 = bf16[512,1024]{1,0:T(8,128)(2,1)S(1)} collective-permute-done((bf16[512,1024]{1,0:T(8,128)(2,1)S(1)}, bf16[512,1024]{1,0:T(8,128)(2,1)S(1)}, u32[]{:S(2)}, u32[]{:S(2)}) %collective-permute-start.24) | collective-permute-done | bytes 1048608 | tf_op jit(solution)/shard_map/ppermute | solution.py:33
  343.4 14.1 %collective-permute-done.15 = bf16[512,1024]{1,0:T(8,128)(2,1)S(1)} collective-permute-done((bf16[512,1024]{1,0:T(8,128)(2,1)S(1)}, bf16[512,1024]{1,0:T(8,128)(2,1)S(1)}, u32[]{:S(2)}, u32[]{:S(2)}) %collective-permute-start.15) | collective-permute-done | bytes 1048608 | tf_op jit(solution)/shard_map/ppermute | solution.py:33
  367.3 5.0 copy-done.2
  378.1 13.7 %shard_map.205 = (bf16[1024,512]{1,0:T(8,128)(2,1)}, f32[8,128]{1,0:T(8,128)}) custom-call(s32[5]{0:T(128)} %pad_add_fusion.table, f32[1024,512]{1,0:T(8,128)} %fusion.113.qkv_ref, f32[1024,128]{1,0:T(8,128)} %get-tuple-element.166.cos_ref, f32[1024,128]{1,0:T(8,128)} %get-tuple-element.167.sin_ref, f32[2,128]{1,0:T(2,128)} %maximum_convert_fusion.1.gain_ref, ...), custom_call_target="tpu_custom_call" | custom-call | flops 15000000512 | bytes 6000000 | tf_op jit(solution)/shard_map/pallas_call | solution.py:267
  404.6 13.9 %shard_map.206 = (bf16[1024,512]{1,0:T(8,128)(2,1)}, f32[8,128]{1,0:T(8,128)}) custom-call(s32[5]{0:T(128)} %pad_add_fusion.table, f32[1024,512]{1,0:T(8,128)} %fusion.114.qkv_ref, f32[1024,128]{1,0:T(8,128)} %get-tuple-element.166.cos_ref, f32[1024,128]{1,0:T(8,128)} %get-tuple-element.167.sin_ref, f32[2,128]{1,0:T(2,128)} %maximum_convert_fusion.1.gain_ref, ...), custom_call_target="tpu_custom_call" | custom-call | flops 15000000512 | bytes 6000000 | tf_op jit(solution)/shard_map/pallas_call | solution.py:267
  421.7 12.0 %collective-permute-done.30 = bf16[1024,768]{0,1:T(8,128)(2,1)} collective-permute-done((bf16[1024,768]{0,1:T(8,128)(2,1)S(1)}, bf16[1024,768]{0,1:T(8,128)(2,1)}, u32[]{:S(2)}, u32[]{:S(2)}) %collective-permute-start.30) | collective-permute-done | bytes 1572896 | tf_op jit(solution)/shard_map/ppermute | solution.py:37
  437.3 5.7 reshape.118
  448.0 4.4 constant_dynamic-slice_fusion.3
  455.9 10.5 %collective-permute-done.31 = bf16[4,128,768]{2,1,0:T(8,128)(2,1)} collective-permute-done((bf16[4,128,768]{2,1,0:T(8,128)(2,1)S(1)}, bf16[4,128,768]{2,1,0:T(8,128)(2,1)}, u32[]{:S(2)}, u32[]{:S(2)}) %collective-permute-start.31) | collective-permute-done | bytes 786464 | tf_op jit(solution)/shard_map/ppermute | solution.py:33
  468.7 6.7 %fusion = bf16[4,128,3456]{2,1,0:T(8,128)(2,1)} fusion(bf16[4,128,3456]{2,1,0:T(8,128)(2,1)} %collective-permute-done.35, f32[4,2,128,3456]{3,2,1,0:T(8,128)} %bitcast.122, s32[]{:T(128)S(6)} %select_n.208), kind=kLoop, calls=%fused_computation.3 | loop fusion | flops 5308416 | bytes 14155780 | tf_op jit(solution)/shard_map/convert_element_type | solution.py:466
  488.5 14.6 %collective-permute-done.17 = bf16[256,1024]{1,0:T(8,128)(2,1)S(1)} collective-permute-done((bf16[256,1024]{1,0:T(8,128)(2,1)}, bf16[256,1024]{1,0:T(8,128)(2,1)S(1)}, u32[]{:S(2)}, u32[]{:S(2)}) %collective-permute-start.17) | collective-permute-done | bytes 524320 | tf_op jit(solution)/shard_map/ppermute | solution.py:298
  514.6 12.4 %collective-permute-done.18 = bf16[2,256,1024]{2,1,0:T(8,128)(2,1)S(1)} collective-permute-done((bf16[2,256,1024]{2,1,0:T(8,128)(2,1)S(1)}, bf16[2,256,1024]{2,1,0:T(8,128)(2,1)S(1)}, u32[]{:S(2)}, u32[]{:S(2)}) %collective-permute-start.18) | collective-permute-done | bytes 1048608 | tf_op jit(solution)/shard_map/ppermute | solution.py:37
  531.1 55.9 %psum.7 = f32[2,1088]{1,0:T(2,128)S(1)} all-reduce(f32[2,1088]{1,0:T(2,128)S(1)} %pad_maximum_fusion.26), channel_id=1, replica_groups=mesh['dp'=4,'context'=4,'tensor'=2] {'dp','context','tensor'}, use_global_device_ids=true, to_apply=%region_8.9 | all-reduce | flops 2176 | bytes 17408 | tf_op jit(solution)/shard_map/psum | solution.py:546
  601.2 20.4 %collective-permute-done.33 = bf16[128,768]{0,1:T(8,128)(2,1)S(1)} collective-permute-done((bf16[128,768]{0,1:T(8,128)(2,1)S(1)}, bf16[128,768]{0,1:T(8,128)(2,1)S(1)}, u32[]{:S(2)}, u32[]{:S(2)}) %collective-permute-start.33) | collective-permute-done | bytes 196640 | tf_op jit(solution)/shard_map/ppermute | solution.py:33
  (363 shorter events, 269.6 us)
Async XLA Ops:
  7.2 55.2 %all-gather.5.cloned.1.call-start = ((), (), s32[]{:S(2)}) async-start(), calls=%async_computation.2 | async-start | bytes 1966080 | tf_op jit(solution)/shard_map/all_gather | solution.py:342
  14.0 118.6 %all-gather.7.cloned.1.call-start = ((), (), s32[]{:S(2)}) async-start(), calls=%async_computation.3 | async-start | bytes 4423680 | tf_op jit(solution)/shard_map/all_gather | solution.py:362
  15.1 22.3 %collective-permute-start.1 = (bf16[256,1024]{1,0:T(8,128)(2,1)}, bf16[256,1024]{1,0:T(8,128)(2,1)S(1)}, u32[]{:S(2)}, u32[]{:S(2)}) collective-permute-start(bf16[256,1024]{1,0:T(8,128)(2,1)} %get-tuple-element.131), channel_id=1, source_target_pairs={{0,4},{2,0},{4,6},{6,2},{1,5},{3,1},{5,7},{7,3},{8,12},{10,8},{12,... | collective-permute-start | bytes 1572872 | tf_op jit(solution)/shard_map/ppermute | solution.py:376
  18.1 19.3 %collective-permute-start = (bf16[256,1024]{1,0:T(8,128)(2,1)}, bf16[256,1024]{1,0:T(8,128)(2,1)S(1)}, u32[]{:S(2)}, u32[]{:S(2)}) collective-permute-start(bf16[256,1024]{1,0:T(8,128)(2,1)} %get-tuple-element.130), channel_id=1, source_target_pairs={{0,0},{2,4},{4,2},{6,6},{1,1},{3,5},{5,3},{7,7},{8,8},{10,12},{12,... | collective-permute-start | bytes 1572872 | tf_op jit(solution)/shard_map/ppermute | solution.py:373
  23.8 568.1 %reduce-scatter.7.cloned.1.call-start = ((), (), s32[]{:S(2)}) async-start(), calls=%async_computation.4 | async-start | bytes 983040
  39.2 30.9 %collective-permute-start.2 = (bf16[512,1024]{1,0:T(8,128)(2,1)}, bf16[512,1024]{1,0:T(8,128)(2,1)}, u32[]{:S(2)}, u32[]{:S(2)}) collective-permute-start(bf16[512,1024]{1,0:T(8,128)(2,1)} %fusion.34), channel_id=1, source_target_pairs={{0,2},{2,0},{4,6},{6,4},{1,3},{3,1},{5,7},{7,5},{8,10},{10,8},{12,... | collective-permute-start | bytes 3145736 | tf_op jit(solution)/shard_map/ppermute | solution.py:29
  64.8 26.3 %collective-permute-start.4 = (bf16[1024,512]{0,1:T(8,128)(2,1)}, bf16[1024,512]{0,1:T(8,128)(2,1)}, u32[]{:S(2)}, u32[]{:S(2)}) collective-permute-start(bf16[1024,512]{0,1:T(8,128)(2,1)} %slice.230), channel_id=1, source_target_pairs={{0,1},{1,0},{2,3},{3,2},{4,5},{5,4},{6,7},{7,6},{8,9},{9,8},{10,11... | collective-permute-start | bytes 3145736 | tf_op jit(solution)/shard_map/ppermute | solution.py:37
  69.5 34.0 %collective-permute-start.5 = (bf16[1024,256]{0,1:T(8,128)(2,1)S(1)}, bf16[1024,256]{0,1:T(8,128)(2,1)S(1)}, u32[]{:S(2)}, u32[]{:S(2)}) collective-permute-start(bf16[1024,256]{0,1:T(8,128)(2,1)S(1)} %slice.232), channel_id=1, source_target_pairs={{0,1},{1,0},{2,3},{3,2},{4,5},{5,4},{6,7},{7,6},{8,9},{9,8},{10,11... | collective-permute-start | bytes 1572872 | tf_op jit(solution)/shard_map/ppermute | solution.py:37
  106.4 33.4 %collective-permute-start.6 = (bf16[512,1024]{1,0:T(8,128)(2,1)S(1)}, bf16[512,1024]{1,0:T(8,128)(2,1)}, u32[]{:S(2)}, u32[]{:S(2)}) collective-permute-start(bf16[512,1024]{1,0:T(8,128)(2,1)S(1)} %slice.378), channel_id=1, source_target_pairs={{0,2},{2,0},{4,6},{6,4},{1,3},{3,1},{5,7},{7,5},{8,10},{10,8},{12,... | collective-permute-start | bytes 3145736 | tf_op jit(solution)/shard_map/ppermute | solution.py:29
  110.9 35.9 %collective-permute-start.19 = (bf16[4,256,1024]{2,1,0:T(8,128)(2,1)}, bf16[4,256,1024]{2,1,0:T(8,128)(2,1)}, u32[]{:S(2)}, u32[]{:S(2)}) collective-permute-start(bf16[4,256,1024]{2,1,0:T(8,128)(2,1)} %broadcast_select_fusion.2), channel_id=1, source_target_pairs={{0,0},{2,4},{4,2},{6,6},{1,1},{3,5},{5,3},{7,7},{8,8},{10,12},{12,... | collective-permute-start | bytes 6291464 | tf_op jit(solution)/shard_map/ppermute | solution.py:385
  128.2 43.2 %collective-permute-start.20 = (bf16[4,256,1024]{2,1,0:T(8,128)(2,1)}, bf16[4,256,1024]{2,1,0:T(8,128)(2,1)}, u32[]{:S(2)}, u32[]{:S(2)}) collective-permute-start(bf16[4,256,1024]{2,1,0:T(8,128)(2,1)} %broadcast_select_fusion.2), channel_id=1, source_target_pairs={{0,4},{2,0},{4,6},{6,2},{1,5},{3,1},{5,7},{7,3},{8,12},{10,8},{12,... | collective-permute-start | bytes 6291464 | tf_op jit(solution)/shard_map/ppermute | solution.py:386
  139.9 62.9 %collective-permute-start.7 = (bf16[4,128,3456]{1,0,2:T(4,128)(2,1)}, bf16[4,128,3456]{1,0,2:T(4,128)(2,1)}, u32[]{:S(2)}, u32[]{:S(2)}) collective-permute-start(bf16[4,128,3456]{1,0,2:T(4,128)(2,1)} %reshape.116), channel_id=1, source_target_pairs={{0,2},{2,0},{4,6},{6,4},{1,3},{3,1},{5,7},{7,5},{8,10},{10,8},{12,... | collective-permute-start | bytes 10616840 | tf_op jit(solution)/shard_map/ppermute | solution.py:29
  143.9 38.8 %collective-permute-start.9 = (bf16[512,1024]{1,0:T(8,128)(2,1)}, bf16[512,1024]{1,0:T(8,128)(2,1)}, u32[]{:S(2)}, u32[]{:S(2)}) collective-permute-start(bf16[512,1024]{1,0:T(8,128)(2,1)} %get-tuple-element.84), channel_id=1, source_target_pairs={{0,4},{4,0},{2,6},{6,2},{1,5},{5,1},{3,7},{7,3},{8,12},{12,8},{10,... | collective-permute-start | bytes 3145736 | tf_op jit(solution)/shard_map/ppermute | solution.py:33
  145.4 41.9 %collective-permute-start.8 = (bf16[512,1024]{1,0:T(8,128)(2,1)}, bf16[512,1024]{1,0:T(8,128)(2,1)S(1)}, u32[]{:S(2)}, u32[]{:S(2)}) collective-permute-start(bf16[512,1024]{1,0:T(8,128)(2,1)} %get-tuple-element.84), channel_id=1, source_target_pairs={{0,1},{1,0},{2,3},{3,2},{4,5},{5,4},{6,7},{7,6},{8,9},{9,8},{10,11... | collective-permute-start | bytes 3145736 | tf_op jit(solution)/shard_map/ppermute | solution.py:37
  244.5 60.5 %collective-permute-start.23 = (bf16[256,1024]{1,0:T(8,128)(2,1)S(1)}, bf16[256,1024]{1,0:T(8,128)(2,1)S(1)}, u32[]{:S(2)}, u32[]{:S(2)}) collective-permute-start(bf16[256,1024]{1,0:T(8,128)(2,1)S(1)} %get-tuple-element.135), channel_id=1, source_target_pairs={{0,1},{1,0},{2,3},{3,2},{4,5},{5,4},{6,7},{7,6},{8,9},{9,8},{10,11... | collective-permute-start | bytes 1572872 | tf_op jit(solution)/shard_map/ppermute | solution.py:37
  263.1 55.6 %collective-permute-start.12 = (bf16[256,1024]{1,0:T(8,128)(2,1)}, bf16[256,1024]{1,0:T(8,128)(2,1)}, u32[]{:S(2)}, u32[]{:S(2)}) collective-permute-start(bf16[256,1024]{1,0:T(8,128)(2,1)} %get-tuple-element.138), channel_id=1, source_target_pairs={{0,4},{4,0},{2,6},{6,2},{1,5},{5,1},{3,7},{7,3},{8,12},{12,8},{10,... | collective-permute-start | bytes 1572872 | tf_op jit(solution)/shard_map/ppermute | solution.py:33
  305.2 32.1 %collective-permute-start.24 = (bf16[512,1024]{1,0:T(8,128)(2,1)S(1)}, bf16[512,1024]{1,0:T(8,128)(2,1)S(1)}, u32[]{:S(2)}, u32[]{:S(2)}) collective-permute-start(bf16[512,1024]{1,0:T(8,128)(2,1)S(1)} %pad_maximum_fusion.14), channel_id=1, source_target_pairs={{0,4},{4,0},{2,6},{6,2},{1,5},{5,1},{3,7},{7,3},{8,12},{12,8},{10,... | collective-permute-start | bytes 3145736 | tf_op jit(solution)/shard_map/ppermute | solution.py:33
  315.1 26.1 %collective-permute-start.22 = (bf16[512,1024]{1,0:T(8,128)(2,1)S(1)}, bf16[512,1024]{1,0:T(8,128)(2,1)S(1)}, u32[]{:S(2)}, u32[]{:S(2)}) collective-permute-start(bf16[512,1024]{1,0:T(8,128)(2,1)S(1)} %pad_maximum_fusion.13), channel_id=1, source_target_pairs={{0,1},{1,0},{2,3},{3,2},{4,5},{5,4},{6,7},{7,6},{8,9},{9,8},{10,11... | collective-permute-start | bytes 3145736 | tf_op jit(solution)/shard_map/ppermute | solution.py:37
  318.6 38.9 %collective-permute-start.15 = (bf16[512,1024]{1,0:T(8,128)(2,1)S(1)}, bf16[512,1024]{1,0:T(8,128)(2,1)S(1)}, u32[]{:S(2)}, u32[]{:S(2)}) collective-permute-start(bf16[512,1024]{1,0:T(8,128)(2,1)S(1)} %pad_maximum_fusion.10), channel_id=1, source_target_pairs={{0,4},{4,0},{2,6},{6,2},{1,5},{5,1},{3,7},{7,3},{8,12},{12,8},{10,... | collective-permute-start | bytes 3145736 | tf_op jit(solution)/shard_map/ppermute | solution.py:33
  320.1 40.7 %collective-permute-start.13 = (bf16[512,1024]{1,0:T(8,128)(2,1)S(1)}, bf16[512,1024]{1,0:T(8,128)(2,1)S(1)}, u32[]{:S(2)}, u32[]{:S(2)}) collective-permute-start(bf16[512,1024]{1,0:T(8,128)(2,1)S(1)} %pad_maximum_fusion.9), channel_id=1, source_target_pairs={{0,1},{1,0},{2,3},{3,2},{4,5},{5,4},{6,7},{7,6},{8,9},{9,8},{10,11... | collective-permute-start | bytes 3145736 | tf_op jit(solution)/shard_map/ppermute | solution.py:37
  374.5 94.2 %collective-permute-start.35 = (bf16[4,128,3456]{2,1,0:T(8,128)(2,1)}, bf16[4,128,3456]{2,1,0:T(8,128)(2,1)}, u32[]{:S(2)}, u32[]{:S(2)}) collective-permute-start(bf16[4,128,3456]{2,1,0:T(8,128)(2,1)} %fusion.25), channel_id=1, source_target_pairs={{0,2},{2,0},{4,6},{6,4},{1,3},{3,1},{5,7},{7,5},{8,10},{10,8},{12,... | collective-permute-start | bytes 10616840 | tf_op jit(solution)/shard_map/ppermute | solution.py:29
  397.2 36.5 %collective-permute-start.30 = (bf16[1024,768]{0,1:T(8,128)(2,1)S(1)}, bf16[1024,768]{0,1:T(8,128)(2,1)}, u32[]{:S(2)}, u32[]{:S(2)}) collective-permute-start(bf16[1024,768]{0,1:T(8,128)(2,1)S(1)} %pad_maximum_fusion.7), channel_id=1, source_target_pairs={{0,1},{1,0},{2,3},{3,2},{4,5},{5,4},{6,7},{7,6},{8,9},{9,8},{10,11... | collective-permute-start | bytes 4718600 | tf_op jit(solution)/shard_map/ppermute | solution.py:37
  447.6 18.8 %collective-permute-start.31 = (bf16[4,128,768]{2,1,0:T(8,128)(2,1)S(1)}, bf16[4,128,768]{2,1,0:T(8,128)(2,1)}, u32[]{:S(2)}, u32[]{:S(2)}) collective-permute-start(bf16[4,128,768]{2,1,0:T(8,128)(2,1)S(1)} %bitcast.157), channel_id=1, source_target_pairs={{0,4},{4,0},{2,6},{6,2},{1,5},{5,1},{3,7},{7,3},{8,12},{12,8},{10,... | collective-permute-start | bytes 2359304 | tf_op jit(solution)/shard_map/ppermute | solution.py:33
  468.6 125.1 %reduce-scatter.9.cloned.1.call-start = ((), (), s32[]{:S(2)}) async-start(), calls=%async_computation.5 | async-start | bytes 4423680
  485.0 24.3 %collective-permute-start.26 = (bf16[512,1024]{1,0:T(8,128)(2,1)}, bf16[512,1024]{1,0:T(8,128)(2,1)S(1)}, u32[]{:S(2)}, u32[]{:S(2)}) collective-permute-start(bf16[512,1024]{1,0:T(8,128)(2,1)} %slice.377), channel_id=1, source_target_pairs={{0,2},{2,0},{4,6},{6,4},{1,3},{3,1},{5,7},{7,5},{8,10},{10,8},{12,... | collective-permute-start | bytes 3145736 | tf_op jit(solution)/shard_map/ppermute | solution.py:29
  487.8 15.3 %collective-permute-start.17 = (bf16[256,1024]{1,0:T(8,128)(2,1)}, bf16[256,1024]{1,0:T(8,128)(2,1)S(1)}, u32[]{:S(2)}, u32[]{:S(2)}) collective-permute-start(bf16[256,1024]{1,0:T(8,128)(2,1)} %get-tuple-element.136), channel_id=1, source_target_pairs={{4,0},{0,2},{6,4},{2,6},{5,1},{1,3},{7,5},{3,7},{12,8},{8,10},{14,... | collective-permute-start | bytes 1572872 | tf_op jit(solution)/shard_map/ppermute | solution.py:298
  504.4 22.6 %collective-permute-start.18 = (bf16[2,256,1024]{2,1,0:T(8,128)(2,1)S(1)}, bf16[2,256,1024]{2,1,0:T(8,128)(2,1)S(1)}, u32[]{:S(2)}, u32[]{:S(2)}) collective-permute-start(bf16[2,256,1024]{2,1,0:T(8,128)(2,1)S(1)} %pad_maximum_fusion.11), channel_id=1, source_target_pairs={{0,1},{1,0},{2,3},{3,2},{4,5},{5,4},{6,7},{7,6},{8,9},{9,8},{10,11... | collective-permute-start | bytes 3145736 | tf_op jit(solution)/shard_map/ppermute | solution.py:37
  511.8 16.1 %collective-permute-start.27 = (bf16[256,1024]{1,0:T(8,128)(2,1)S(1)}, bf16[256,1024]{1,0:T(8,128)(2,1)S(1)}, u32[]{:S(2)}, u32[]{:S(2)}) collective-permute-start(bf16[256,1024]{1,0:T(8,128)(2,1)S(1)} %get-tuple-element.133), channel_id=1, source_target_pairs={{0,0},{2,4},{4,2},{6,6},{1,1},{3,5},{5,3},{7,7},{8,8},{10,12},{12,... | collective-permute-start | bytes 1572872 | tf_op jit(solution)/shard_map/ppermute | solution.py:297
  512.7 15.1 %collective-permute-start.28 = (bf16[256,1024]{1,0:T(8,128)(2,1)S(1)}, bf16[256,1024]{1,0:T(8,128)(2,1)S(1)}, u32[]{:S(2)}, u32[]{:S(2)}) collective-permute-start(bf16[256,1024]{1,0:T(8,128)(2,1)S(1)} %get-tuple-element.132), channel_id=1, source_target_pairs={{4,0},{0,2},{6,4},{2,6},{5,1},{1,3},{7,5},{3,7},{12,8},{8,10},{14,... | collective-permute-start | bytes 1572872 | tf_op jit(solution)/shard_map/ppermute | solution.py:298
  528.9 70.2 %collective-permute-start.29 = (bf16[2,256,1024]{2,1,0:T(8,128)(2,1)}, bf16[2,256,1024]{2,1,0:T(8,128)(2,1)}, u32[]{:S(2)}, u32[]{:S(2)}) collective-permute-start(bf16[2,256,1024]{2,1,0:T(8,128)(2,1)} %pad_maximum_fusion.15), channel_id=1, source_target_pairs={{0,1},{1,0},{2,3},{3,2},{4,5},{5,4},{6,7},{7,6},{8,9},{9,8},{10,11... | collective-permute-start | bytes 3145736 | tf_op jit(solution)/shard_map/ppermute | solution.py:37
  595.6 27.1 %collective-permute-start.36 = (bf16[128,3456]{0,1:T(8,128)(2,1)S(1)}, bf16[128,3456]{0,1:T(8,128)(2,1)S(1)}, u32[]{:S(2)}, u32[]{:S(2)}) collective-permute-start(bf16[128,3456]{0,1:T(8,128)(2,1)S(1)} %copy.85), channel_id=1, source_target_pairs={{0,4},{4,0},{2,6},{6,2},{1,5},{5,1},{3,7},{7,3},{8,12},{12,8},{10,... | collective-permute-start | bytes 2654216 | tf_op jit(solution)/shard_map/ppermute | solution.py:33
  599.1 22.5 %collective-permute-start.33 = (bf16[128,768]{0,1:T(8,128)(2,1)S(1)}, bf16[128,768]{0,1:T(8,128)(2,1)S(1)}, u32[]{:S(2)}, u32[]{:S(2)}) collective-permute-start(bf16[128,768]{0,1:T(8,128)(2,1)S(1)} %collective-permute-done.32), channel_id=1, source_target_pairs={{0,4},{4,0},{2,6},{6,2},{1,5},{5,1},{3,7},{7,3},{8,12},{12,8},{10,... | collective-permute-start | bytes 589832 | tf_op jit(solution)/shard_map/ppermute | solution.py:33
  (73 other events, 601.4 us)
Sparse Core Ops, SparseCore 0:
  14.1 48.2 all-gather.4
  64.5 68.0 all-gather.6
  468.8 20.3 reduce-scatter.6
  491.4 66.0 reduce-scatter.8

commit v2 on v1

--- a/solution.py
+++ b/solution.py
@@ -4,6 +4,7 @@
 import jax.numpy as jnp
 from jax import lax
 from jax.experimental import pallas as pl
+from jax.experimental.layout import Layout, with_layout_constraint
 from jax.experimental.pallas import tpu as pltpu
 from jax.sharding import PartitionSpec as P
 
@@ -19,10 +20,10 @@
 LANE_SWAP = [(0, 1), (1, 0), (2, 3), (3, 2)]
 PAIR_SWAP = [(0, 2), (2, 0), (1, 3), (3, 1)]
 SIDE_SWAP = [(0, 1), (1, 0)]
-TURN = [(0, 0), (1, 2), (2, 1), (3, 3)]
+TURN = [(1, 2), (2, 1)]
 TWIST_IN = [(0, 2), (1, 0), (2, 3), (3, 1)]
 TWIST_OUT = [(b, a) for a, b in TWIST_IN]
-CROSS = [(0, 0), (1, 2), (2, 1), (3, 3), (4, 4), (5, 6), (6, 5), (7, 7)]
+CROSS = [(1, 2), (2, 1), (5, 6), (6, 5)]
 
 
 def lane_swap(value):
@@ -37,8 +38,22 @@
     return lax.ppermute(value, "tensor", SIDE_SWAP)
 
 
-def cross_swap(value):
-    return lax.ppermute(value, ("context", "tensor"), CROSS)
+def cross_swap(value, lane, side):
+    moved = lax.ppermute(value, ("context", "tensor"), CROSS)
+    return jnp.where(lane == side, value, moved)
+
+
+def turn(value, pair, lane):
+    moved = lax.ppermute(value, "context", TURN)
+    return jnp.where(pair == lane, value, moved)
+
+
+def after(value, *others):
+    return lax.optimization_barrier((value,) + others)[0]
+
+
+def row_major(value):
+    return with_layout_constraint(value, Layout(tuple(range(value.ndim))))
 
 
 def nn(left, right):
@@ -258,7 +273,7 @@
         in_specs=[pl.BlockSpec(memory_space=pltpu.SMEM)] + [whole_spec()] * 4,
         out_specs=(whole_spec(),) * 4,
         scratch_shapes=[pltpu.VMEM((2, full_len, 128), bf16)],
-        cost_estimate=pl.CostEstimate(flops=6 * 10**9, bytes_accessed=5 * 10**6, transcendentals=3 * 10**6),
+        cost_estimate=pl.CostEstimate(flops=10**9, bytes_accessed=10**6, transcendentals=0),
     )(table, qkv, cosine, sine, gains)
 
 
@@ -280,29 +295,344 @@
             pltpu.VMEM((2, full_len, HD), f32),
             pltpu.VMEM((2, full_len, HD), f32),
         ],
-        cost_estimate=pl.CostEstimate(flops=15 * 10**9, bytes_accessed=6 * 10**6, transcendentals=3 * 10**6),
+        cost_estimate=pl.CostEstimate(flops=2 * 10**9, bytes_accessed=10**6, transcendentals=0),
     )(table, qkv, cosine, sine, gains, qr, kr, out, inverse, grad)
+
+
+def feed_forward_kernel(
+    shards,
+    turned,
+    table,
+    normed_ref,
+    first_ref,
+    second_ref,
+    own_ref,
+    far_ref,
+    feed_ref,
+    back_ref,
+    hidden_ref,
+    gate_grad_ref,
+    up_grad_ref,
+    weight_ref,
+    sems,
+):
+    step = pl.program_id(0)
+    lane = lax.rem(lax.axis_index("context"), 2)
+    width, columns = weight_ref.shape
+    hidden = columns // 3
+    half_shard = width // shards // 2
+    parts = [slice(0, hidden), slice(hidden, 2 * hidden), slice(2 * hidden, 3 * hidden)]
+
+    def copies(part):
+        found = []
+        for owner in range(shards):
+            source = pl.ds(owner * half_shard, half_shard)
+            for far, ref in ((0, own_ref), (1, far_ref)):
+                place = (2 * owner + (1 - lane if far else lane)) * half_shard
+                found.append(
+                    pltpu.make_async_copy(
+                        ref.at[source, parts[part]],
+                        weight_ref.at[pl.ds(pl.multiple_of(place, half_shard), half_shard), parts[part]],
+                        sems.at[part, 2 * owner + far],
+                    )
+                )
+        return found
+
+    @pl.when(step == 0)
+    def _():
+        for part in range(3):
+            for copy in copies(part):
+                copy.start()
+
+    def ready(part):
+        @pl.when(step == 0)
+        def _():
+            for copy in copies(part):
+                copy.wait()
+
+    normed = normed_ref[...]
+    use_first = (step == 0) != turned
+    grad = jnp.where(use_first, first_ref[0], second_ref[0])
+    ready(0)
+    gate_proj = nn(normed, weight_ref[:, parts[0]])
+    ready(1)
+    up_proj = nn(normed, weight_ref[:, parts[1]])
+    ready(2)
+    hidden_grad = nn(grad, weight_ref[:, parts[2]])
+    sigmoid_gate = 1.0 / (1.0 + jnp.exp(-gate_proj))
+    silu_gate = gate_proj * sigmoid_gate
+    hidden_low = (silu_gate * up_proj).astype(bf16)
+    gate_grad = (
+        hidden_grad * up_proj * (sigmoid_gate + silu_gate * (1.0 - sigmoid_gate))
+    ).astype(bf16)
+    up_grad = (hidden_grad * silu_gate).astype(bf16)
+    hidden_ref[...] = hidden_low
+    gate_grad_ref[...] = gate_grad
+    up_grad_ref[...] = up_grad
+    back = nt(gate_grad, weight_ref[:, parts[0]]) + nt(up_grad, weight_ref[:, parts[1]])
+    back_ref[...] = back.astype(back_ref.dtype)
+    feed_ref[...] = nt(hidden_low, weight_ref[:, parts[2]]).astype(feed_ref.dtype)
+
+
+def feed_forward(sequence, turned, out_dtype, shards, normed, up_first, up_second, own, far):
+    rows, width = normed.shape
+    tile = rows // 2
+    columns = own.shape[1]
+    hidden = columns // 3
+    grad_spec = pl.BlockSpec((1, tile, width), lambda i, t: (t[0], 0, 0))
+    return pl.pallas_call(
+        functools.partial(feed_forward_kernel, shards, turned),
+        grid_spec=pltpu.PrefetchScalarGridSpec(
+            num_scalar_prefetch=1,
+            grid=(2,),
+            in_specs=[
+                pl.BlockSpec((tile, width), lambda i, t: (i, 0)),
+                grad_spec,
+                grad_spec,
+                pl.BlockSpec(memory_space=pl.ANY),
+                pl.BlockSpec(memory_space=pl.ANY),
+            ],
+            out_specs=[
+                pl.BlockSpec((tile, width), lambda i, t: (i, 0)),
+                pl.BlockSpec((tile, width), lambda i, t: (i, 0)),
+                pl.BlockSpec((tile, hidden), lambda i, t: (i, 0)),
+                pl.BlockSpec((tile, hidden), lambda i, t: (i, 0)),
+                pl.BlockSpec((tile, hidden), lambda i, t: (i, 0)),
+            ],
+            scratch_shapes=[
+                pltpu.VMEM((width, columns), bf16),
+                pltpu.SemaphoreType.DMA((3, 2 * shards)),
+            ],
+        ),
+        out_shape=[
+            jax.ShapeDtypeStruct((rows, width), out_dtype),
+            jax.ShapeDtypeStruct((rows, width), out_dtype),
+            jax.ShapeDtypeStruct((rows, hidden), bf16),
+            jax.ShapeDtypeStruct((rows, hidden), bf16),
+            jax.ShapeDtypeStruct((rows, hidden), bf16),
+        ],
+        cost_estimate=pl.CostEstimate(
+            flops=rows * width * hidden, bytes_accessed=10**6, transcendentals=0
+        ),
+    )(sequence[None], normed, up_first, up_second, own, far)
+
+
+def store_halves(which, shards, total_ref, near_ref, far_ref):
+    half = total_ref.shape[0] // shards // 2
+    for owner in range(shards):
+        rows = slice(owner * half, (owner + 1) * half)
+        near = pl.ds(pl.multiple_of((2 * owner + which) * half, half), half)
+        far = pl.ds(pl.multiple_of((2 * owner + 1 - which) * half, half), half)
+        near_ref[rows, :] = total_ref[near, :].astype(bf16)
+        far_ref[rows, :] = total_ref[far, :].astype(bf16)
+
+
+def left_grad_kernel(shards, *refs):
+    lefts, rights = refs[:4], refs[4:8]
+    near_ref, far_ref, total_ref = refs[8:]
+    lane = lax.rem(lax.axis_index("context"), 2)
+    total_ref[...] = sum(tn(left[...], right[...]) for left, right in zip(lefts, rights))
+    store_halves(lane, shards, total_ref, near_ref, far_ref)
+
+
+def left_grad(shards, lefts, rights):
+    rows, width = lefts[0].shape
+    hidden = rights[0].shape[1]
+    tile = hidden // 3
+    half = width // 2
+    return pl.pallas_call(
+        functools.partial(left_grad_kernel, shards),
+        grid=(3,),
+        in_specs=[pl.BlockSpec((rows, width), lambda j: (0, 0))] * 4
+        + [pl.BlockSpec((rows, tile), lambda j: (0, j))] * 4,
+        out_specs=[pl.BlockSpec((half, tile), lambda j: (0, j))] * 2,
+        out_shape=[jax.ShapeDtypeStruct((half, hidden), bf16)] * 2,
+        scratch_shapes=[pltpu.VMEM((width, tile), f32)],
+        cost_estimate=pl.CostEstimate(
+            flops=rows * width * hidden, bytes_accessed=10**6, transcendentals=0
+        ),
+    )(*lefts, *rights)
+
+
+def down_grad_kernel(shards, table, first_ref, second_ref, *refs):
+    rights = refs[:4]
+    near_ref, far_ref, total_ref = refs[4:]
+    lane = lax.rem(lax.axis_index("context"), 2)
+    tile = first_ref.shape[1]
+    total = None
+    for index, right in enumerate(rights):
+        order = (first_ref, second_ref) if index < 2 else (second_ref, first_ref)
+        for part, left in enumerate(order):
+            term = tn(left[table[index]], right[part * tile : (part + 1) * tile, :])
+            total = term if total is None else total + term
+    total_ref[...] = total
+    store_halves(lane, shards, total_ref, near_ref, far_ref)
+
+
+def down_grad(shards, sequences, up_first, up_second, rights):
+    rows, hidden = rights[0].shape
+    width = up_first.shape[2]
+    tile = hidden // 3
+    half = width // 2
+    whole = pl.BlockSpec(up_first.shape, lambda j, t: (0, 0, 0))
+    return pl.pallas_call(
+        functools.partial(down_grad_kernel, shards),
+        grid_spec=pltpu.PrefetchScalarGridSpec(
+            num_scalar_prefetch=1,
+            grid=(3,),
+            in_specs=[whole, whole] + [pl.BlockSpec((rows, tile), lambda j, t: (0, j))] * 4,
+            out_specs=[pl.BlockSpec((half, tile), lambda j, t: (0, j))] * 2,
+            scratch_shapes=[pltpu.VMEM((width, tile), f32)],
+        ),
+        out_shape=[jax.ShapeDtypeStruct((half, hidden), bf16)] * 2,
+        cost_estimate=pl.CostEstimate(
+            flops=rows * width * hidden, bytes_accessed=10**6, transcendentals=0
+        ),
+    )(sequences, up_first, up_second, *rights)
+
+
+def attn_grad_kernel(shards, normed_ref, grad_ref, upstream_ref, mixed_ref, near_ref, far_ref, total_ref):
+    pair = lax.axis_index("context") // 2
+    columns = grad_ref.shape[1]
+    total_ref[:, :columns] = tn(normed_ref[...], grad_ref[...])
+    total_ref[:, columns:] = tn(upstream_ref[...], mixed_ref[...])
+    store_halves(pair, shards, total_ref, near_ref, far_ref)
+
+
+def attn_weight_grad(shards, normed, grad, upstream, mixed):
+    width = normed.shape[1]
+    columns = grad.shape[1] + mixed.shape[1]
+    return pl.pallas_call(
+        functools.partial(attn_grad_kernel, shards),
+        in_specs=[whole_spec()] * 4,
+        out_specs=[whole_spec()] * 2,
+        out_shape=[jax.ShapeDtypeStruct((width // 2, columns), bf16)] * 2,
+        scratch_shapes=[pltpu.VMEM((width, columns), f32)],
+        cost_estimate=pl.CostEstimate(
+            flops=10**8, bytes_accessed=10**6, transcendentals=0
+        ),
+    )(normed, grad, upstream, mixed)
+
+
+def join_ffn_kernel(pieces, outs):
+    context = lax.axis_index("context")
+    pair, lane = context // 2, lax.rem(context, 2)
+    gate_ref, up_ref, down_ref = outs
+    half, columns = pieces[0][0].shape
+    hidden = columns // 3
+    for row in range(2):
+        for column in range(2):
+            for part in range(3):
+                cols = slice(part * hidden, (part + 1) * hidden)
+                values = [
+                    jnp.where(pair == column, pieces[a][0][:, cols], pieces[a][1][:, cols])
+                    for a in range(2)
+                ]
+                value = jnp.where(lane == row, values[0], values[1]).astype(f32)
+                rows = slice(row * half, (row + 1) * half)
+                into = slice(column * hidden, (column + 1) * hidden)
+                if part == 2:
+                    down_ref[into, rows] = value.T
+                else:
+                    (gate_ref, up_ref)[part][rows, into] = value
+
+
+def join_ffn(near, near_pair, far, far_pair):
+    half, columns = near.shape
+    hidden = columns // 3
+
+    def kernel(a, b, c, d, *outs):
+        join_ffn_kernel([[a, b], [c, d]], outs)
+
+    return pl.pallas_call(
+        kernel,
+        in_specs=[whole_spec()] * 4,
+        out_specs=[whole_spec()] * 3,
+        out_shape=[
+            jax.ShapeDtypeStruct((2 * half, 2 * hidden), f32),
+            jax.ShapeDtypeStruct((2 * half, 2 * hidden), f32),
+            jax.ShapeDtypeStruct((2 * hidden, 2 * half), f32),
+        ],
+        cost_estimate=pl.CostEstimate(flops=10**6, bytes_accessed=10**6, transcendentals=0),
+    )(near, near_pair, far, far_pair)
+
+
+def join_attn(q_cols, kv_cols, near, near_pair, far, far_pair):
+    half, columns = near.shape
+    o_rows = columns - q_cols - 2 * kv_cols
+    cuts = [
+        slice(0, q_cols),
+        slice(q_cols, q_cols + kv_cols),
+        slice(q_cols + kv_cols, q_cols + 2 * kv_cols),
+        slice(q_cols + 2 * kv_cols, columns),
+    ]
+
+    def kernel(a, b, c, d, q_ref, k_ref, v_ref, o_ref):
+        context = lax.axis_index("context")
+        pair, lane = context // 2, lax.rem(context, 2)
+        for column in range(2):
+            for row in range(2):
+                rows = slice(row * half, (row + 1) * half)
+                for part, cols in enumerate(cuts):
+                    one = jnp.where(pair == row, a[:, cols], b[:, cols])
+                    two = jnp.where(pair == row, c[:, cols], d[:, cols])
+                    value = jnp.where(lane == column, one, two).astype(f32)
+                    wide = cols.stop - cols.start
+                    into = slice(column * wide, (column + 1) * wide)
+                    if part == 3:
+                        o_ref[into, rows] = value.T
+                    else:
+                        (q_ref, k_ref, v_ref)[part][rows, into] = value
+
+    return pl.pallas_call(
+        kernel,
+        in_specs=[whole_spec()] * 4,
+        out_specs=[whole_spec()] * 4,
+        out_shape=[
+            jax.ShapeDtypeStruct((2 * half, 2 * q_cols), f32),
+            jax.ShapeDtypeStruct((2 * half, 2 * kv_cols), f32),
+            jax.ShapeDtypeStruct((2 * half, 2 * kv_cols), f32),
+            jax.ShapeDtypeStruct((2 * o_rows, 2 * half), f32),
+        ],
+        cost_estimate=pl.CostEstimate(flops=10**6, bytes_accessed=2 * 10**6, transcendentals=0),
+    )(near, near_pair, far, far_pair)
+
+
+def join_rows(places, values, out_dtype):
+    block, width = values[0].shape
+
+    def kernel(table, a, b, c, d, out_ref):
+        for index, ref in enumerate((a, b, c, d)):
+
+            @pl.when(table[index] == pl.program_id(0))
+            def _():
+                out_ref[0] = ref[...].astype(out_dtype)
+
+    return pl.pallas_call(
+        kernel,
+        grid_spec=pltpu.PrefetchScalarGridSpec(
+            num_scalar_prefetch=1,
+            grid=(4,),
+            in_specs=[pl.BlockSpec((block, width), lambda i, t: (0, 0))] * 4,
+            out_specs=pl.BlockSpec((1, block, width), lambda i, t: (i, 0, 0)),
+        ),
+        out_shape=jax.ShapeDtypeStruct((4, block, width), out_dtype),
+        cost_estimate=pl.CostEstimate(flops=10**6, bytes_accessed=10**6, transcendentals=0),
+    )(places, *values)
 
 
 def cut(value, index, size, axis):
     return lax.dynamic_slice_in_dim(value, index * size, size, axis)
 
 
-def pick(flag, first, second):
-    return jnp.where(flag, first, second)
-
-
-def spread(half, lane, side, out_dtype):
-    block = half.shape[0] // 2
-    first = lax.ppermute(half[:block], "context", TURN)
-    second = lax.ppermute(half[block:], "context", TWIST_OUT)
-    near = jnp.stack([first, second])
-    far = side_swap(near)
-    result = jnp.zeros((4,) + first.shape, out_dtype)
-    for value, pair, other in ((near[0], 0, 0), (near[1], 1, 0), (far[0], 0, 1), (far[1], 1, 1)):
-        place = 2 * lax.rem(lane + pair, 2) + lax.rem(side + other, 2)
-        result = lax.dynamic_update_slice(result, value.astype(out_dtype)[None], (place, 0, 0))
-    return result
+def spread(first_rows, second_rows, pair, lane, side, out_dtype):
+    first = turn(first_rows, pair, lane)
+    second = lax.ppermute(second_rows, "context", TWIST_OUT)
+    values = [first, second, side_swap(first), side_swap(second)]
+    places = jnp.stack(
+        [2 * lane + side, 2 * (1 - lane) + side, 2 * lane + 1 - side, 2 * (1 - lane) + 1 - side]
+    ).astype(jnp.int32)
+    return join_rows(places, values, out_dtype)
 
 
 def on_device(
@@ -326,22 +656,25 @@
     owner = lax.axis_index("dp")
     shards = lax.axis_size("dp")
     shard = width // shards
+    half_shard = shard // 2
     mine = 2 * pair + side
 
     q_cols, kv_cols, o_rows = query_weight.shape[1] // 2, key_weight.shape[1] // 2, out_weight.shape[0] // 2
-    attn_shard = jnp.concatenate(
-        [
-            cut(query_weight, lane, q_cols, 1),
-            cut(key_weight, lane, kv_cols, 1),
-            cut(value_weight, lane, kv_cols, 1),
-            cut(out_weight, lane, o_rows, 0).T,
-        ],
-        axis=1,
+    attn_shard = row_major(
+        jnp.concatenate(
+            [
+                cut(query_weight, lane, q_cols, 1),
+                cut(key_weight, lane, kv_cols, 1),
+                cut(value_weight, lane, kv_cols, 1),
+                cut(out_weight, lane, o_rows, 0).T,
+            ],
+            axis=1,
+        )
     )
     qkv_cols = q_cols + 2 * kv_cols
-    attn_own = lax.all_gather(cross_swap(attn_shard), "dp", axis=0, tiled=True)
-    qkv_own, out_own = attn_own[:, :qkv_cols], attn_own[:, qkv_cols:]
-    qkv_far, out_far = side_swap(qkv_own), side_swap(out_own)
+    attn_own = lax.all_gather(row_major(cross_swap(attn_shard, lane, side)), "dp", axis=0, tiled=True)
+    qkv_own, out_own = row_major(attn_own[:, :qkv_cols]), row_major(attn_own[:, qkv_cols:])
+    qkv_far, out_far = row_major(side_swap(qkv_own)), row_major(side_swap(out_own))
 
     gains_all = lax.all_gather(jnp.concatenate([norm_gains, head_gains], axis=1), "dp", axis=0)
     gains_full = gains_all[:, :, :shard].transpose(1, 0, 2).reshape(2, width).astype(f32)
@@ -350,28 +683,20 @@
     gain_attn, gain_ffn = gains_full[0], gains_full[1]
 
     hidden = gate_weight.shape[1] // 2
-    half_shard = shard // 2
-    ffn_shard = jnp.concatenate(
-        [
-            cut(cut(gate_weight, lane, half_shard, 0), pair, hidden, 1),
-            cut(cut(up_weight, lane, half_shard, 0), pair, hidden, 1),
-            cut(cut(down_weight, lane, half_shard, 1), pair, hidden, 0).T,
-        ],
-        axis=1,
-    )
-    ffn_own = lax.all_gather(ffn_shard, "dp", axis=0, tiled=True).reshape(shards, half_shard, 3 * hidden)
-    ffn_far = lane_swap(ffn_own)
-    ffn_full = jnp.concatenate(
-        [pick(lane == 0, ffn_own, ffn_far), pick(lane == 0, ffn_far, ffn_own)], axis=1
-    ).reshape(width, 3 * hidden)
-    gate_full, up_full, down_full = (
-        ffn_full[:, :hidden],
-        ffn_full[:, hidden : 2 * hidden],
-        ffn_full[:, 2 * hidden :],
-    )
-
-    first_in = lax.ppermute(
-        lax.dynamic_index_in_dim(inputs, 2 * lane + side, 0, False), "context", TURN
+    ffn_shard = row_major(
+        jnp.concatenate(
+            [
+                cut(cut(gate_weight, lane, half_shard, 0), pair, hidden, 1),
+                cut(cut(up_weight, lane, half_shard, 0), pair, hidden, 1),
+                cut(cut(down_weight, lane, half_shard, 1), pair, hidden, 0).T,
+            ],
+            axis=1,
+        )
+    )
+    ffn_own = row_major(lax.all_gather(ffn_shard, "dp", axis=0, tiled=True))
+
+    first_in = turn(
+        lax.dynamic_index_in_dim(inputs, 2 * lane + side, 0, False), pair, lane
     )
     second_in = lax.ppermute(
         lax.dynamic_index_in_dim(inputs, 2 * (1 - lane) + side, 0, False), "context", TWIST_IN
@@ -382,13 +707,9 @@
     position = context * block_len + jnp.arange(block_len, dtype=jnp.int32)
     live = position[None, :] < lengths[:, None]
     upstream_low = jnp.where(live[:, :, None], cotangent, jnp.zeros((), bf16))
-    up_first = lax.ppermute(upstream_low, "context", TURN)
+    upstream_low = after(upstream_low, first_in, second_in)
+    up_first = turn(upstream_low, pair, lane)
     up_second = lax.ppermute(upstream_low, "context", TWIST_IN)
-
-    def upstream_rows(sequence, turned):
-        one = lax.dynamic_index_in_dim(up_first, sequence, 0, False)
-        two = lax.dynamic_index_in_dim(up_second, sequence, 0, False)
-        return jnp.concatenate([two, one] if turned else [one, two], axis=0)
 
     scale_one = rms_scale(x_half)
     normal_one = x_half * scale_one
@@ -399,6 +720,7 @@
     table = jnp.concatenate([local_block, lax.dynamic_slice_in_dim(lengths, mine, 1)]).astype(jnp.int32)
     cosine, sine = rope_tables(full_len)
     qkv = [nn(normed_one, qkv_own), nn(normed_one, qkv_far)]
+    qkv[1] = after(qkv[1], up_first, up_second)
     mixed, inverse, q_rot, k_rot = zip(
         *[attend_forward(table, value, cosine, sine, head_pair) for value in qkv]
     )
@@ -408,90 +730,89 @@
     scale_two = rms_scale(middle)
     normal_two = middle * scale_two
     normed_a = (normal_two * gain_ffn).astype(bf16)
+    ffn_own = after(ffn_own, normed_a)
+    ffn_far = row_major(lane_swap(ffn_own))
     normed_b = side_swap(normed_a)
     normed_c = pair_swap(normed_a)
+
+    far_pair = 2 * (1 - pair)
+    sequences = jnp.stack(
+        [mine, 2 * pair + 1 - side, far_pair + side, far_pair + 1 - side]
+    ).astype(jnp.int32)
+
+    def run(index, normed, out_dtype):
+        return feed_forward(
+            sequences[index], index >= 2, out_dtype, shards, normed, up_first, up_second, ffn_own, ffn_far
+        )
+
+    done_a = run(0, normed_a, f32)
+    normed_b, normed_c = after(normed_b, done_a[0]), after(normed_c, done_a[0])
     normed_d = jnp.concatenate(
         [side_swap(normed_c[:block_len]), pair_swap(normed_b[block_len:])], axis=0
     )
-
-    def feed_forward(normed, grad):
-        gate_proj = nn(normed, gate_full)
-        up_proj = nn(normed, up_full)
-        hidden_grad = nn(grad, down_full)
-        sigmoid_gate = jax.nn.sigmoid(gate_proj)
-        silu_gate = gate_proj * sigmoid_gate
-        hidden_low = (silu_gate * up_proj).astype(bf16)
-        gate_grad = (
-            hidden_grad * up_proj * sigmoid_gate * (1.0 + gate_proj * (1.0 - sigmoid_gate))
-        ).astype(bf16)
-        up_grad = (hidden_grad * silu_gate).astype(bf16)
-        feed = nt(hidden_low, down_full)
-        back = nt(gate_grad, gate_full) + nt(up_grad, up_full)
-        return feed, back, hidden_low, gate_grad, up_grad
-
-    far_pair = 2 * (1 - pair)
-    grads = {
-        "a": upstream_rows(mine, False),
-        "b": upstream_rows(2 * pair + 1 - side, False),
-        "c": upstream_rows(far_pair + side, True),
-        "d": upstream_rows(far_pair + 1 - side, True),
-    }
-    normed = {"a": normed_a, "b": normed_b, "c": normed_c, "d": normed_d}
-    done = {key: feed_forward(normed[key], grads[key]) for key in "abdc"}
-
-    def gather_sum(which):
-        part = {key: done[key][which] for key in "abcd"}
-        low_d = part["d"].astype(bf16)
-        from_side = side_swap(low_d[block_len:])
-        from_pair = pair_swap(low_d[:block_len])
-        send_b = jnp.concatenate(
-            [part["b"][:block_len] + from_pair.astype(f32), part["b"][block_len:]], axis=0
-        ).astype(bf16)
-        send_c = jnp.concatenate(
-            [part["c"][:block_len], part["c"][block_len:] + from_side.astype(f32)], axis=0
-        ).astype(bf16)
-        return part["a"] + side_swap(send_b).astype(f32) + pair_swap(send_c).astype(f32)
-
-    back_two = gather_sum(1)
-    normed_rows = jnp.concatenate([normed[key] for key in "abcd"], axis=0)
-    grad_rows = jnp.concatenate([grads[key] for key in "abcd"], axis=0)
-    hidden_rows = jnp.concatenate([done[key][2] for key in "abcd"], axis=0)
-    gate_rows = jnp.concatenate([done[key][3] for key in "abcd"], axis=0)
-    up_rows = jnp.concatenate([done[key][4] for key in "abcd"], axis=0)
-    ffn_grad = jnp.concatenate(
-        [tn(normed_rows, gate_rows), tn(normed_rows, up_rows), tn(grad_rows, hidden_rows)], axis=1
-    ).reshape(shards, 2, half_shard, 3 * hidden)
-    ffn_send = lax.dynamic_index_in_dim(ffn_grad, 1 - lane, 1, False).astype(bf16)
-    ffn_keep = lax.dynamic_index_in_dim(ffn_grad, lane, 1, False)
-    ffn_sum = (ffn_keep + lane_swap(ffn_send).astype(f32)).astype(bf16).reshape(shards * half_shard, 3 * hidden)
-    ffn_piece = lax.psum_scatter(ffn_sum, "dp", scatter_dimension=0, tiled=True)
+    done_b = run(1, normed_b, bf16)
+    done_d = run(3, after(normed_d, done_b[0]), bf16)
+    done_c = run(2, after(normed_c, done_d[0]), bf16)
+
+    def first_stage(which):
+        return side_swap(done_d[which][block_len:]), pair_swap(done_d[which][:block_len])
+
+    def second_stage(which, from_side, from_pair):
+        b, c = done_b[which], done_c[which]
+        send_b = jnp.concatenate([b[:block_len] + from_pair, b[block_len:]], axis=0)
+        send_c = jnp.concatenate([c[:block_len], c[block_len:] + from_side], axis=0)
+        return send_b, send_c
+
+    back_from = first_stage(1)
+    rights = [(done_a, done_b, done_c, done_d)[i][2] for i in range(4)]
+    down_near, down_far = down_grad(shards, sequences, up_first, up_second, rights)
+    send_b, send_c = second_stage(1, *back_from)
+    back_b, back_c = side_swap(send_b), pair_swap(send_c)
+    lefts = [normed_a, normed_b, normed_c, normed_d]
+    lefts[0] = after(normed_a, send_b, send_c, down_near)
+    gates = [(done_a, done_b, done_c, done_d)[i][3] for i in range(4)]
+    ups = [(done_a, done_b, done_c, done_d)[i][4] for i in range(4)]
+    gate_near, gate_far = left_grad(shards, lefts, gates)
+    lefts[0] = after(lefts[0], gate_near)
+    up_near, up_far = left_grad(shards, lefts, ups)
+    ffn_sum = jnp.concatenate(
+        [
+            gate_near + lane_swap(gate_far),
+            up_near + lane_swap(up_far),
+            down_near + lane_swap(down_far),
+        ],
+        axis=1,
+    )
+    ffn_piece = row_major(lax.psum_scatter(row_major(ffn_sum), "dp", scatter_dimension=0, tiled=True))
     ffn_pair = pair_swap(ffn_piece)
-    both = jnp.concatenate([ffn_piece, ffn_pair], axis=1)
-    both_far = lane_swap(both)
-    low_rows, high_rows = pick(lane == 0, both, both_far), pick(lane == 0, both_far, both)
-    rows_all = jnp.concatenate([low_rows, high_rows], axis=0).astype(f32)
-    near_cols, far_cols = rows_all[:, : 3 * hidden], rows_all[:, 3 * hidden :]
-    left, right = pick(pair == 0, near_cols, far_cols), pick(pair == 0, far_cols, near_cols)
-    gate_shard, up_shard, down_turned = [
-        jnp.concatenate(
-            [left[:, i * hidden : (i + 1) * hidden], right[:, i * hidden : (i + 1) * hidden]], axis=1
-        )
-        for i in range(3)
-    ]
-    down_shard = down_turned.T
-
-    feed_sum = gather_sum(0)
+    gate_shard, up_shard, down_shard = join_ffn(
+        ffn_piece, ffn_pair, lane_swap(ffn_piece), lane_swap(ffn_pair)
+    )
+
+    upstream = jnp.concatenate(
+        [
+            lax.dynamic_index_in_dim(up_first, mine, 0, False),
+            lax.dynamic_index_in_dim(up_second, mine, 0, False),
+        ],
+        axis=0,
+    ).astype(f32)
+    back_two = done_a[1] + back_b.astype(f32) + back_c.astype(f32)
+    gain_ffn_grad = jnp.sum(back_two * normal_two, axis=0)
+    middle_grad = upstream + norm_back(back_two * gain_ffn, normal_two, scale_two)
+    feed_from = first_stage(0)
+    send_b, send_c = second_stage(0, *feed_from)
+    send_b, send_c = after(send_b, back_two), after(send_c, back_two)
+    feed_sum = done_a[0] + side_swap(send_b).astype(f32) + pair_swap(send_c).astype(f32)
     out_half = (middle + feed_sum).astype(bf16)
-    outputs = spread(out_half, lane, side, bf16)
-
-    gain_ffn_grad = jnp.sum(back_two * normal_two, axis=0)
-    middle_grad = grads["a"].astype(f32) + norm_back(back_two * gain_ffn, normal_two, scale_two)
-    attn_low = middle_grad.astype(bf16)
+
+    attn_low = after(middle_grad.astype(bf16), up_near)
     attn_grad = jnp.concatenate([attn_low, lane_swap(attn_low)], axis=0)
     weights = [(qkv_own, out_own), (qkv_far, out_far)]
-    parts, back_one, gain_parts = [], None, 0.0
+    pieces, back_one, gain_parts = {}, None, 0.0
     for which in (1, 0):
         mixed_grad = nn(attn_grad, weights[which][1]).astype(bf16)
+        if which == 0:
+            mixed_grad = after(mixed_grad, pieces[1][0], send_b, send_c)
         qkv_grad, gain_part = attend_backward(
             table,
             qkv[which],
@@ -504,49 +825,37 @@
             inverse[which],
             mixed_grad,
         )
-        parts.append(
-            jnp.concatenate([tn(normed_one, qkv_grad), tn(attn_grad, mixed[which])], axis=1)
-        )
+        pieces[which] = attn_weight_grad(shards, normed_one, qkv_grad, attn_grad, mixed[which])
         term = nt(qkv_grad, weights[which][0])
         back_one = term if back_one is None else back_one + term
         gain_parts = gain_parts + gain_part
     back_recv = lane_swap(back_one[half_len:].astype(bf16))
     back_half = back_one[:half_len] + back_recv.astype(f32)
     gain_attn_grad = jnp.sum(back_half * normal_one, axis=0)
-    input_half = middle_grad + norm_back(back_half * gain_attn, normal_one, scale_one)
-    input_grad = spread(input_half.astype(bf16), lane, side, f32)
-
-    attn_sum = (parts[1] + side_swap(parts[0].astype(bf16)).astype(f32)).reshape(
-        shards, 2, half_shard, qkv_cols + o_rows
-    )
-    attn_send = lax.dynamic_index_in_dim(attn_sum, 1 - pair, 1, False).astype(bf16)
-    attn_keep = lax.dynamic_index_in_dim(attn_sum, pair, 1, False)
-    attn_sum = (attn_keep + pair_swap(attn_send).astype(f32)).astype(bf16)
-    attn_piece = lax.psum_scatter(
-        attn_sum.reshape(shards * half_shard, qkv_cols + o_rows), "dp", scatter_dimension=0, tiled=True
-    )
-    attn_piece = cross_swap(attn_piece)
+    outputs = spread(out_half[:block_len], out_half[block_len:], pair, lane, side, bf16)
+    back_half = after(back_half, out_half)
+    input_half = (middle_grad + norm_back(back_half * gain_attn, normal_one, scale_one)).astype(bf16)
+    input_grad = spread(input_half[:block_len], input_half[block_len:], pair, lane, side, f32)
+
+    near, far = (mine_part + side_swap(other) for mine_part, other in zip(pieces[0], pieces[1]))
+    attn_sum = row_major(near + pair_swap(far))
+    attn_piece = row_major(lax.psum_scatter(attn_sum, "dp", scatter_dimension=0, tiled=True))
+    attn_piece = cross_swap(attn_piece, lane, side)
     piece_pair = pair_swap(attn_piece)
-    columns = jnp.concatenate(
-        [pick(pair == 0, attn_piece, piece_pair), pick(pair == 0, piece_pair, attn_piece)], axis=0
-    )
-    columns_far = lane_swap(columns)
-    left = pick(lane == 0, columns, columns_far).astype(f32)
-    right = pick(lane == 0, columns_far, columns).astype(f32)
-    query_shard = jnp.concatenate([left[:, :q_cols], right[:, :q_cols]], axis=1)
-    key_shard = jnp.concatenate(
-        [left[:, q_cols : q_cols + kv_cols], right[:, q_cols : q_cols + kv_cols]], axis=1
-    )
-    value_shard = jnp.concatenate(
-        [left[:, q_cols + kv_cols : qkv_cols], right[:, q_cols + kv_cols : qkv_cols]], axis=1
-    )
-    out_shard = jnp.concatenate([left[:, qkv_cols:].T, right[:, qkv_cols:].T], axis=0)
+    query_shard, key_shard, value_shard, out_shard = join_attn(
+        q_cols, kv_cols, attn_piece, piece_pair, lane_swap(attn_piece), lane_swap(piece_pair)
+    )
 
     head_grad = gain_parts[:2, :HD] + gain_parts[:2, HD:]
-    gain_total = lax.psum(
-        jnp.concatenate([jnp.stack([gain_attn_grad, gain_ffn_grad]), head_grad], axis=1),
-        ("dp", "context", "tensor"),
-    )
+    gain_total = jnp.concatenate([jnp.stack([gain_attn_grad, gain_ffn_grad]), head_grad], axis=1)
+    gain_total = gain_total + lane_swap(gain_total)
+    gain_total = gain_total + side_swap(gain_total)
+    gain_total = gain_total + pair_swap(gain_total)
+    hop = 1
+    while hop < shards:
+        pairs = [(i, i ^ hop) for i in range(shards)]
+        gain_total = gain_total + lax.ppermute(gain_total, "dp", pairs)
+        hop *= 2
     gain_shard = cut(gain_total[:, :width], owner, shard, 1)
     head_shard = cut(gain_total[:, width:], owner, HD // shards, 1)
     return (

time: 670 us -> 512 us (0.76); the launches traced: 657 us -> 507 us
  Pallas kernels: 43 us -> 162 us
  matrix products: 120 us -> 23.4 us
  local copies, waits for them, and re-layouts: 107 us -> 31.4 us
  waiting for transfers between devices: 175 us -> 118 us
  blocking collectives: 68.1 us -> 12.2 us
  starting transfers between devices: 64.7 us -> 96.6 us
  other arithmetic: 64.1 us -> 48.3 us
    pallas_call x0 -> x13, Pallas kernels: none -> 119 us  [the longest x4 54.8 us: feed_forward(): pl.pallas_call(functools.partial(feed_forward_kernel, shards, turned), gr...]
    psum x1 -> x0, blocking collectives: 55.9 us -> none  [on_device(): lax.psum(jnp.concatenate([jnp.stack([gain_attn_grad, gain_ffn_grad]), hea...]
    dot_general x7 -> x0, matrix products: 40.1 us -> none  [tn(): lax.dot_general(left, right, (((0,), (0,)), ((), ())), preferred_element_...]
    unnamed x150 -> x94, local copies, waits for them, and re-layouts: 47.4 us -> 10.9 us
    dot_general x16 -> x4, matrix products: 48.8 us -> 14 us  [nn(): return jnp.dot(left, right, preferred_element_type=f32)]
    dot_general x16 -> x4, matrix products: 31 us -> 9.34 us  [nt(): lax.dot_general(left, right, (((1,), (1,)), ((), ())), preferred_element_...]
    ppermute x1, waiting for transfers between devices: 23.5 us -> 4.63 us  [on_device(): up_second = lax.ppermute(upstream_low, 'context', TWIST_IN)]
    ppermute x9 -> x10, waiting for transfers between devices: 76.2 us -> 59 us  [pair_swap(): return lax.ppermute(value, 'context', PAIR_SWAP)]
  transfers between devices with their start and end apart: 42 -> 54, of which waited for: 18 -> 22; matrix products, arithmetic and copies ran while one was open for 33% -> 17% of each run, Pallas kernels for 7% -> 28%
where the time goes in v2:
time: 512 us; the launch traced here: 507 us
  Pallas kernels  162 us (32%)
  waiting for transfers between devices  118 us (23%)
  starting transfers between devices  96.6 us (19%)
  other arithmetic  48.3 us (9%)
  local copies, waits for them, and re-layouts  31.4 us (6%)
  matrix products  23.4 us (5%)
  between operations  14.9 us (3%)
  blocking collectives  12.2 us (2%)
    ppermute x10, waiting for transfers between devices, pair_swap(): return lax.ppermute(value, 'context', PAIR_SWAP)  59 us
    pallas_call x4, Pallas kernels, feed_forward(): pl.pallas_call(functools.partial(feed_forward_kernel, shards, turned), gr...  54.8 us
    ppermute x15, waiting for transfers between devices, side_swap(): return lax.ppermute(value, 'tensor', SIDE_SWAP)  40.2 us
    pallas_call x2, Pallas kernels, attend_backward(): pl.pallas_call(attend_backward_kernel, out_shape=(jax.ShapeDtypeStruct((f...  27.9 us
    ppermute x13, starting transfers between devices, lane_swap(): return lax.ppermute(value, 'context', LANE_SWAP)  23.9 us
    pallas_call x2, Pallas kernels, left_grad(): pl.pallas_call(functools.partial(left_grad_kernel, shards), grid=(3,), in...  22.9 us
    ppermute x15, starting transfers between devices, side_swap(): return lax.ppermute(value, 'tensor', SIDE_SWAP)  17.6 us
    ppermute x2, starting transfers between devices, spread(): second = lax.ppermute(second_rows, 'context', TWIST_OUT)  16.6 us
  transfers between devices with their start and end apart: 54, of which 22 were waited for; matrix products, arithmetic and copies ran while one was open for 17% of the time, Pallas kernels for 28%

profile of v2, /device:TPU:0, one launch (start us, length us, event | category | flops | bytes accessed | tf_op | source)
XLA Modules:
  0.0 506.8 jit_solution(6888971439954713890)
XLA Ops:
  23.2 12.2 %all-gather.1 = bf16[4,2,272]{2,1,0:T(2,128)(2,1)S(1)} all-gather(bf16[1,2,272]{2,1,0:T(2,128)(2,1)S(1)} %maximum_bitcast_fusion), channel_id=2, replica_groups=mesh['dp'=4,'context'=4,'tensor'=2] {'dp'}, dimensions={0}, use_global_device_ids=true | all-gather | bytes 5440 | tf_op jit(solution)/shard_map/all_gather | solution.py:679
  39.9 10.3 %collective-permute-start.6 = (bf16[4,256,1024]{2,1,0:T(8,128)(2,1)}, bf16[4,256,1024]{2,1,0:T(8,128)(2,1)S(1)}, u32[]{:S(2)}, u32[]{:S(2)}) collective-permute-start(bf16[4,256,1024]{2,1,0:T(8,128)(2,1)} %broadcast_select_fusion), channel_id=1, source_target_pairs={{0,4},{2,0},{4,6},{6,2},{1,5},{3,1},{5,7},{7,3},{8,12},{10,8},{12,... | collective-permute-start | bytes 6291464 | tf_op jit(solution)/shard_map/ppermute | solution.py:712
  71.0 4.1 fusion.18.qkv_ref
  75.2 7.4 %shard_map.203 = (bf16[1024,256]{1,0:T(8,128)(2,1)}, f32[1024,256]{1,0:T(8,128)}, bf16[1024,256]{1,0:T(8,128)(2,1)}, bf16[1024,128]{1,0:T(8,128)(2,1)}) custom-call(s32[5]{0:T(128)} %pad_add_fusion.1.table, f32[1024,512]{1,0:T(8,128)} %fusion.18.qkv_ref, f32[1024,128]{1,0:T(8,128)} %get-tuple-element.174.cos_ref, f32[1024,128]{1,0:T(8,128)} %get-tuple-element.175.sin_ref, ...), custom_call_target="tpu_custom_call" | custom-call | flops 1000000000 | bytes 1000000 | tf_op jit(solution)/shard_map/pallas_call | solution.py:265
  86.1 4.4 fusion.22.qkv_ref
  90.5 4.6 collective-permute-done.6.second_ref
  95.1 8.2 %shard_map.204 = (bf16[1024,256]{1,0:T(8,128)(2,1)}, f32[1024,256]{1,0:T(8,128)}, bf16[1024,256]{1,0:T(8,128)(2,1)}, bf16[1024,128]{1,0:T(8,128)(2,1)}) custom-call(s32[5]{0:T(128)} %pad_add_fusion.1.table, f32[1024,512]{1,0:T(8,128)} %fusion.22.qkv_ref, f32[1024,128]{1,0:T(8,128)} %get-tuple-element.174.cos_ref, f32[1024,128]{1,0:T(8,128)} %get-tuple-element.175.sin_ref, ...), custom_call_target="tpu_custom_call" | custom-call | flops 1000000000 | bytes 1000000 | tf_op jit(solution)/shard_map/pallas_call | solution.py:265
  107.7 20.8 %collective-permute-start.8 = (bf16[512,1024]{1,0:T(8,128)(2,1)S(1)}, bf16[512,1024]{1,0:T(8,128)(2,1)S(1)}, u32[]{:S(2)}, u32[]{:S(2)}) collective-permute-start(bf16[512,1024]{1,0:T(8,128)(2,1)S(1)} %slice.171), channel_id=1, source_target_pairs={{0,2},{2,0},{4,6},{6,4},{1,3},{3,1},{5,7},{7,5},{8,10},{10,8},{12,... | collective-permute-start | bytes 3145736 | tf_op jit(solution)/shard_map/ppermute | solution.py:30
  142.1 13.9 %shard_map.205 = (f32[512,1024]{1,0:T(8,128)}, f32[512,1024]{1,0:T(8,128)}, bf16[512,1152]{1,0:T(8,128)(2,1)}, bf16[512,1152]{1,0:T(8,128)(2,1)}, bf16[512,1152]{1,0:T(8,128)(2,1)}) custom-call(s32[1]{0:T(128)} %bitcast.11.table, bf16[512,1024]{1,0:T(8,128)(2,1)} %multiply_convert_fusion.normed_ref.refs_0_, ...), custom_call_target="tpu_custom_call" | custom-call | flops 603979776 | bytes 1000000 | tf_op jit(solution)/shard_map/pallas_call | solution.py:383
  156.0 4.6 collective-permute-done.11.normed_ref.refs_2_
  164.8 13.6 %shard_map.206 = (bf16[512,1024]{1,0:T(8,128)(2,1)}, bf16[512,1024]{1,0:T(8,128)(2,1)}, bf16[512,1152]{1,0:T(8,128)(2,1)}, bf16[512,1152]{1,0:T(8,128)(2,1)}, bf16[512,1152]{1,0:T(8,128)(2,1)}) custom-call(s32[1]{0:T(128)} %bitcast.14.table, bf16[512,1024]{1,0:T(8,128)(2,1)} %collective-permute-done.10.normed_ref.refs_1_, ...), custom_call_target="tpu_custom_call" | custom-call | flops 603979776 | bytes 1000000 | tf_op jit(solution)/shard_map/pallas_call | solution.py:383
  179.5 13.8 %shard_map.207 = (bf16[512,1024]{1,0:T(8,128)(2,1)}, bf16[512,1024]{1,0:T(8,128)(2,1)}, bf16[512,1152]{1,0:T(8,128)(2,1)}, bf16[512,1152]{1,0:T(8,128)(2,1)}, bf16[512,1152]{1,0:T(8,128)(2,1)}) custom-call(s32[1]{0:T(128)} %bitcast.15.table, bf16[512,1024]{1,0:T(8,128)(2,1)} %copy-done.10, bf16[4,256,1024]{2,1,0:T(8,128)(2,1)} %broadcast_select_fusion.1.first_ref, ...), custom_call_target="tpu_custom_call" | custom-call | flops 603979776 | bytes 1000000 | tf_op jit(solution)/shard_map/pallas_call | solution.py:383
  199.9 13.6 %shard_map.208 = (bf16[512,1024]{1,0:T(8,128)(2,1)}, bf16[512,1024]{1,0:T(8,128)(2,1)}, bf16[512,1152]{1,0:T(8,128)(2,1)}, bf16[512,1152]{1,0:T(8,128)(2,1)}, bf16[512,1152]{1,0:T(8,128)(2,1)}) custom-call(s32[1]{0:T(128)} %bitcast.16.table, bf16[512,1024]{1,0:T(8,128)(2,1)} %collective-permute-done.11.normed_ref.refs_2_, ...), custom_call_target="tpu_custom_call" | custom-call | flops 603979776 | bytes 1000000 | tf_op jit(solution)/shard_map/pallas_call | solution.py:383
  213.5 12.3 %shard_map.210 = (bf16[512,1152]{1,0:T(8,128)(2,1)}, bf16[512,1152]{1,0:T(8,128)(2,1)}) custom-call(s32[4]{0:T(128)} %pad_add_fusion.2.table, bf16[4,256,1024]{2,1,0:T(8,128)(2,1)} %broadcast_select_fusion.1.first_ref, bf16[4,256,1024]{2,1,0:T(8,128)(2,1)} %copy-done, bf16[512,1152]{1,0:T(8,128)(2,1)} %get-tuple-element.96.refs_0_, ...), custom_call_target="tpu_custom_call" | custom-call | flops 603979776 | bytes 1000000 | tf_op jit(solution)/shard_map/pallas_call | solution.py:478
  228.5 11.4 %shard_map.211 = (bf16[512,1152]{1,0:T(8,128)(2,1)}, bf16[512,1152]{1,0:T(8,128)(2,1)}) custom-call(bf16[512,1024]{1,0:T(8,128)(2,1)} %multiply_convert_fusion.normed_ref.refs_0_, bf16[512,1024]{1,0:T(8,128)(2,1)} %collective-permute-done.10.normed_ref.refs_1_, bf16[512,1024]{1,0:T(8,128)(2,1)} %collective-permute-done.11.normed_ref.refs_2_, ...), custom_call_target="tpu_custom_call" | custom-call | flops 603979776 | bytes 1000000 | tf_op jit(solution)/shard_map/pallas_call | solution.py:443
  240.5 11.4 %shard_map.212 = (bf16[512,1152]{1,0:T(8,128)(2,1)}, bf16[512,1152]{1,0:T(8,128)(2,1)}) custom-call(bf16[512,1024]{1,0:T(8,128)(2,1)} %multiply_convert_fusion.normed_ref.refs_0_, bf16[512,1024]{1,0:T(8,128)(2,1)} %collective-permute-done.10.normed_ref.refs_1_, bf16[512,1024]{1,0:T(8,128)(2,1)} %collective-permute-done.11.normed_ref.refs_2_, ...), custom_call_target="tpu_custom_call" | custom-call | flops 603979776 | bytes 1000000 | tf_op jit(solution)/shard_map/pallas_call | solution.py:443
  255.6 11.4 %collective-permute-done.14 = bf16[256,1024]{1,0:T(8,128)(2,1)S(1)} collective-permute-done((bf16[256,1024]{1,0:T(8,128)(2,1)}, bf16[256,1024]{1,0:T(8,128)(2,1)S(1)}, u32[]{:S(2)}, u32[]{:S(2)}) %collective-permute-start.14) | collective-permute-done | bytes 524320 | tf_op jit(solution)/shard_map/ppermute | solution.py:34
  275.8 13.1 %collective-permute-done.18 = bf16[512,1024]{1,0:T(8,128)(2,1)S(1)} collective-permute-done((bf16[512,1024]{1,0:T(8,128)(2,1)}, bf16[512,1024]{1,0:T(8,128)(2,1)S(1)}, u32[]{:S(2)}, u32[]{:S(2)}) %collective-permute-start.18) | collective-permute-done | bytes 1048608 | tf_op jit(solution)/shard_map/ppermute | solution.py:34
  299.9 17.7 %collective-permute-done.21 = bf16[512,1024]{1,0:T(8,128)(2,1)S(1)} collective-permute-done((bf16[512,1024]{1,0:T(8,128)(2,1)S(1)}, bf16[512,1024]{1,0:T(8,128)(2,1)S(1)}, u32[]{:S(2)}, u32[]{:S(2)}) %collective-permute-start.21) | collective-permute-done | bytes 1048608 | tf_op jit(solution)/shard_map/ppermute | solution.py:34
  327.5 13.9 %shard_map.213 = (bf16[1024,512]{1,0:T(8,128)(2,1)}, f32[8,128]{1,0:T(8,128)}) custom-call(s32[5]{0:T(128)} %pad_add_fusion.1.table, f32[1024,512]{1,0:T(8,128)} %fusion.22.qkv_ref, f32[1024,128]{1,0:T(8,128)} %get-tuple-element.174.cos_ref, f32[1024,128]{1,0:T(8,128)} %get-tuple-element.175.sin_ref, f32[2,128]{1,0:T(2,128)} %maximum_convert_fusion.gain_ref, ...), custom_call_target="tpu_custom_call" | custom-call | flops 2000000000 | bytes 1000000 | tf_op jit(solution)/shard_map/pallas_call | solution.py:282
  341.4 5.9 %shard_map.214 = (bf16[512,768]{1,0:T(8,128)(2,1)}, bf16[512,768]{1,0:T(8,128)(2,1)}) custom-call(bf16[1024,1024]{1,0:T(8,128)(2,1)} %pad_maximum_fusion.1.normed_ref, bf16[1024,512]{1,0:T(8,128)(2,1)} %get-tuple-element.114.grad_ref, bf16[1024,1024]{1,0:T(8,128)(2,1)} %copy-done.8, bf16[1024,256]{1,0:T(8,128)(2,1)} %get-tuple-element.77.out_ref.mixed_ref), custom_call_target="tpu_custom_call" | custom-call | flops 100000000 | bytes 1000000 | tf_op jit(solution)/shard_map/pallas_call | solution.py:505
  349.9 14.0 %shard_map.215 = (bf16[1024,512]{1,0:T(8,128)(2,1)}, f32[8,128]{1,0:T(8,128)}) custom-call(s32[5]{0:T(128)} %pad_add_fusion.1.table, f32[1024,512]{1,0:T(8,128)} %fusion.18.qkv_ref, f32[1024,128]{1,0:T(8,128)} %get-tuple-element.174.cos_ref, f32[1024,128]{1,0:T(8,128)} %get-tuple-element.175.sin_ref, f32[2,128]{1,0:T(2,128)} %maximum_convert_fusion.gain_ref, ...), custom_call_target="tpu_custom_call" | custom-call | flops 2000000000 | bytes 1000000 | tf_op jit(solution)/shard_map/pallas_call | solution.py:282
  373.2 8.5 %collective-permute-start.23 = (bf16[256,1024]{1,0:T(8,128)(2,1)}, bf16[256,1024]{1,0:T(8,128)(2,1)}, u32[]{:S(2)}, u32[]{:S(2)}) collective-permute-start(bf16[256,1024]{1,0:T(8,128)(2,1)} %get-tuple-element.151), channel_id=1, source_target_pairs={{4,0},{0,2},{6,4},{2,6},{5,1},{1,3},{7,5},{3,7},{12,8},{8,10},{14,... | collective-permute-start | bytes 1572872 | tf_op jit(solution)/shard_map/ppermute | solution.py:630
  383.2 5.7 %shard_map.217 = (bf16[512,768]{1,0:T(8,128)(2,1)}, bf16[512,768]{1,0:T(8,128)(2,1)}) custom-call(bf16[1024,1024]{1,0:T(8,128)(2,1)} %pad_maximum_fusion.1.normed_ref, bf16[1024,512]{1,0:T(8,128)(2,1)} %get-tuple-element.120.grad_ref, bf16[1024,1024]{1,0:T(8,128)(2,1)} %copy-done.8, bf16[1024,256]{1,0:T(8,128)(2,1)} %get-tuple-element.74.out_ref.mixed_ref), custom_call_target="tpu_custom_call" | custom-call | flops 100000000 | bytes 1000000 | tf_op jit(solution)/shard_map/pallas_call | solution.py:505
  398.3 9.1 %collective-permute-done.32 = bf16[512,768]{1,0:T(8,128)(2,1)} collective-permute-done((bf16[512,768]{1,0:T(8,128)(2,1)}, bf16[512,768]{1,0:T(8,128)(2,1)}, u32[]{:S(2)}, u32[]{:S(2)}) %collective-permute-start.32) | collective-permute-done | bytes 786464 | tf_op jit(solution)/shard_map/ppermute | solution.py:38
  407.4 5.5 %collective-permute-done.34 = bf16[512,768]{1,0:T(8,128)(2,1)S(1)} collective-permute-done((bf16[512,768]{1,0:T(8,128)(2,1)S(1)}, bf16[512,768]{1,0:T(8,128)(2,1)S(1)}, u32[]{:S(2)}, u32[]{:S(2)}) %collective-permute-start.34) | collective-permute-done | bytes 786464 | tf_op jit(solution)/shard_map/ppermute | solution.py:34
  425.6 8.1 %collective-permute-start.29 = (bf16[256,1024]{1,0:T(8,128)(2,1)}, bf16[256,1024]{1,0:T(8,128)(2,1)}, u32[]{:S(2)}, u32[]{:S(2)}) collective-permute-start(bf16[256,1024]{1,0:T(8,128)(2,1)} %get-tuple-element.149), channel_id=1, source_target_pairs={{4,0},{0,2},{6,4},{2,6},{5,1},{1,3},{7,5},{3,7},{12,8},{8,10},{14,... | collective-permute-start | bytes 1572872 | tf_op jit(solution)/shard_map/ppermute | solution.py:630
  435.3 9.6 %collective-permute-done.46 = f32[2,1088]{1,0:T(2,128)S(1)} collective-permute-done((f32[2,1088]{1,0:T(2,128)S(1)}, f32[2,1088]{1,0:T(2,128)S(1)}, u32[]{:S(2)}, u32[]{:S(2)}) %collective-permute-start.46) | collective-permute-done | bytes 8736 | tf_op jit(solution)/shard_map/ppermute | solution.py:38
  448.0 5.0 collective-permute-done.47
  475.2 9.5 %collective-permute-done.31.d = bf16[256,1024]{1,0:T(8,128)(2,1)} collective-permute-done((bf16[256,1024]{1,0:T(8,128)(2,1)}, bf16[256,1024]{1,0:T(8,128)(2,1)}, u32[]{:S(2)}, u32[]{:S(2)}) %collective-permute-start.31) | collective-permute-done | bytes 524320 | tf_op jit(solution)/shard_map/ppermute | solution.py:38
  484.7 4.7 shard_map.216
  494.1 5.9 %shard_map.219 = (f32[256,2304]{1,0:T(8,128)}, f32[256,2304]{1,0:T(8,128)}, f32[2304,256]{1,0:T(8,128)}) custom-call(bf16[128,3456]{1,0:T(8,128)(2,1)} %reduce-scatter.5.cloned.1.call-done.a, bf16[128,3456]{1,0:T(8,128)(2,1)} %copy-done.33, bf16[128,3456]{1,0:T(8,128)(2,1)} %copy-done.34, bf16[128,3456]{1,0:T(8,128)(2,1)} %collective-permute-done.44.d), custom_call_target="tpu_custom_call" | custom-call | flops 1000000 | bytes 1000000 | tf_op jit(solution)/shard_map/pallas_call | solution.py:547
  (287 shorter events, 177.6 us)
Async XLA Ops:
  7.2 52.2 %all-gather.5.cloned.1.call-start = ((), (), s32[]{:S(2)}) async-start(), calls=%async_computation.2 | async-start | bytes 1966080 | tf_op jit(solution)/shard_map/all_gather | solution.py:675
  11.0 122.9 %all-gather.7.cloned.1.call-start = ((), (), s32[]{:S(2)}) async-start(), calls=%async_computation.3 | async-start | bytes 4423680 | tf_op jit(solution)/shard_map/all_gather | solution.py:696
  12.0 25.1 %collective-permute-start.1 = (bf16[256,1024]{1,0:T(8,128)(2,1)}, bf16[256,1024]{1,0:T(8,128)(2,1)S(1)}, u32[]{:S(2)}, u32[]{:S(2)}) collective-permute-start(bf16[256,1024]{1,0:T(8,128)(2,1)} %get-tuple-element.148), channel_id=1, source_target_pairs={{0,4},{2,0},{4,6},{6,2},{1,5},{3,1},{5,7},{7,3},{8,12},{10,8},{12,... | collective-permute-start | bytes 1572872 | tf_op jit(solution)/shard_map/ppermute | solution.py:701
  15.0 22.1 %collective-permute-start = (bf16[256,1024]{1,0:T(8,128)(2,1)S(1)}, bf16[256,1024]{1,0:T(8,128)(2,1)}, u32[]{:S(2)}, u32[]{:S(2)}) collective-permute-start(bf16[256,1024]{1,0:T(8,128)(2,1)S(1)} %get-tuple-element.147), channel_id=1, source_target_pairs={{2,4},{4,2},{3,5},{5,3},{10,12},{12,10},{11,13},{13,11},{18,20},{2... | collective-permute-start | bytes 1572872 | tf_op jit(solution)/shard_map/ppermute | solution.py:47
  23.1 398.2 %reduce-scatter.5.cloned.1.call-start = ((), (), s32[]{:S(2)}) async-start(), calls=%async_computation.5 | async-start | bytes 4423680 | tf_op jit(solution)/shard_map/reduce_scatter | solution.py:786
  37.1 29.3 %collective-permute-start.5 = (bf16[4,256,1024]{2,1,0:T(8,128)(2,1)}, bf16[4,256,1024]{2,1,0:T(8,128)(2,1)}, u32[]{:S(2)}, u32[]{:S(2)}) collective-permute-start(bf16[4,256,1024]{2,1,0:T(8,128)(2,1)} %broadcast_select_fusion), channel_id=1, source_target_pairs={{2,4},{4,2},{3,5},{5,3},{10,12},{12,10},{11,13},{13,11},{18,20},{2... | collective-permute-start | bytes 6291464 | tf_op jit(solution)/shard_map/ppermute | solution.py:47
  39.9 55.2 %collective-permute-start.6 = (bf16[4,256,1024]{2,1,0:T(8,128)(2,1)}, bf16[4,256,1024]{2,1,0:T(8,128)(2,1)S(1)}, u32[]{:S(2)}, u32[]{:S(2)}) collective-permute-start(bf16[4,256,1024]{2,1,0:T(8,128)(2,1)} %broadcast_select_fusion), channel_id=1, source_target_pairs={{0,4},{2,0},{4,6},{6,2},{1,5},{3,1},{5,7},{7,3},{8,12},{10,8},{12,... | collective-permute-start | bytes 6291464 | tf_op jit(solution)/shard_map/ppermute | solution.py:712
  61.7 24.3 %collective-permute-start.4 = (bf16[1024,512]{1,0:T(8,128)(2,1)}, bf16[1024,512]{1,0:T(8,128)(2,1)}, u32[]{:S(2)}, u32[]{:S(2)}) collective-permute-start(bf16[1024,512]{1,0:T(8,128)(2,1)} %slice.134), channel_id=1, source_target_pairs={{0,1},{1,0},{2,3},{3,2},{4,5},{5,4},{6,7},{7,6},{8,9},{9,8},{10,11... | collective-permute-start | bytes 3145736 | tf_op jit(solution)/shard_map/ppermute | solution.py:38
  70.7 32.6 %collective-permute-start.7 = (bf16[1024,256]{1,0:T(8,128)(2,1)}, bf16[1024,256]{1,0:T(8,128)(2,1)}, u32[]{:S(2)}, u32[]{:S(2)}) collective-permute-start(bf16[1024,256]{1,0:T(8,128)(2,1)} %slice.136), channel_id=1, source_target_pairs={{0,1},{1,0},{2,3},{3,2},{4,5},{5,4},{6,7},{7,6},{8,9},{9,8},{10,11... | collective-permute-start | bytes 1572872 | tf_op jit(solution)/shard_map/ppermute | solution.py:38
  107.7 23.1 %collective-permute-start.8 = (bf16[512,1024]{1,0:T(8,128)(2,1)S(1)}, bf16[512,1024]{1,0:T(8,128)(2,1)S(1)}, u32[]{:S(2)}, u32[]{:S(2)}) collective-permute-start(bf16[512,1024]{1,0:T(8,128)(2,1)S(1)} %slice.171), channel_id=1, source_target_pairs={{0,2},{2,0},{4,6},{6,4},{1,3},{3,1},{5,7},{7,5},{8,10},{10,8},{12,... | collective-permute-start | bytes 3145736 | tf_op jit(solution)/shard_map/ppermute | solution.py:30
  134.3 26.3 %collective-permute-start.11 = (bf16[512,1024]{1,0:T(8,128)(2,1)}, bf16[512,1024]{1,0:T(8,128)(2,1)}, u32[]{:S(2)}, u32[]{:S(2)}) collective-permute-start(bf16[512,1024]{1,0:T(8,128)(2,1)} %multiply_convert_fusion.normed_ref.refs_0_), channel_id=1, source_target_pairs={{0,4},{4,0},{2,6},{6,2},{1,5},{5,1},{3,7},{7,3},{8,12},{12,8},{10,... | collective-permute-start | bytes 3145736 | tf_op jit(solution)/shard_map/ppermute | solution.py:34
  136.6 25.5 %collective-permute-start.10 = (bf16[512,1024]{1,0:T(8,128)(2,1)}, bf16[512,1024]{1,0:T(8,128)(2,1)}, u32[]{:S(2)}, u32[]{:S(2)}) collective-permute-start(bf16[512,1024]{1,0:T(8,128)(2,1)} %multiply_convert_fusion.normed_ref.refs_0_), channel_id=1, source_target_pairs={{0,1},{1,0},{2,3},{3,2},{4,5},{5,4},{6,7},{7,6},{8,9},{9,8},{10,11... | collective-permute-start | bytes 3145736 | tf_op jit(solution)/shard_map/ppermute | solution.py:38
  195.7 30.1 %collective-permute-start.17 = (bf16[256,1024]{1,0:T(8,128)(2,1)}, bf16[256,1024]{1,0:T(8,128)(2,1)S(1)}, u32[]{:S(2)}, u32[]{:S(2)}) collective-permute-start(bf16[256,1024]{1,0:T(8,128)(2,1)} %get-tuple-element.160), channel_id=1, source_target_pairs={{0,1},{1,0},{2,3},{3,2},{4,5},{5,4},{6,7},{7,6},{8,9},{9,8},{10,11... | collective-permute-start | bytes 1572872 | tf_op jit(solution)/shard_map/ppermute | solution.py:38
  198.2 28.7 %collective-permute-start.15 = (bf16[256,1024]{1,0:T(8,128)(2,1)}, bf16[256,1024]{1,0:T(8,128)(2,1)S(1)}, u32[]{:S(2)}, u32[]{:S(2)}) collective-permute-start(bf16[256,1024]{1,0:T(8,128)(2,1)} %get-tuple-element.159), channel_id=1, source_target_pairs={{0,4},{4,0},{2,6},{6,2},{1,5},{5,1},{3,7},{7,3},{8,12},{12,8},{10,... | collective-permute-start | bytes 1572872 | tf_op jit(solution)/shard_map/ppermute | solution.py:34
  199.5 54.0 %collective-permute-start.20 = (bf16[256,1024]{1,0:T(8,128)(2,1)}, bf16[256,1024]{1,0:T(8,128)(2,1)}, u32[]{:S(2)}, u32[]{:S(2)}) collective-permute-start(bf16[256,1024]{1,0:T(8,128)(2,1)} %get-tuple-element.156), channel_id=1, source_target_pairs={{0,1},{1,0},{2,3},{3,2},{4,5},{5,4},{6,7},{7,6},{8,9},{9,8},{10,11... | collective-permute-start | bytes 1572872 | tf_op jit(solution)/shard_map/ppermute | solution.py:38
  225.7 45.2 %collective-permute-start.41 = (bf16[512,1152]{1,0:T(8,128)(2,1)}, bf16[512,1152]{1,0:T(8,128)(2,1)S(1)}, u32[]{:S(2)}, u32[]{:S(2)}) collective-permute-start(bf16[512,1152]{1,0:T(8,128)(2,1)} %get-tuple-element.131), channel_id=1, source_target_pairs={{0,2},{2,0},{4,6},{6,4},{1,3},{3,1},{5,7},{7,5},{8,10},{10,8},{12,... | collective-permute-start | bytes 3538952 | tf_op jit(solution)/shard_map/ppermute | solution.py:30
  239.9 31.9 %collective-permute-start.39 = (bf16[512,1152]{1,0:T(8,128)(2,1)}, bf16[512,1152]{1,0:T(8,128)(2,1)S(1)}, u32[]{:S(2)}, u32[]{:S(2)}) collective-permute-start(bf16[512,1152]{1,0:T(8,128)(2,1)} %get-tuple-element.129), channel_id=1, source_target_pairs={{0,2},{2,0},{4,6},{6,4},{1,3},{3,1},{5,7},{7,5},{8,10},{10,8},{12,... | collective-permute-start | bytes 3538952 | tf_op jit(solution)/shard_map/ppermute | solution.py:30
  253.6 35.4 %collective-permute-start.18 = (bf16[512,1024]{1,0:T(8,128)(2,1)}, bf16[512,1024]{1,0:T(8,128)(2,1)S(1)}, u32[]{:S(2)}, u32[]{:S(2)}) collective-permute-start(bf16[512,1024]{1,0:T(8,128)(2,1)} %pad_maximum_fusion.5), channel_id=1, source_target_pairs={{0,4},{4,0},{2,6},{6,2},{1,5},{5,1},{3,7},{7,3},{8,12},{12,8},{10,... | collective-permute-start | bytes 3145736 | tf_op jit(solution)/shard_map/ppermute | solution.py:34
  267.0 24.4 %collective-permute-start.16 = (bf16[512,1024]{1,0:T(8,128)(2,1)}, bf16[512,1024]{1,0:T(8,128)(2,1)}, u32[]{:S(2)}, u32[]{:S(2)}) collective-permute-start(bf16[512,1024]{1,0:T(8,128)(2,1)} %pad_maximum_fusion.4), channel_id=1, source_target_pairs={{0,1},{1,0},{2,3},{3,2},{4,5},{5,4},{6,7},{7,6},{8,9},{9,8},{10,11... | collective-permute-start | bytes 3145736 | tf_op jit(solution)/shard_map/ppermute | solution.py:38
  275.4 177.7 %reduce-scatter.3.cloned.1.call-start = ((), (), s32[]{:S(2)}) async-start(), calls=%async_computation.4 | async-start | bytes 983040 | tf_op jit(solution)/shard_map/reduce_scatter | solution.py:842
  294.2 23.4 %collective-permute-start.21 = (bf16[512,1024]{1,0:T(8,128)(2,1)S(1)}, bf16[512,1024]{1,0:T(8,128)(2,1)S(1)}, u32[]{:S(2)}, u32[]{:S(2)}) collective-permute-start(bf16[512,1024]{1,0:T(8,128)(2,1)S(1)} %copy-done.28), channel_id=1, source_target_pairs={{0,4},{4,0},{2,6},{6,2},{1,5},{5,1},{3,7},{7,3},{8,12},{12,8},{10,... | collective-permute-start | bytes 3145736 | tf_op jit(solution)/shard_map/ppermute | solution.py:34
  296.0 23.1 %collective-permute-start.19 = (bf16[512,1024]{1,0:T(8,128)(2,1)S(1)}, bf16[512,1024]{1,0:T(8,128)(2,1)S(1)}, u32[]{:S(2)}, u32[]{:S(2)}) collective-permute-start(bf16[512,1024]{1,0:T(8,128)(2,1)S(1)} %copy-done.29), channel_id=1, source_target_pairs={{0,1},{1,0},{2,3},{3,2},{4,5},{5,4},{6,7},{7,6},{8,9},{9,8},{10,11... | collective-permute-start | bytes 3145736 | tf_op jit(solution)/shard_map/ppermute | solution.py:38
  369.2 26.3 %collective-permute-start.27 = (bf16[512,1024]{1,0:T(8,128)(2,1)S(1)}, bf16[512,1024]{1,0:T(8,128)(2,1)}, u32[]{:S(2)}, u32[]{:S(2)}) collective-permute-start(bf16[512,1024]{1,0:T(8,128)(2,1)S(1)} %slice.170), channel_id=1, source_target_pairs={{0,2},{2,0},{4,6},{6,4},{1,3},{3,1},{5,7},{7,5},{8,10},{10,8},{12,... | collective-permute-start | bytes 3145736 | tf_op jit(solution)/shard_map/ppermute | solution.py:30
  373.2 47.5 %collective-permute-start.23 = (bf16[256,1024]{1,0:T(8,128)(2,1)}, bf16[256,1024]{1,0:T(8,128)(2,1)}, u32[]{:S(2)}, u32[]{:S(2)}) collective-permute-start(bf16[256,1024]{1,0:T(8,128)(2,1)} %get-tuple-element.151), channel_id=1, source_target_pairs={{4,0},{0,2},{6,4},{2,6},{5,1},{1,3},{7,5},{3,7},{12,8},{8,10},{14,... | collective-permute-start | bytes 1572872 | tf_op jit(solution)/shard_map/ppermute | solution.py:630
  381.7 25.8 %collective-permute-start.32 = (bf16[512,768]{1,0:T(8,128)(2,1)}, bf16[512,768]{1,0:T(8,128)(2,1)}, u32[]{:S(2)}, u32[]{:S(2)}) collective-permute-start(bf16[512,768]{1,0:T(8,128)(2,1)} %get-tuple-element.118), channel_id=1, source_target_pairs={{0,1},{1,0},{2,3},{3,2},{4,5},{5,4},{6,7},{7,6},{8,9},{9,8},{10,11... | collective-permute-start | bytes 2359304 | tf_op jit(solution)/shard_map/ppermute | solution.py:38
  419.1 28.2 %collective-permute-start.24 = (bf16[256,1024]{1,0:T(8,128)(2,1)}, bf16[256,1024]{1,0:T(8,128)(2,1)}, u32[]{:S(2)}, u32[]{:S(2)}) collective-permute-start(bf16[256,1024]{1,0:T(8,128)(2,1)} %get-tuple-element.152.a), channel_id=1, source_target_pairs={{0,1},{1,0},{2,3},{3,2},{4,5},{5,4},{6,7},{7,6},{8,9},{9,8},{10,11... | collective-permute-start | bytes 1572872 | tf_op jit(solution)/shard_map/ppermute | solution.py:38
  420.7 33.3 %collective-permute-start.25 = (bf16[256,1024]{1,0:T(8,128)(2,1)}, bf16[256,1024]{1,0:T(8,128)(2,1)}, u32[]{:S(2)}, u32[]{:S(2)}) collective-permute-start(bf16[256,1024]{1,0:T(8,128)(2,1)} %collective-permute-done.23.b), channel_id=1, source_target_pairs={{0,1},{1,0},{2,3},{3,2},{4,5},{5,4},{6,7},{7,6},{8,9},{9,8},{10,11... | collective-permute-start | bytes 1572872 | tf_op jit(solution)/shard_map/ppermute | solution.py:38
  421.3 25.9 %collective-permute-start.42 = (bf16[128,3456]{1,0:T(8,128)(2,1)}, bf16[128,3456]{1,0:T(8,128)(2,1)S(1)}, u32[]{:S(2)}, u32[]{:S(2)}) collective-permute-start(bf16[128,3456]{1,0:T(8,128)(2,1)} %reduce-scatter.5.cloned.1.call-done.a), channel_id=1, source_target_pairs={{0,4},{4,0},{2,6},{6,2},{1,5},{5,1},{3,7},{7,3},{8,12},{12,8},{10,... | collective-permute-start | bytes 2654216 | tf_op jit(solution)/shard_map/ppermute | solution.py:34
  425.6 35.0 %collective-permute-start.29 = (bf16[256,1024]{1,0:T(8,128)(2,1)}, bf16[256,1024]{1,0:T(8,128)(2,1)}, u32[]{:S(2)}, u32[]{:S(2)}) collective-permute-start(bf16[256,1024]{1,0:T(8,128)(2,1)} %get-tuple-element.149), channel_id=1, source_target_pairs={{4,0},{0,2},{6,4},{2,6},{5,1},{1,3},{7,5},{3,7},{12,8},{8,10},{14,... | collective-permute-start | bytes 1572872 | tf_op jit(solution)/shard_map/ppermute | solution.py:630
  444.9 48.2 %collective-permute-start.43 = (bf16[128,3456]{1,0:T(8,128)(2,1)S(1)}, bf16[128,3456]{1,0:T(8,128)(2,1)S(1)}, u32[]{:S(2)}, u32[]{:S(2)}) collective-permute-start(bf16[128,3456]{1,0:T(8,128)(2,1)S(1)} %copy-done.32), channel_id=1, source_target_pairs={{0,2},{2,0},{4,6},{6,4},{1,3},{3,1},{5,7},{7,5},{8,10},{10,8},{12,... | collective-permute-start | bytes 2654216 | tf_op jit(solution)/shard_map/ppermute | solution.py:30
  447.2 45.9 %collective-permute-start.44 = (bf16[128,3456]{1,0:T(8,128)(2,1)S(1)}, bf16[128,3456]{1,0:T(8,128)(2,1)}, u32[]{:S(2)}, u32[]{:S(2)}) collective-permute-start(bf16[128,3456]{1,0:T(8,128)(2,1)S(1)} %collective-permute-done.42.b), channel_id=1, source_target_pairs={{0,2},{2,0},{4,6},{6,4},{1,3},{3,1},{5,7},{7,5},{8,10},{10,8},{12,... | collective-permute-start | bytes 2654216 | tf_op jit(solution)/shard_map/ppermute | solution.py:30
  461.9 22.8 %collective-permute-start.31 = (bf16[256,1024]{1,0:T(8,128)(2,1)}, bf16[256,1024]{1,0:T(8,128)(2,1)}, u32[]{:S(2)}, u32[]{:S(2)}) collective-permute-start(bf16[256,1024]{1,0:T(8,128)(2,1)} %collective-permute-done.29.b), channel_id=1, source_target_pairs={{0,1},{1,0},{2,3},{3,2},{4,5},{5,4},{6,7},{7,6},{8,9},{9,8},{10,11... | collective-permute-start | bytes 1572872 | tf_op jit(solution)/shard_map/ppermute | solution.py:38
  (67 other events, 777.0 us)
Sparse Core Ops, SparseCore 0:
  11.1 48.1 all-gather.4
  61.5 68.7 all-gather.6
  275.5 65.6 reduce-scatter.4
  415.3 22.0 reduce-scatter.2

commit v3 on v2

--- a/solution.py
+++ b/solution.py
@@ -767,9 +767,11 @@
     rights = [(done_a, done_b, done_c, done_d)[i][2] for i in range(4)]
     down_near, down_far = down_grad(shards, sequences, up_first, up_second, rights)
     send_b, send_c = second_stage(1, *back_from)
+    lefts = [normed_a, normed_b, normed_c, normed_d]
+    send_b, send_c, lefts[0], down_near = lax.optimization_barrier(
+        (send_b, send_c, normed_a, down_near)
+    )
     back_b, back_c = side_swap(send_b), pair_swap(send_c)
-    lefts = [normed_a, normed_b, normed_c, normed_d]
-    lefts[0] = after(normed_a, send_b, send_c, down_near)
     gates = [(done_a, done_b, done_c, done_d)[i][3] for i in range(4)]
     ups = [(done_a, done_b, done_c, done_d)[i][4] for i in range(4)]
     gate_near, gate_far = left_grad(shards, lefts, gates)

time: 512 us -> 512 us (level)
  no operation moved by 1% of the time
where the time goes in v3:
time: 512 us; the launch traced here: 507 us
  Pallas kernels  162 us (32%)
  waiting for transfers between devices  118 us (23%)
  starting transfers between devices  96.6 us (19%)
  other arithmetic  48.3 us (9%)
  local copies, waits for them, and re-layouts  31.4 us (6%)
  matrix products  23.4 us (5%)
  between operations  14.9 us (3%)
  blocking collectives  12.2 us (2%)
    ppermute x10, waiting for transfers between devices, pair_swap(): return lax.ppermute(value, 'context', PAIR_SWAP)  59 us
    pallas_call x4, Pallas kernels, feed_forward(): pl.pallas_call(functools.partial(feed_forward_kernel, shards, turned), gr...  54.8 us
    ppermute x15, waiting for transfers between devices, side_swap(): return lax.ppermute(value, 'tensor', SIDE_SWAP)  40.2 us
    pallas_call x2, Pallas kernels, attend_backward(): pl.pallas_call(attend_backward_kernel, out_shape=(jax.ShapeDtypeStruct((f...  27.9 us
    ppermute x13, starting transfers between devices, lane_swap(): return lax.ppermute(value, 'context', LANE_SWAP)  23.9 us
    pallas_call x2, Pallas kernels, left_grad(): pl.pallas_call(functools.partial(left_grad_kernel, shards), grid=(3,), in...  22.9 us
    ppermute x15, starting transfers between devices, side_swap(): return lax.ppermute(value, 'tensor', SIDE_SWAP)  17.4 us
    ppermute x2, starting transfers between devices, spread(): second = lax.ppermute(second_rows, 'context', TWIST_OUT)  16.6 us
  transfers between devices with their start and end apart: 54, of which 22 were waited for; matrix products, arithmetic and copies ran while one was open for 17% of the time, Pallas kernels for 28%

profile of v3, /device:TPU:0, one launch (start us, length us, event | category | flops | bytes accessed | tf_op | source)
XLA Modules:
  0.0 506.8 jit_solution(7227532669641487867)
XLA Ops:
  23.2 12.2 %all-gather.1 = bf16[4,2,272]{2,1,0:T(2,128)(2,1)S(1)} all-gather(bf16[1,2,272]{2,1,0:T(2,128)(2,1)S(1)} %maximum_bitcast_fusion), channel_id=2, replica_groups=mesh['dp'=4,'context'=4,'tensor'=2] {'dp'}, dimensions={0}, use_global_device_ids=true | all-gather | bytes 5440 | tf_op jit(solution)/shard_map/all_gather | solution.py:679
  39.9 10.3 %collective-permute-start.6 = (bf16[4,256,1024]{2,1,0:T(8,128)(2,1)}, bf16[4,256,1024]{2,1,0:T(8,128)(2,1)S(1)}, u32[]{:S(2)}, u32[]{:S(2)}) collective-permute-start(bf16[4,256,1024]{2,1,0:T(8,128)(2,1)} %broadcast_select_fusion), channel_id=1, source_target_pairs={{0,4},{2,0},{4,6},{6,2},{1,5},{3,1},{5,7},{7,3},{8,12},{10,8},{12,... | collective-permute-start | bytes 6291464 | tf_op jit(solution)/shard_map/ppermute | solution.py:712
  71.0 4.1 fusion.18.qkv_ref
  75.2 7.4 %shard_map.203 = (bf16[1024,256]{1,0:T(8,128)(2,1)}, f32[1024,256]{1,0:T(8,128)}, bf16[1024,256]{1,0:T(8,128)(2,1)}, bf16[1024,128]{1,0:T(8,128)(2,1)}) custom-call(s32[5]{0:T(128)} %pad_add_fusion.1.table, f32[1024,512]{1,0:T(8,128)} %fusion.18.qkv_ref, f32[1024,128]{1,0:T(8,128)} %get-tuple-element.180.cos_ref, f32[1024,128]{1,0:T(8,128)} %get-tuple-element.181.sin_ref, ...), custom_call_target="tpu_custom_call" | custom-call | flops 1000000000 | bytes 1000000 | tf_op jit(solution)/shard_map/pallas_call | solution.py:265
  86.1 4.4 fusion.22.qkv_ref
  90.5 4.6 collective-permute-done.6.second_ref
  95.1 8.2 %shard_map.204 = (bf16[1024,256]{1,0:T(8,128)(2,1)}, f32[1024,256]{1,0:T(8,128)}, bf16[1024,256]{1,0:T(8,128)(2,1)}, bf16[1024,128]{1,0:T(8,128)(2,1)}) custom-call(s32[5]{0:T(128)} %pad_add_fusion.1.table, f32[1024,512]{1,0:T(8,128)} %fusion.22.qkv_ref, f32[1024,128]{1,0:T(8,128)} %get-tuple-element.180.cos_ref, f32[1024,128]{1,0:T(8,128)} %get-tuple-element.181.sin_ref, ...), custom_call_target="tpu_custom_call" | custom-call | flops 1000000000 | bytes 1000000 | tf_op jit(solution)/shard_map/pallas_call | solution.py:265
  107.7 20.8 %collective-permute-start.8 = (bf16[512,1024]{1,0:T(8,128)(2,1)S(1)}, bf16[512,1024]{1,0:T(8,128)(2,1)S(1)}, u32[]{:S(2)}, u32[]{:S(2)}) collective-permute-start(bf16[512,1024]{1,0:T(8,128)(2,1)S(1)} %slice.171), channel_id=1, source_target_pairs={{0,2},{2,0},{4,6},{6,4},{1,3},{3,1},{5,7},{7,5},{8,10},{10,8},{12,... | collective-permute-start | bytes 3145736 | tf_op jit(solution)/shard_map/ppermute | solution.py:30
  142.1 13.9 %shard_map.205 = (f32[512,1024]{1,0:T(8,128)}, f32[512,1024]{1,0:T(8,128)}, bf16[512,1152]{1,0:T(8,128)(2,1)}, bf16[512,1152]{1,0:T(8,128)(2,1)}, bf16[512,1152]{1,0:T(8,128)(2,1)}) custom-call(s32[1]{0:T(128)} %bitcast.11.table, bf16[512,1024]{1,0:T(8,128)(2,1)} %multiply_convert_fusion.normed_ref.refs_0_, ...), custom_call_target="tpu_custom_call" | custom-call | flops 603979776 | bytes 1000000 | tf_op jit(solution)/shard_map/pallas_call | solution.py:383
  156.0 4.6 collective-permute-done.11.normed_ref.refs_2_
  164.8 13.6 %shard_map.206 = (bf16[512,1024]{1,0:T(8,128)(2,1)}, bf16[512,1024]{1,0:T(8,128)(2,1)}, bf16[512,1152]{1,0:T(8,128)(2,1)}, bf16[512,1152]{1,0:T(8,128)(2,1)}, bf16[512,1152]{1,0:T(8,128)(2,1)}) custom-call(s32[1]{0:T(128)} %bitcast.14.table, bf16[512,1024]{1,0:T(8,128)(2,1)} %collective-permute-done.10.normed_ref.refs_1_, ...), custom_call_target="tpu_custom_call" | custom-call | flops 603979776 | bytes 1000000 | tf_op jit(solution)/shard_map/pallas_call | solution.py:383
  179.5 13.8 %shard_map.207 = (bf16[512,1024]{1,0:T(8,128)(2,1)}, bf16[512,1024]{1,0:T(8,128)(2,1)}, bf16[512,1152]{1,0:T(8,128)(2,1)}, bf16[512,1152]{1,0:T(8,128)(2,1)}, bf16[512,1152]{1,0:T(8,128)(2,1)}) custom-call(s32[1]{0:T(128)} %bitcast.15.table, bf16[512,1024]{1,0:T(8,128)(2,1)} %copy-done.10, bf16[4,256,1024]{2,1,0:T(8,128)(2,1)} %broadcast_select_fusion.1.first_ref, ...), custom_call_target="tpu_custom_call" | custom-call | flops 603979776 | bytes 1000000 | tf_op jit(solution)/shard_map/pallas_call | solution.py:383
  199.9 13.6 %shard_map.208 = (bf16[512,1024]{1,0:T(8,128)(2,1)}, bf16[512,1024]{1,0:T(8,128)(2,1)}, bf16[512,1152]{1,0:T(8,128)(2,1)}, bf16[512,1152]{1,0:T(8,128)(2,1)}, bf16[512,1152]{1,0:T(8,128)(2,1)}) custom-call(s32[1]{0:T(128)} %bitcast.16.table, bf16[512,1024]{1,0:T(8,128)(2,1)} %collective-permute-done.11.normed_ref.refs_2_, ...), custom_call_target="tpu_custom_call" | custom-call | flops 603979776 | bytes 1000000 | tf_op jit(solution)/shard_map/pallas_call | solution.py:383
  213.5 12.3 %shard_map.209 = (bf16[512,1152]{1,0:T(8,128)(2,1)}, bf16[512,1152]{1,0:T(8,128)(2,1)}) custom-call(s32[4]{0:T(128)} %pad_add_fusion.2.table, bf16[4,256,1024]{2,1,0:T(8,128)(2,1)} %broadcast_select_fusion.1.first_ref, bf16[4,256,1024]{2,1,0:T(8,128)(2,1)} %copy-done, bf16[512,1152]{1,0:T(8,128)(2,1)} %get-tuple-element.93.refs_0_, ...), custom_call_target="tpu_custom_call" | custom-call | flops 603979776 | bytes 1000000 | tf_op jit(solution)/shard_map/pallas_call | solution.py:478
  228.5 11.4 %shard_map.211 = (bf16[512,1152]{1,0:T(8,128)(2,1)}, bf16[512,1152]{1,0:T(8,128)(2,1)}) custom-call(bf16[512,1024]{1,0:T(8,128)(2,1)} %multiply_convert_fusion.normed_ref.refs_0_, bf16[512,1024]{1,0:T(8,128)(2,1)} %collective-permute-done.10.normed_ref.refs_1_, bf16[512,1024]{1,0:T(8,128)(2,1)} %collective-permute-done.11.normed_ref.refs_2_, ...), custom_call_target="tpu_custom_call" | custom-call | flops 603979776 | bytes 1000000 | tf_op jit(solution)/shard_map/pallas_call | solution.py:443
  240.5 11.4 %shard_map.212 = (bf16[512,1152]{1,0:T(8,128)(2,1)}, bf16[512,1152]{1,0:T(8,128)(2,1)}) custom-call(bf16[512,1024]{1,0:T(8,128)(2,1)} %multiply_convert_fusion.normed_ref.refs_0_, bf16[512,1024]{1,0:T(8,128)(2,1)} %collective-permute-done.10.normed_ref.refs_1_, bf16[512,1024]{1,0:T(8,128)(2,1)} %collective-permute-done.11.normed_ref.refs_2_, ...), custom_call_target="tpu_custom_call" | custom-call | flops 603979776 | bytes 1000000 | tf_op jit(solution)/shard_map/pallas_call | solution.py:443
  255.6 11.4 %collective-permute-done.14 = bf16[256,1024]{1,0:T(8,128)(2,1)S(1)} collective-permute-done((bf16[256,1024]{1,0:T(8,128)(2,1)}, bf16[256,1024]{1,0:T(8,128)(2,1)S(1)}, u32[]{:S(2)}, u32[]{:S(2)}) %collective-permute-start.14) | collective-permute-done | bytes 524320 | tf_op jit(solution)/shard_map/ppermute | solution.py:34
  275.8 13.1 %collective-permute-done.18 = bf16[512,1024]{1,0:T(8,128)(2,1)S(1)} collective-permute-done((bf16[512,1024]{1,0:T(8,128)(2,1)}, bf16[512,1024]{1,0:T(8,128)(2,1)S(1)}, u32[]{:S(2)}, u32[]{:S(2)}) %collective-permute-start.18) | collective-permute-done | bytes 1048608 | tf_op jit(solution)/shard_map/ppermute | solution.py:34
  299.9 17.7 %collective-permute-done.21 = bf16[512,1024]{1,0:T(8,128)(2,1)S(1)} collective-permute-done((bf16[512,1024]{1,0:T(8,128)(2,1)S(1)}, bf16[512,1024]{1,0:T(8,128)(2,1)S(1)}, u32[]{:S(2)}, u32[]{:S(2)}) %collective-permute-start.21) | collective-permute-done | bytes 1048608 | tf_op jit(solution)/shard_map/ppermute | solution.py:34
  327.5 13.9 %shard_map.213 = (bf16[1024,512]{1,0:T(8,128)(2,1)}, f32[8,128]{1,0:T(8,128)}) custom-call(s32[5]{0:T(128)} %pad_add_fusion.1.table, f32[1024,512]{1,0:T(8,128)} %fusion.22.qkv_ref, f32[1024,128]{1,0:T(8,128)} %get-tuple-element.180.cos_ref, f32[1024,128]{1,0:T(8,128)} %get-tuple-element.181.sin_ref, f32[2,128]{1,0:T(2,128)} %maximum_convert_fusion.gain_ref, ...), custom_call_target="tpu_custom_call" | custom-call | flops 2000000000 | bytes 1000000 | tf_op jit(solution)/shard_map/pallas_call | solution.py:282
  341.4 5.9 %shard_map.214 = (bf16[512,768]{1,0:T(8,128)(2,1)}, bf16[512,768]{1,0:T(8,128)(2,1)}) custom-call(bf16[1024,1024]{1,0:T(8,128)(2,1)} %pad_maximum_fusion.1.normed_ref, bf16[1024,512]{1,0:T(8,128)(2,1)} %get-tuple-element.119.grad_ref, bf16[1024,1024]{1,0:T(8,128)(2,1)} %copy-done.8, bf16[1024,256]{1,0:T(8,128)(2,1)} %get-tuple-element.80.out_ref.mixed_ref), custom_call_target="tpu_custom_call" | custom-call | flops 100000000 | bytes 1000000 | tf_op jit(solution)/shard_map/pallas_call | solution.py:505
  349.9 14.0 %shard_map.215 = (bf16[1024,512]{1,0:T(8,128)(2,1)}, f32[8,128]{1,0:T(8,128)}) custom-call(s32[5]{0:T(128)} %pad_add_fusion.1.table, f32[1024,512]{1,0:T(8,128)} %fusion.18.qkv_ref, f32[1024,128]{1,0:T(8,128)} %get-tuple-element.180.cos_ref, f32[1024,128]{1,0:T(8,128)} %get-tuple-element.181.sin_ref, f32[2,128]{1,0:T(2,128)} %maximum_convert_fusion.gain_ref, ...), custom_call_target="tpu_custom_call" | custom-call | flops 2000000000 | bytes 1000000 | tf_op jit(solution)/shard_map/pallas_call | solution.py:282
  373.2 8.5 %collective-permute-start.23 = (bf16[256,1024]{1,0:T(8,128)(2,1)}, bf16[256,1024]{1,0:T(8,128)(2,1)}, u32[]{:S(2)}, u32[]{:S(2)}) collective-permute-start(bf16[256,1024]{1,0:T(8,128)(2,1)} %get-tuple-element.157), channel_id=1, source_target_pairs={{4,0},{0,2},{6,4},{2,6},{5,1},{1,3},{7,5},{3,7},{12,8},{8,10},{14,... | collective-permute-start | bytes 1572872 | tf_op jit(solution)/shard_map/ppermute | solution.py:630
  383.2 5.7 %shard_map.217 = (bf16[512,768]{1,0:T(8,128)(2,1)}, bf16[512,768]{1,0:T(8,128)(2,1)}) custom-call(bf16[1024,1024]{1,0:T(8,128)(2,1)} %pad_maximum_fusion.1.normed_ref, bf16[1024,512]{1,0:T(8,128)(2,1)} %get-tuple-element.125.grad_ref, bf16[1024,1024]{1,0:T(8,128)(2,1)} %copy-done.8, bf16[1024,256]{1,0:T(8,128)(2,1)} %get-tuple-element.77.out_ref.mixed_ref), custom_call_target="tpu_custom_call" | custom-call | flops 100000000 | bytes 1000000 | tf_op jit(solution)/shard_map/pallas_call | solution.py:505
  398.3 9.1 %collective-permute-done.32 = bf16[512,768]{1,0:T(8,128)(2,1)} collective-permute-done((bf16[512,768]{1,0:T(8,128)(2,1)}, bf16[512,768]{1,0:T(8,128)(2,1)}, u32[]{:S(2)}, u32[]{:S(2)}) %collective-permute-start.32) | collective-permute-done | bytes 786464 | tf_op jit(solution)/shard_map/ppermute | solution.py:38
  407.4 5.5 %collective-permute-done.34 = bf16[512,768]{1,0:T(8,128)(2,1)S(1)} collective-permute-done((bf16[512,768]{1,0:T(8,128)(2,1)S(1)}, bf16[512,768]{1,0:T(8,128)(2,1)S(1)}, u32[]{:S(2)}, u32[]{:S(2)}) %collective-permute-start.34) | collective-permute-done | bytes 786464 | tf_op jit(solution)/shard_map/ppermute | solution.py:34
  425.6 8.1 %collective-permute-start.29 = (bf16[256,1024]{1,0:T(8,128)(2,1)}, bf16[256,1024]{1,0:T(8,128)(2,1)}, u32[]{:S(2)}, u32[]{:S(2)}) collective-permute-start(bf16[256,1024]{1,0:T(8,128)(2,1)} %get-tuple-element.155), channel_id=1, source_target_pairs={{4,0},{0,2},{6,4},{2,6},{5,1},{1,3},{7,5},{3,7},{12,8},{8,10},{14,... | collective-permute-start | bytes 1572872 | tf_op jit(solution)/shard_map/ppermute | solution.py:630
  435.3 9.6 %collective-permute-done.46 = f32[2,1088]{1,0:T(2,128)S(1)} collective-permute-done((f32[2,1088]{1,0:T(2,128)S(1)}, f32[2,1088]{1,0:T(2,128)S(1)}, u32[]{:S(2)}, u32[]{:S(2)}) %collective-permute-start.46) | collective-permute-done | bytes 8736 | tf_op jit(solution)/shard_map/ppermute | solution.py:38
  448.0 5.0 collective-permute-done.47
  475.2 9.5 %collective-permute-done.31.d = bf16[256,1024]{1,0:T(8,128)(2,1)} collective-permute-done((bf16[256,1024]{1,0:T(8,128)(2,1)}, bf16[256,1024]{1,0:T(8,128)(2,1)}, u32[]{:S(2)}, u32[]{:S(2)}) %collective-permute-start.31) | collective-permute-done | bytes 524320 | tf_op jit(solution)/shard_map/ppermute | solution.py:38
  484.7 4.7 shard_map.216
  494.1 5.9 %shard_map.219 = (f32[256,2304]{1,0:T(8,128)}, f32[256,2304]{1,0:T(8,128)}, f32[2304,256]{1,0:T(8,128)}) custom-call(bf16[128,3456]{1,0:T(8,128)(2,1)} %reduce-scatter.5.cloned.1.call-done.a, bf16[128,3456]{1,0:T(8,128)(2,1)} %copy-done.33, bf16[128,3456]{1,0:T(8,128)(2,1)} %copy-done.34, bf16[128,3456]{1,0:T(8,128)(2,1)} %collective-permute-done.44.d), custom_call_target="tpu_custom_call" | custom-call | flops 1000000 | bytes 1000000 | tf_op jit(solution)/shard_map/pallas_call | solution.py:547
  (287 shorter events, 177.7 us)
Async XLA Ops:
  7.2 52.2 %all-gather.5.cloned.1.call-start = ((), (), s32[]{:S(2)}) async-start(), calls=%async_computation.2 | async-start | bytes 1966080 | tf_op jit(solution)/shard_map/all_gather | solution.py:675
  11.0 122.9 %all-gather.7.cloned.1.call-start = ((), (), s32[]{:S(2)}) async-start(), calls=%async_computation.3 | async-start | bytes 4423680 | tf_op jit(solution)/shard_map/all_gather | solution.py:696
  12.0 25.1 %collective-permute-start.1 = (bf16[256,1024]{1,0:T(8,128)(2,1)}, bf16[256,1024]{1,0:T(8,128)(2,1)S(1)}, u32[]{:S(2)}, u32[]{:S(2)}) collective-permute-start(bf16[256,1024]{1,0:T(8,128)(2,1)} %get-tuple-element.154), channel_id=1, source_target_pairs={{0,4},{2,0},{4,6},{6,2},{1,5},{3,1},{5,7},{7,3},{8,12},{10,8},{12,... | collective-permute-start | bytes 1572872 | tf_op jit(solution)/shard_map/ppermute | solution.py:701
  15.0 22.1 %collective-permute-start = (bf16[256,1024]{1,0:T(8,128)(2,1)S(1)}, bf16[256,1024]{1,0:T(8,128)(2,1)}, u32[]{:S(2)}, u32[]{:S(2)}) collective-permute-start(bf16[256,1024]{1,0:T(8,128)(2,1)S(1)} %get-tuple-element.153), channel_id=1, source_target_pairs={{2,4},{4,2},{3,5},{5,3},{10,12},{12,10},{11,13},{13,11},{18,20},{2... | collective-permute-start | bytes 1572872 | tf_op jit(solution)/shard_map/ppermute | solution.py:47
  23.1 398.2 %reduce-scatter.5.cloned.1.call-start = ((), (), s32[]{:S(2)}) async-start(), calls=%async_computation.5 | async-start | bytes 4423680 | tf_op jit(solution)/shard_map/reduce_scatter | solution.py:788
  37.1 29.3 %collective-permute-start.5 = (bf16[4,256,1024]{2,1,0:T(8,128)(2,1)}, bf16[4,256,1024]{2,1,0:T(8,128)(2,1)}, u32[]{:S(2)}, u32[]{:S(2)}) collective-permute-start(bf16[4,256,1024]{2,1,0:T(8,128)(2,1)} %broadcast_select_fusion), channel_id=1, source_target_pairs={{2,4},{4,2},{3,5},{5,3},{10,12},{12,10},{11,13},{13,11},{18,20},{2... | collective-permute-start | bytes 6291464 | tf_op jit(solution)/shard_map/ppermute | solution.py:47
  39.9 55.2 %collective-permute-start.6 = (bf16[4,256,1024]{2,1,0:T(8,128)(2,1)}, bf16[4,256,1024]{2,1,0:T(8,128)(2,1)S(1)}, u32[]{:S(2)}, u32[]{:S(2)}) collective-permute-start(bf16[4,256,1024]{2,1,0:T(8,128)(2,1)} %broadcast_select_fusion), channel_id=1, source_target_pairs={{0,4},{2,0},{4,6},{6,2},{1,5},{3,1},{5,7},{7,3},{8,12},{10,8},{12,... | collective-permute-start | bytes 6291464 | tf_op jit(solution)/shard_map/ppermute | solution.py:712
  61.7 24.3 %collective-permute-start.4 = (bf16[1024,512]{1,0:T(8,128)(2,1)}, bf16[1024,512]{1,0:T(8,128)(2,1)}, u32[]{:S(2)}, u32[]{:S(2)}) collective-permute-start(bf16[1024,512]{1,0:T(8,128)(2,1)} %slice.134), channel_id=1, source_target_pairs={{0,1},{1,0},{2,3},{3,2},{4,5},{5,4},{6,7},{7,6},{8,9},{9,8},{10,11... | collective-permute-start | bytes 3145736 | tf_op jit(solution)/shard_map/ppermute | solution.py:38
  70.7 32.6 %collective-permute-start.7 = (bf16[1024,256]{1,0:T(8,128)(2,1)}, bf16[1024,256]{1,0:T(8,128)(2,1)}, u32[]{:S(2)}, u32[]{:S(2)}) collective-permute-start(bf16[1024,256]{1,0:T(8,128)(2,1)} %slice.136), channel_id=1, source_target_pairs={{0,1},{1,0},{2,3},{3,2},{4,5},{5,4},{6,7},{7,6},{8,9},{9,8},{10,11... | collective-permute-start | bytes 1572872 | tf_op jit(solution)/shard_map/ppermute | solution.py:38
  107.7 23.1 %collective-permute-start.8 = (bf16[512,1024]{1,0:T(8,128)(2,1)S(1)}, bf16[512,1024]{1,0:T(8,128)(2,1)S(1)}, u32[]{:S(2)}, u32[]{:S(2)}) collective-permute-start(bf16[512,1024]{1,0:T(8,128)(2,1)S(1)} %slice.171), channel_id=1, source_target_pairs={{0,2},{2,0},{4,6},{6,4},{1,3},{3,1},{5,7},{7,5},{8,10},{10,8},{12,... | collective-permute-start | bytes 3145736 | tf_op jit(solution)/shard_map/ppermute | solution.py:30
  134.3 26.3 %collective-permute-start.11 = (bf16[512,1024]{1,0:T(8,128)(2,1)}, bf16[512,1024]{1,0:T(8,128)(2,1)}, u32[]{:S(2)}, u32[]{:S(2)}) collective-permute-start(bf16[512,1024]{1,0:T(8,128)(2,1)} %multiply_convert_fusion.normed_ref.refs_0_), channel_id=1, source_target_pairs={{0,4},{4,0},{2,6},{6,2},{1,5},{5,1},{3,7},{7,3},{8,12},{12,8},{10,... | collective-permute-start | bytes 3145736 | tf_op jit(solution)/shard_map/ppermute | solution.py:34
  136.6 25.5 %collective-permute-start.10 = (bf16[512,1024]{1,0:T(8,128)(2,1)}, bf16[512,1024]{1,0:T(8,128)(2,1)}, u32[]{:S(2)}, u32[]{:S(2)}) collective-permute-start(bf16[512,1024]{1,0:T(8,128)(2,1)} %multiply_convert_fusion.normed_ref.refs_0_), channel_id=1, source_target_pairs={{0,1},{1,0},{2,3},{3,2},{4,5},{5,4},{6,7},{7,6},{8,9},{9,8},{10,11... | collective-permute-start | bytes 3145736 | tf_op jit(solution)/shard_map/ppermute | solution.py:38
  195.7 30.1 %collective-permute-start.15 = (bf16[256,1024]{1,0:T(8,128)(2,1)}, bf16[256,1024]{1,0:T(8,128)(2,1)S(1)}, u32[]{:S(2)}, u32[]{:S(2)}) collective-permute-start(bf16[256,1024]{1,0:T(8,128)(2,1)} %get-tuple-element.166), channel_id=1, source_target_pairs={{0,4},{4,0},{2,6},{6,2},{1,5},{5,1},{3,7},{7,3},{8,12},{12,8},{10,... | collective-permute-start | bytes 1572872 | tf_op jit(solution)/shard_map/ppermute | solution.py:34
  196.8 30.1 %collective-permute-start.16 = (bf16[256,1024]{1,0:T(8,128)(2,1)}, bf16[256,1024]{1,0:T(8,128)(2,1)S(1)}, u32[]{:S(2)}, u32[]{:S(2)}) collective-permute-start(bf16[256,1024]{1,0:T(8,128)(2,1)} %get-tuple-element.165), channel_id=1, source_target_pairs={{0,1},{1,0},{2,3},{3,2},{4,5},{5,4},{6,7},{7,6},{8,9},{9,8},{10,11... | collective-permute-start | bytes 1572872 | tf_op jit(solution)/shard_map/ppermute | solution.py:38
  199.5 54.0 %collective-permute-start.20 = (bf16[256,1024]{1,0:T(8,128)(2,1)}, bf16[256,1024]{1,0:T(8,128)(2,1)}, u32[]{:S(2)}, u32[]{:S(2)}) collective-permute-start(bf16[256,1024]{1,0:T(8,128)(2,1)} %get-tuple-element.162), channel_id=1, source_target_pairs={{0,1},{1,0},{2,3},{3,2},{4,5},{5,4},{6,7},{7,6},{8,9},{9,8},{10,11... | collective-permute-start | bytes 1572872 | tf_op jit(solution)/shard_map/ppermute | solution.py:38
  225.7 45.2 %collective-permute-start.41 = (bf16[512,1152]{1,0:T(8,128)(2,1)}, bf16[512,1152]{1,0:T(8,128)(2,1)S(1)}, u32[]{:S(2)}, u32[]{:S(2)}) collective-permute-start(bf16[512,1152]{1,0:T(8,128)(2,1)} %get-tuple-element.137), channel_id=1, source_target_pairs={{0,2},{2,0},{4,6},{6,4},{1,3},{3,1},{5,7},{7,5},{8,10},{10,8},{12,... | collective-permute-start | bytes 3538952 | tf_op jit(solution)/shard_map/ppermute | solution.py:30
  239.9 31.9 %collective-permute-start.39 = (bf16[512,1152]{1,0:T(8,128)(2,1)}, bf16[512,1152]{1,0:T(8,128)(2,1)S(1)}, u32[]{:S(2)}, u32[]{:S(2)}) collective-permute-start(bf16[512,1152]{1,0:T(8,128)(2,1)} %get-tuple-element.134), channel_id=1, source_target_pairs={{0,2},{2,0},{4,6},{6,4},{1,3},{3,1},{5,7},{7,5},{8,10},{10,8},{12,... | collective-permute-start | bytes 3538952 | tf_op jit(solution)/shard_map/ppermute | solution.py:30
  253.6 35.4 %collective-permute-start.18 = (bf16[512,1024]{1,0:T(8,128)(2,1)}, bf16[512,1024]{1,0:T(8,128)(2,1)S(1)}, u32[]{:S(2)}, u32[]{:S(2)}) collective-permute-start(bf16[512,1024]{1,0:T(8,128)(2,1)} %pad_maximum_fusion.5), channel_id=1, source_target_pairs={{0,4},{4,0},{2,6},{6,2},{1,5},{5,1},{3,7},{7,3},{8,12},{12,8},{10,... | collective-permute-start | bytes 3145736 | tf_op jit(solution)/shard_map/ppermute | solution.py:34
  267.0 24.4 %collective-permute-start.17 = (bf16[512,1024]{1,0:T(8,128)(2,1)}, bf16[512,1024]{1,0:T(8,128)(2,1)}, u32[]{:S(2)}, u32[]{:S(2)}) collective-permute-start(bf16[512,1024]{1,0:T(8,128)(2,1)} %pad_maximum_fusion.4), channel_id=1, source_target_pairs={{0,1},{1,0},{2,3},{3,2},{4,5},{5,4},{6,7},{7,6},{8,9},{9,8},{10,11... | collective-permute-start | bytes 3145736 | tf_op jit(solution)/shard_map/ppermute | solution.py:38
  275.4 177.7 %reduce-scatter.3.cloned.1.call-start = ((), (), s32[]{:S(2)}) async-start(), calls=%async_computation.4 | async-start | bytes 983040 | tf_op jit(solution)/shard_map/reduce_scatter | solution.py:844
  294.2 23.4 %collective-permute-start.21 = (bf16[512,1024]{1,0:T(8,128)(2,1)S(1)}, bf16[512,1024]{1,0:T(8,128)(2,1)S(1)}, u32[]{:S(2)}, u32[]{:S(2)}) collective-permute-start(bf16[512,1024]{1,0:T(8,128)(2,1)S(1)} %copy-done.28), channel_id=1, source_target_pairs={{0,4},{4,0},{2,6},{6,2},{1,5},{5,1},{3,7},{7,3},{8,12},{12,8},{10,... | collective-permute-start | bytes 3145736 | tf_op jit(solution)/shard_map/ppermute | solution.py:34
  296.0 23.1 %collective-permute-start.19 = (bf16[512,1024]{1,0:T(8,128)(2,1)S(1)}, bf16[512,1024]{1,0:T(8,128)(2,1)S(1)}, u32[]{:S(2)}, u32[]{:S(2)}) collective-permute-start(bf16[512,1024]{1,0:T(8,128)(2,1)S(1)} %copy-done.29), channel_id=1, source_target_pairs={{0,1},{1,0},{2,3},{3,2},{4,5},{5,4},{6,7},{7,6},{8,9},{9,8},{10,11... | collective-permute-start | bytes 3145736 | tf_op jit(solution)/shard_map/ppermute | solution.py:38
  369.2 26.3 %collective-permute-start.27 = (bf16[512,1024]{1,0:T(8,128)(2,1)S(1)}, bf16[512,1024]{1,0:T(8,128)(2,1)}, u32[]{:S(2)}, u32[]{:S(2)}) collective-permute-start(bf16[512,1024]{1,0:T(8,128)(2,1)S(1)} %slice.170), channel_id=1, source_target_pairs={{0,2},{2,0},{4,6},{6,4},{1,3},{3,1},{5,7},{7,5},{8,10},{10,8},{12,... | collective-permute-start | bytes 3145736 | tf_op jit(solution)/shard_map/ppermute | solution.py:30
  373.2 47.5 %collective-permute-start.23 = (bf16[256,1024]{1,0:T(8,128)(2,1)}, bf16[256,1024]{1,0:T(8,128)(2,1)}, u32[]{:S(2)}, u32[]{:S(2)}) collective-permute-start(bf16[256,1024]{1,0:T(8,128)(2,1)} %get-tuple-element.157), channel_id=1, source_target_pairs={{4,0},{0,2},{6,4},{2,6},{5,1},{1,3},{7,5},{3,7},{12,8},{8,10},{14,... | collective-permute-start | bytes 1572872 | tf_op jit(solution)/shard_map/ppermute | solution.py:630
  381.7 25.8 %collective-permute-start.32 = (bf16[512,768]{1,0:T(8,128)(2,1)}, bf16[512,768]{1,0:T(8,128)(2,1)}, u32[]{:S(2)}, u32[]{:S(2)}) collective-permute-start(bf16[512,768]{1,0:T(8,128)(2,1)} %get-tuple-element.123), channel_id=1, source_target_pairs={{0,1},{1,0},{2,3},{3,2},{4,5},{5,4},{6,7},{7,6},{8,9},{9,8},{10,11... | collective-permute-start | bytes 2359304 | tf_op jit(solution)/shard_map/ppermute | solution.py:38
  419.1 28.2 %collective-permute-start.24 = (bf16[256,1024]{1,0:T(8,128)(2,1)}, bf16[256,1024]{1,0:T(8,128)(2,1)}, u32[]{:S(2)}, u32[]{:S(2)}) collective-permute-start(bf16[256,1024]{1,0:T(8,128)(2,1)} %get-tuple-element.158.a), channel_id=1, source_target_pairs={{0,1},{1,0},{2,3},{3,2},{4,5},{5,4},{6,7},{7,6},{8,9},{9,8},{10,11... | collective-permute-start | bytes 1572872 | tf_op jit(solution)/shard_map/ppermute | solution.py:38
  420.7 33.3 %collective-permute-start.25 = (bf16[256,1024]{1,0:T(8,128)(2,1)}, bf16[256,1024]{1,0:T(8,128)(2,1)}, u32[]{:S(2)}, u32[]{:S(2)}) collective-permute-start(bf16[256,1024]{1,0:T(8,128)(2,1)} %collective-permute-done.23.b), channel_id=1, source_target_pairs={{0,1},{1,0},{2,3},{3,2},{4,5},{5,4},{6,7},{7,6},{8,9},{9,8},{10,11... | collective-permute-start | bytes 1572872 | tf_op jit(solution)/shard_map/ppermute | solution.py:38
  421.3 25.9 %collective-permute-start.42 = (bf16[128,3456]{1,0:T(8,128)(2,1)}, bf16[128,3456]{1,0:T(8,128)(2,1)S(1)}, u32[]{:S(2)}, u32[]{:S(2)}) collective-permute-start(bf16[128,3456]{1,0:T(8,128)(2,1)} %reduce-scatter.5.cloned.1.call-done.a), channel_id=1, source_target_pairs={{0,4},{4,0},{2,6},{6,2},{1,5},{5,1},{3,7},{7,3},{8,12},{12,8},{10,... | collective-permute-start | bytes 2654216 | tf_op jit(solution)/shard_map/ppermute | solution.py:34
  425.6 35.0 %collective-permute-start.29 = (bf16[256,1024]{1,0:T(8,128)(2,1)}, bf16[256,1024]{1,0:T(8,128)(2,1)}, u32[]{:S(2)}, u32[]{:S(2)}) collective-permute-start(bf16[256,1024]{1,0:T(8,128)(2,1)} %get-tuple-element.155), channel_id=1, source_target_pairs={{4,0},{0,2},{6,4},{2,6},{5,1},{1,3},{7,5},{3,7},{12,8},{8,10},{14,... | collective-permute-start | bytes 1572872 | tf_op jit(solution)/shard_map/ppermute | solution.py:630
  444.9 48.2 %collective-permute-start.43 = (bf16[128,3456]{1,0:T(8,128)(2,1)S(1)}, bf16[128,3456]{1,0:T(8,128)(2,1)S(1)}, u32[]{:S(2)}, u32[]{:S(2)}) collective-permute-start(bf16[128,3456]{1,0:T(8,128)(2,1)S(1)} %copy-done.32), channel_id=1, source_target_pairs={{0,2},{2,0},{4,6},{6,4},{1,3},{3,1},{5,7},{7,5},{8,10},{10,8},{12,... | collective-permute-start | bytes 2654216 | tf_op jit(solution)/shard_map/ppermute | solution.py:30
  447.3 45.9 %collective-permute-start.44 = (bf16[128,3456]{1,0:T(8,128)(2,1)S(1)}, bf16[128,3456]{1,0:T(8,128)(2,1)}, u32[]{:S(2)}, u32[]{:S(2)}) collective-permute-start(bf16[128,3456]{1,0:T(8,128)(2,1)S(1)} %collective-permute-done.42.b), channel_id=1, source_target_pairs={{0,2},{2,0},{4,6},{6,4},{1,3},{3,1},{5,7},{7,5},{8,10},{10,8},{12,... | collective-permute-start | bytes 2654216 | tf_op jit(solution)/shard_map/ppermute | solution.py:30
  461.9 22.8 %collective-permute-start.31 = (bf16[256,1024]{1,0:T(8,128)(2,1)}, bf16[256,1024]{1,0:T(8,128)(2,1)}, u32[]{:S(2)}, u32[]{:S(2)}) collective-permute-start(bf16[256,1024]{1,0:T(8,128)(2,1)} %collective-permute-done.29.b), channel_id=1, source_target_pairs={{0,1},{1,0},{2,3},{3,2},{4,5},{5,4},{6,7},{7,6},{8,9},{9,8},{10,11... | collective-permute-start | bytes 1572872 | tf_op jit(solution)/shard_map/ppermute | solution.py:38
  (67 other events, 777.0 us)
Sparse Core Ops, SparseCore 0:
  11.1 48.1 all-gather.4
  61.5 68.7 all-gather.6
  275.5 65.6 reduce-scatter.4
  415.3 22.0 reduce-scatter.2
